TPU v7x, 32 devices: a whole 2x2x4 slice. The times are simulated.
32 devices in a mesh: inner: 4 (over y, core), outer: 8 (over z, x).
Axes of the slice: x: 2, y: 2, z: 4, core: 2. Of those that a mesh axis runs over, the one named last changes fastest.
Arguments:
- layer_input: bfloat16 [4096, 2048], P(('inner', 'outer')), may hold values from -6 to 6
- segments: int32 [4096], P(('inner', 'outer')), may hold values from 0 to 11, as said below
- positions: int32 [4096], P(('inner', 'outer')), may hold values from 0 to 511, as said below
- query_key_value_weight: bfloat16 [2048, 1920], P(('inner', 'outer')), may hold values from -0.125 to 0.125
- w_out: bfloat16 [2048, 1280], P(('inner', 'outer')), may hold values from -2.5 to 2.5
- w_gate: bfloat16 [2048, 5120], P(('inner', 'outer')), may hold values from -0.125 to 0.125
- w_up: bfloat16 [2048, 5120], P(('inner', 'outer')), may hold values from -0.125 to 0.125
- w_down: bfloat16 [2048, 5120], P(('inner', 'outer')), may hold values from -0.078125 to 0.078125
- g_attn: float32 [2048], replicated, may hold values from 0.1 to 1.9
- g_ffn: float32 [2048], replicated, may hold values from 0.1 to 1.9
- g_query: float32 [64], replicated, may hold values from 0.1 to 1.9
- g_key: float32 [64], replicated, may hold values from 0.1 to 1.9
- cotangent: bfloat16 [4096, 2048], P(('inner', 'outer')), may hold values from -6 to 6
Outputs:
- result: bfloat16 [4096, 2048], P(('inner', 'outer'))
- input_grad: bfloat16 [4096, 2048], P(('inner', 'outer'))
- w_qkv_grad: float32 [2048, 1920], P(('inner', 'outer'))
- w_out_grad: float32 [2048, 1280], P(('inner', 'outer'))
- w_gate_grad: float32 [2048, 5120], P(('inner', 'outer'))
- w_up_grad: float32 [2048, 5120], P(('inner', 'outer'))
- w_down_grad: float32 [2048, 5120], P(('inner', 'outer'))
- g_attn_grad: float32 [2048], replicated
- g_ffn_grad: float32 [2048], replicated
- g_query_grad: float32 [64], replicated
- g_key_grad: float32 [64], replicated
Inputs may be any that keep to these rules, and one draw needn't show every extreme that they name: `segments`: segment numbers never fall along the tokens; each packed sequence of 1024 tokens holds exactly three documents, numbered on from the previous sequence's: a first one of 1 to 511 tokens, then one of 512 tokens, then the rest. `positions`: A token's position is its index in its document: 0 at each segment's first token, rising by one per token.
All inputs are finite; a program needn't handle non-finite values.
Results may differ from a plain program's by a relative error of at most 0.015.
Values may be sent and summed in bfloat16 or wider, within the bound.
No kernel may reach another device: no remote copies, remote signals or barrier semaphores. Data moves between devices by JAX's collectives and lax.ppermute only.
A program may use at most 384 MiB of HBM per device.

v0:
```python
import jax
import jax.numpy as jnp
from jax import lax
from jax.sharding import PartitionSpec as P

QUERY_HEADS = 20
KEY_VALUE_HEADS = 5
HEAD_DIM = 64


norm_eps = 1e-06


def product(left, right):
    return jnp.dot(left, right, preferred_element_type=jnp.float32)


def product_nt(left, right):
    return lax.dot_general(
        left, right, (((1,), (1,)), ((), ())), preferred_element_type=jnp.float32
    )


def product_tn(left, right):
    return lax.dot_general(
        left, right, (((0,), (0,)), ((), ())), preferred_element_type=jnp.float32
    )


def row_scale(values):
    return lax.rsqrt(jnp.mean(values * values, axis=-1, keepdims=True) + norm_eps)


def rotary_tables(positions):
    half_size = HEAD_DIM // 2
    frequency = 10000.0 ** (-jnp.arange(half_size, dtype=jnp.float32) / half_size)
    angles = positions.astype(jnp.float32)[:, None] * frequency[None, :]
    angles = jnp.concatenate([angles, angles], axis=-1)
    return (jnp.cos(angles)[:, None, :], jnp.sin(angles)[:, None, :])


def rotate(values, cosine, sine_part):
    half_size = values.shape[-1] // 2
    turned = jnp.concatenate([-values[..., half_size:], values[..., :half_size]], axis=-1)
    return values * cosine + turned * sine_part


def rotate_back(gradient, cosine, sine_part):
    shifted = gradient * sine_part
    half_size = gradient.shape[-1] // 2
    turned = jnp.concatenate([shifted[..., half_size:], -shifted[..., :half_size]], axis=-1)
    return gradient * cosine + turned


def norm_back(normed, inv_rms, gain_vec, gradient):
    weighted = gradient * gain_vec
    inputs_grad = inv_rms * (
        weighted - normed * jnp.mean(weighted * normed, axis=-1, keepdims=True)
    )
    return (inputs_grad, gradient * normed)


def spread_all(term_fn, share_rows):
    return lax.psum_scatter(
        term_fn(jnp.int32(0), share_rows * lax.axis_size(("inner", "outer"))),
        ("inner", "outer"),
        scatter_dimension=0,
        tiled=True,
    )


def attend_forward(query_heads, key_head_count, value_head_count, allowed):
    queries_per_group = QUERY_HEADS // KEY_VALUE_HEADS

    def one_head(head_index):
        query_head = query_heads[head_index]
        key_head = key_head_count[head_index // queries_per_group]
        value_head = value_head_count[head_index // queries_per_group]
        scores = jnp.where(allowed, product_nt(query_head, key_head), -1e30)
        row_max = jnp.max(scores, axis=-1, keepdims=True)
        exponent = jnp.exp(scores - row_max)
        row_total = jnp.sum(exponent, axis=-1, keepdims=True)
        probabilities = (exponent / row_total).astype(jnp.bfloat16)
        head_out = product(probabilities, value_head).astype(jnp.bfloat16)
        return (head_out, (row_max + jnp.log(row_total))[:, 0])

    return lax.map(one_head, jnp.arange(QUERY_HEADS))


def attend_backward(query_heads, key_head_count, value_head_count, out_grads, log_totals, allowed):
    queries_per_group = QUERY_HEADS // KEY_VALUE_HEADS

    def heads_per_group(kv_index):
        key_head = key_head_count[kv_index]
        value_head = value_head_count[kv_index]

        def per_query(running, member):
            key_grad, value_grad = running
            head_index = kv_index * queries_per_group + member
            query_head = query_heads[head_index]
            head_grad = out_grads[head_index]
            log_total = log_totals[head_index]
            scores = product_nt(query_head, key_head)
            probabilities = jnp.where(allowed, jnp.exp(scores - log_total[:, None]), 0.0)
            prob_grads = product_nt(head_grad, value_head)
            row_dot = jnp.sum(probabilities * prob_grads, axis=-1, keepdims=True)
            score_grads = (probabilities * (prob_grads - row_dot)).astype(jnp.bfloat16)
            query_grad = product(score_grads, key_head)
            key_grad = key_grad + product_tn(score_grads, query_head)
            value_grad = value_grad + product_tn(probabilities.astype(jnp.bfloat16), head_grad)
            return ((key_grad, value_grad), query_grad)

        zero_block = jnp.zeros(key_head.shape, jnp.float32)
        (key_grad, value_grad), query_grads = lax.scan(
            per_query, (zero_block, zero_block), jnp.arange(queries_per_group)
        )
        key_grad, value_grad = (
            lax.psum_scatter(
                key_grad.astype(jnp.bfloat16), "outer", scatter_dimension=0, tiled=True
            ).astype(jnp.float32),
            lax.psum_scatter(
                value_grad.astype(jnp.bfloat16), "outer", scatter_dimension=0, tiled=True
            ).astype(jnp.float32),
        )
        return (query_grads, key_grad, value_grad)

    return lax.map(heads_per_group, jnp.arange(KEY_VALUE_HEADS))


def local(
    layer_input,
    segments,
    positions,
    query_key_value_weight,
    w_out,
    w_gate,
    w_up,
    w_down,
    g_attn,
    g_ffn,
    g_query,
    g_key,
    cotangent,
):
    total_row_count = layer_input.shape[0]
    model_width = layer_input.shape[1]
    inner_count = lax.axis_size("inner")
    outer_count = lax.axis_size("outer")
    query_columns = QUERY_HEADS * HEAD_DIM
    key_value_columns = KEY_VALUE_HEADS * HEAD_DIM
    factor = HEAD_DIM ** (-0.5)
    inputs = layer_input.astype(jnp.float32)
    scale_in = row_scale(inputs)
    normed_in = inputs * scale_in
    normed_low = (normed_in * g_attn).astype(jnp.bfloat16)
    qkv_full, out_full = (
        lax.all_gather(query_key_value_weight, ("inner", "outer"), axis=0, tiled=True),
        lax.all_gather(w_out, ("inner", "outer"), axis=0, tiled=True),
    )
    joined_projection = product(normed_low, qkv_full)
    query_raw = joined_projection[:, :query_columns].reshape(total_row_count, QUERY_HEADS, HEAD_DIM)
    key_unnormed = joined_projection[:, query_columns : query_columns + key_value_columns].reshape(
        total_row_count, KEY_VALUE_HEADS, HEAD_DIM
    )
    value_unnormed = joined_projection[:, query_columns + key_value_columns :]
    query_scale = row_scale(query_raw)
    query_normed = query_raw * query_scale
    key_scale = row_scale(key_unnormed)
    key_normed = key_unnormed * key_scale
    cosine, sine_part = rotary_tables(positions)
    query_low = (rotate(query_normed * g_query, cosine, sine_part) * factor).astype(jnp.bfloat16)
    key_low = rotate(key_normed * g_key, cosine, sine_part).astype(jnp.bfloat16)
    value_low = value_unnormed.astype(jnp.bfloat16)
    key_everything, value_everything, segment_all = (
        lax.all_gather(
            key_low.reshape(total_row_count, key_value_columns), "outer", axis=0, tiled=True
        ),
        lax.all_gather(value_low, "outer", axis=0, tiled=True),
        lax.all_gather(segments, "outer", axis=0, tiled=True),
    )
    sequence_length = key_everything.shape[0]
    query_heads = query_low.transpose(1, 0, 2)
    key_head_count = key_everything.reshape(sequence_length, KEY_VALUE_HEADS, HEAD_DIM).transpose(
        1, 0, 2
    )
    value_head_count = value_everything.reshape(
        sequence_length, KEY_VALUE_HEADS, HEAD_DIM
    ).transpose(1, 0, 2)
    query_index = lax.axis_index("outer") * total_row_count + jnp.arange(total_row_count)
    key_index = jnp.arange(sequence_length)
    allowed = (segments[:, None] == segment_all[None, :]) & (
        key_index[None, :] <= query_index[:, None]
    )
    heads_out, log_totals = attend_forward(query_heads, key_head_count, value_head_count, allowed)
    attended = heads_out.transpose(1, 0, 2).reshape(total_row_count, query_columns)
    branch_one = product_nt(attended, out_full)
    middle = inputs + branch_one
    scale_mid = row_scale(middle)
    normed_mid = middle * scale_mid
    mid_low = (normed_mid * g_ffn).astype(jnp.bfloat16)
    gate_full, up_full, down_full = (
        lax.all_gather(w_gate, ("inner", "outer"), axis=0, tiled=True),
        lax.all_gather(w_up, ("inner", "outer"), axis=0, tiled=True),
        lax.all_gather(w_down, ("inner", "outer"), axis=0, tiled=True),
    )
    gate_pre = product(mid_low, gate_full)
    up_pre = product(mid_low, up_full)
    sigmoid_gate = jax.nn.sigmoid(gate_pre)
    activated = gate_pre * sigmoid_gate
    hidden = (activated * up_pre).astype(jnp.bfloat16)
    branch_two = product_nt(hidden, down_full)
    hidden_grad = product(cotangent, down_full)
    silu_slope = sigmoid_gate * (1.0 + gate_pre * (1.0 - sigmoid_gate))
    gate_grad = (hidden_grad * up_pre * silu_slope).astype(jnp.bfloat16)
    up_grad = (hidden_grad * activated).astype(jnp.bfloat16)
    mid_low_grad = product_nt(gate_grad, gate_full) + product_nt(up_grad, up_full)
    share_rows = model_width // (inner_count * outer_count)

    def down_term(offset, span):
        return product_tn(cotangent, hidden)

    def gate_up_term(offset, span):
        return jnp.concatenate(
            [product_tn(mid_low, gate_grad), product_tn(mid_low, up_grad)], axis=1
        )

    w_down_grad = spread_all(down_term, share_rows)
    gate_up_grad = spread_all(gate_up_term, share_rows)
    w_gate_grad = gate_up_grad[:, : w_gate.shape[1]]
    w_up_grad = gate_up_grad[:, w_gate.shape[1] :]
    result = (middle + branch_two).astype(jnp.bfloat16)
    grad_out = cotangent.astype(jnp.float32)
    mid_norm_grad, ffn_gain_terms = norm_back(normed_mid, scale_mid, g_ffn, mid_low_grad)
    middle_grad = grad_out + mid_norm_grad
    branch_grad = middle_grad.astype(jnp.bfloat16)
    attended_grad = product(branch_grad, out_full).astype(jnp.bfloat16)
    head_grads = attended_grad.reshape(total_row_count, QUERY_HEADS, HEAD_DIM).transpose(1, 0, 2)
    query_grads, key_grads, value_grads = attend_backward(
        query_heads, key_head_count, value_head_count, head_grads, log_totals, allowed
    )
    query_grad = query_grads.reshape(QUERY_HEADS, total_row_count, HEAD_DIM).transpose(1, 0, 2)
    key_grad = key_grads.transpose(1, 0, 2)
    value_grad = value_grads.transpose(1, 0, 2).reshape(total_row_count, key_value_columns)
    query_rot_grad = rotate_back(query_grad * factor, cosine, sine_part)
    query_in_grad, query_gain_terms = norm_back(query_normed, query_scale, g_query, query_rot_grad)
    key_rot_grad = rotate_back(key_grad, cosine, sine_part)
    key_in_grad, key_gain_terms = norm_back(key_normed, key_scale, g_key, key_rot_grad)
    joined_grad = jnp.concatenate(
        [
            query_in_grad.reshape(total_row_count, query_columns),
            key_in_grad.reshape(total_row_count, key_value_columns),
            value_grad,
        ],
        axis=1,
    )
    joined_grad = joined_grad.astype(jnp.bfloat16)
    normed_in_grad = product_nt(joined_grad, qkv_full)
    attn_grads = lax.psum_scatter(
        jnp.concatenate(
            [product_tn(branch_grad, attended), product_tn(normed_low, joined_grad)], axis=1
        ),
        ("inner", "outer"),
        scatter_dimension=0,
        tiled=True,
    )
    w_out_grad = attn_grads[:, :query_columns]
    w_qkv_grad = attn_grads[:, query_columns:]
    in_norm_grad, attn_gain_terms = norm_back(normed_in, scale_in, g_attn, normed_in_grad)
    input_grad = (middle_grad + in_norm_grad).astype(jnp.bfloat16)
    gain_sums = lax.psum(
        (
            jnp.sum(attn_gain_terms, axis=0),
            jnp.sum(ffn_gain_terms, axis=0),
            jnp.sum(query_gain_terms, axis=(0, 1)),
            jnp.sum(key_gain_terms, axis=(0, 1)),
        ),
        ("inner", "outer"),
    )
    return (
        result,
        input_grad,
        w_qkv_grad,
        w_out_grad,
        w_gate_grad,
        w_up_grad,
        w_down_grad,
        gain_sums[0],
        gain_sums[1],
        gain_sums[2],
        gain_sums[3],
    )


def solution(mesh):
    in_specs = (
        P(("inner", "outer"), None),
        P(("inner", "outer")),
        P(("inner", "outer")),
        P(("inner", "outer"), None),
        P(("inner", "outer"), None),
        P(("inner", "outer"), None),
        P(("inner", "outer"), None),
        P(("inner", "outer"), None),
        P(),
        P(),
        P(),
        P(),
        P(("inner", "outer"), None),
    )
    out_specs = (
        P(("inner", "outer"), None),
        P(("inner", "outer"), None),
        P(("inner", "outer"), None),
        P(("inner", "outer"), None),
        P(("inner", "outer"), None),
        P(("inner", "outer"), None),
        P(("inner", "outer"), None),
        P(),
        P(),
        P(),
        P(),
    )
    return jax.shard_map(local, mesh=mesh, in_specs=in_specs, out_specs=out_specs, check_vma=False)
```

profile of v0, /device:TPU:0, one launch (start us, length us, event | category | flops | bytes accessed | tf_op | source)
XLA Modules:
  0.0 4653.7 jit_solution(7471980853060299006)
XLA Ops:
  12.0 22.3 all-gather
  35.8 53.4 %all-gather.7.cloned.1.call-done = bf16[2048,1920]{1,0:T(8,128)(2,1)} async-done(((bf16[64,1920]{1,0:T(8,128)(2,1)}), bf16[2048,1920]{1,0:T(8,128)(2,1)}) %all-gather.7.cloned.1.call-update) | async-done | bytes 7864336 | tf_op jit(solution)/shard_map/all_gather | solution.py:157
  89.2 4.5 fusion.63
  94.7 29.8 all_gather.25
  126.7 33.4 all_gather.27
  161.3 2.3 copy.84
  163.6 172.5 %while.48 = (s32[]{:T(128)}, bf16[20,128,64]{1,2,0:T(8,128)(2,1)S(1)}, f32[20,128]{1,0:T(8,128)}, s32[20]{0:T(128)S(1)}, bf16[20,128,64]{2,1,0:T(8,128)(2,1)S(1)...) while((s32[]{:T(128)}, ...), condition=%wide.region_6.7_spmd.clone, body=%wide.region_3.6_spmd.clone.sunk | while | flops 34873236 | bytes 2156950 | solution.py:87
  336.1 4.5 multiply_reduce_fusion.3
  340.9 11.6 fusion.74
  352.4 84.4 %all-gather.11.cloned.1.call-done = bf16[2048,5120]{1,0:T(8,128)(2,1)} async-done(((bf16[64,5120]{1,0:T(8,128)(2,1)}), bf16[2048,5120]{1,0:T(8,128)(2,1)}) %all-gather.11.cloned.1.call-update) | async-done | bytes 20971536 | tf_op jit(solution)/shard_map/all_gather | solution.py:202
  436.8 11.3 fusion.73
  448.1 124.1 %all-gather.15.cloned.1.call-done = bf16[2048,5120]{1,0:T(8,128)(2,1)} async-done(((bf16[64,5120]{1,0:T(8,128)(2,1)}), bf16[2048,5120]{1,0:T(8,128)(2,1)}) %all-gather.15.cloned.1.call-update) | async-done | bytes 20971536 | tf_op jit(solution)/shard_map/all_gather | solution.py:204
  572.3 14.0 multiply_convert_fusion.1
  586.3 12.2 fusion.75
  598.5 12.1 multiply_reduce_fusion.1
  611.6 5.5 fusion.55
  619.9 790.2 %while.50 = (s32[]{:T(128)}, f32[5,4,128,64]{2,3,1,0:T(8,128)}, f32[5,128,64]{1,2,0:T(8,128)}, bf16[5,128,64]{1,2,0:T(8,128)(2,1)}, s32[5]{0:T(128)}, /*index=5*...) while((s32[]{:T(128)}, f32[5,4,128,64]{2,3,1,0:T(8,128)}, ...), condition=%wide.region_15.16_spmd.clone, body=%wide.region_9.15_spmd.clone.sunk | while | flops 85737352 | bytes 9380057 | solution.py:127
  626.2 24.9 while.51
  654.6 57.0 %reduce-scatter.26.cloned.1.call-done = bf16[128,64]{1,0:T(8,128)(2,1)} async-done(((bf16[1024,64]{1,0:T(8,128)(2,1)}), bf16[128,64]{1,0:T(8,128)(2,1)}) %reduce-scatter.26.cloned.1.call-update) | async-done | bytes 16400 | tf_op jit(solution)/shard_map/while
  713.0 62.7 %reduce-scatter.24.cloned.1.call-done = bf16[128,64]{1,0:T(8,128)(2,1)} async-done(((bf16[1024,64]{1,0:T(8,128)(2,1)}), bf16[128,64]{1,0:T(8,128)(2,1)}) %reduce-scatter.24.cloned.1.call-update) | async-done | bytes 16400 | tf_op jit(solution)/shard_map/while
  783.5 24.9 while.51
  811.9 57.9 %reduce-scatter.26.cloned.1.call-done = bf16[128,64]{1,0:T(8,128)(2,1)} async-done(((bf16[1024,64]{1,0:T(8,128)(2,1)}), bf16[128,64]{1,0:T(8,128)(2,1)}) %reduce-scatter.26.cloned.1.call-update) | async-done | bytes 16400 | tf_op jit(solution)/shard_map/while
  871.2 62.8 %reduce-scatter.24.cloned.1.call-done = bf16[128,64]{1,0:T(8,128)(2,1)} async-done(((bf16[1024,64]{1,0:T(8,128)(2,1)}), bf16[128,64]{1,0:T(8,128)(2,1)}) %reduce-scatter.24.cloned.1.call-update) | async-done | bytes 16400 | tf_op jit(solution)/shard_map/while
  941.8 25.0 while.51
  970.1 57.9 %reduce-scatter.26.cloned.1.call-done = bf16[128,64]{1,0:T(8,128)(2,1)} async-done(((bf16[1024,64]{1,0:T(8,128)(2,1)}), bf16[128,64]{1,0:T(8,128)(2,1)}) %reduce-scatter.26.cloned.1.call-update) | async-done | bytes 16400 | tf_op jit(solution)/shard_map/while
  1029.6 62.8 %reduce-scatter.24.cloned.1.call-done = bf16[128,64]{1,0:T(8,128)(2,1)} async-done(((bf16[1024,64]{1,0:T(8,128)(2,1)}), bf16[128,64]{1,0:T(8,128)(2,1)}) %reduce-scatter.24.cloned.1.call-update) | async-done | bytes 16400 | tf_op jit(solution)/shard_map/while
  1100.1 25.0 while.51
  1128.5 57.9 %reduce-scatter.26.cloned.1.call-done = bf16[128,64]{1,0:T(8,128)(2,1)} async-done(((bf16[1024,64]{1,0:T(8,128)(2,1)}), bf16[128,64]{1,0:T(8,128)(2,1)}) %reduce-scatter.26.cloned.1.call-update) | async-done | bytes 16400 | tf_op jit(solution)/shard_map/while
  1187.8 62.8 %reduce-scatter.24.cloned.1.call-done = bf16[128,64]{1,0:T(8,128)(2,1)} async-done(((bf16[1024,64]{1,0:T(8,128)(2,1)}), bf16[128,64]{1,0:T(8,128)(2,1)}) %reduce-scatter.24.cloned.1.call-update) | async-done | bytes 16400 | tf_op jit(solution)/shard_map/while
  1258.4 24.9 while.51
  1286.7 57.9 %reduce-scatter.26.cloned.1.call-done = bf16[128,64]{1,0:T(8,128)(2,1)} async-done(((bf16[1024,64]{1,0:T(8,128)(2,1)}), bf16[128,64]{1,0:T(8,128)(2,1)}) %reduce-scatter.26.cloned.1.call-update) | async-done | bytes 16400 | tf_op jit(solution)/shard_map/while
  1346.1 62.6 %reduce-scatter.24.cloned.1.call-done = bf16[128,64]{1,0:T(8,128)(2,1)} async-done(((bf16[1024,64]{1,0:T(8,128)(2,1)}), bf16[128,64]{1,0:T(8,128)(2,1)}) %reduce-scatter.24.cloned.1.call-update) | async-done | bytes 16400 | tf_op jit(solution)/shard_map/while
  1415.7 2.3 fusion.58
  1419.6 10.9 pad_maximum_fusion.1
  1430.5 25.9 copy.93
  1456.5 18.2 fusion.77
  1474.6 16.4 fusion.76
  1491.1 54.2 %pad_maximum_fusion = f32[2048,10240]{1,0:T(8,128)} fusion(f32[2048,5120]{1,0:T(8,128)} %fusion.77, f32[2048,5120]{1,0:T(8,128)} %fusion.76), kind=kLoop, calls=%fused_computation.54 | loop fusion | flops 20971520 | bytes 167772160 | tf_op jit(solution)/shard_map/concatenate | solution.py:223
  1546.7 16.3 convolution_bitcast_fusion.1
  1563.1 39.1 copy.95
  1603.3 7.0 fusion.49
  1610.4 50.4 %all-reduce = (f32[2048]{0:T(1024)}, f32[2048]{0:T(1024)}, f32[64]{0:T(128)}, f32[64]{0:T(128)}) all-reduce(f32[2048]{0:T(1024)S(1)} %get-tuple-element.543, f32[2048]{0:T(1024)S(1)} %copy-done.33, f32[64]{0:T(128)S(1)} %copy-done.41, f32[64]{0:T(128)S(1)} %copy-done.42), channel_id=1, replica_groups=mesh['inner'=4,'outer'=8] {'inner','outer'}, use_global_device_ids=true, to_apply=%region_23.24 | all-reduce | flops 4224 | bytes 33792 | tf_op jit(solution)/shard_map/psum | solution.py:270
  1660.7 2.5 fusion.48
  1663.2 11.9 fusion.38
  1675.1 335.3 %reduce-scatter.20.cloned.1.call-done = f32[64,3200]{1,0:T(8,128)} async-done(((f32[2048,3200]{1,0:T(8,128)}), f32[64,3200]{1,0:T(8,128)}) %reduce-scatter.20.cloned.1.call-update) | async-done | bytes 819216
  2014.0 1749.6 %reduce-scatter.18.cloned.1.call-done = f32[64,10240]{1,0:T(8,128)} async-done(((f32[2048,10240]{1,0:T(8,128)}), f32[64,10240]{1,0:T(8,128)}) %reduce-scatter.18.cloned.1.call-update) | async-done | bytes 2621456 | tf_op jit(solution)/shard_map/reduce_scatter | solution.py:64
  3763.6 3.5 fusion.70
  3767.1 879.5 %reduce-scatter.22.cloned.1.call-done = f32[64,5120]{1,0:T(8,128)} async-done(((f32[2048,5120]{1,0:T(8,128)}), f32[64,5120]{1,0:T(8,128)}) %reduce-scatter.22.cloned.1.call-update) | async-done | bytes 1310736
  (551 shorter events, 282.0 us)
Async XLA Ops:
  7.2 28.5 copy-start.2
  7.2 82.0 %copy-start.24 = (f32[2048]{0:T(1024)S(1)}, f32[2048]{0:T(1024)}, u32[]{:S(2)}) copy-start(f32[2048]{0:T(1024)} %param.27) | copy-start | bytes 24580
  7.2 82.0 %all-gather.7.cloned.1.call-start = ((), (), s32[]{:S(2)}) async-start(), calls=%async_computation.5 | async-start | bytes 8110080 | tf_op jit(solution)/shard_map/all_gather | solution.py:157
  7.9 328.2 %all-gather.9.cloned.1.call-start = ((), (), s32[]{:S(2)}) async-start(), calls=%async_computation.6 | async-start | bytes 5406720 | tf_op jit(solution)/shard_map/all_gather | solution.py:158
  8.7 332.2 %all-gather.13.cloned.1.call-start = ((), (), s32[]{:S(2)}) async-start(), calls=%async_computation.8 | async-start | bytes 21626880 | tf_op jit(solution)/shard_map/all_gather | solution.py:203
  9.4 427.4 %all-gather.11.cloned.1.call-start = ((), (), s32[]{:S(2)}) async-start(), calls=%async_computation.7 | async-start | bytes 21626880 | tf_op jit(solution)/shard_map/all_gather | solution.py:202
  10.0 562.3 %all-gather.15.cloned.1.call-start = ((), (), s32[]{:S(2)}) async-start(), calls=%async_computation.9 | async-start | bytes 21626880 | tf_op jit(solution)/shard_map/all_gather | solution.py:204
  35.6 90.5 %copy-start.20 = (f32[128,64]{0,1:T(8,128)}, f32[128,64]{0,1:T(8,128)S(1)}, u32[]{:S(2)}) copy-start(f32[128,64]{0,1:T(8,128)S(1)} %get-tuple-element.647) | copy-start | bytes 98308
  35.6 90.5 %copy-start.21 = (f32[128,64]{0,1:T(8,128)}, f32[128,64]{0,1:T(8,128)S(1)}, u32[]{:S(2)}) copy-start(f32[128,64]{0,1:T(8,128)S(1)} %get-tuple-element.646) | copy-start | bytes 98308
  35.8 53.4 %copy-start.36 = (f32[128]{0:T(128)}, f32[128]{0:T(128)S(1)}, u32[]{:S(2)}) copy-start(f32[128]{0:T(128)S(1)} %add_rsqrt_fusion.3) | copy-start | bytes 1540
  94.1 31.8 copy-start.11
  94.3 31.6 copy-start.34
  94.4 31.7 copy-start.28
  336.1 4.6 copy-start.16
  336.1 4.5 copy-start.32
  340.6 269.9 %copy-start = (f32[128,2048]{1,0:T(8,128)}, f32[128,2048]{1,0:T(8,128)S(1)}, u32[]{:S(2)}) copy-start(f32[128,2048]{1,0:T(8,128)S(1)} %get-tuple-element.649) | copy-start | bytes 3145732
  586.3 12.2 copy-start.8
  586.3 12.2 copy-start.10
  598.5 12.1 copy-start.14
  610.6 6.5 slice-start.3
  611.6 5.5 copy-start.4
  611.6 5.6 slice-start.4
  619.9 91.7 %reduce-scatter.26.cloned.1.call-start = ((), (), s32[]{:S(2)}) async-start(), calls=%async_computation.14 | async-start | bytes 294912 | tf_op jit(solution)/shard_map/while
  652.0 123.7 %reduce-scatter.24.cloned.1.call-start = ((), (), s32[]{:S(2)}) async-start(), calls=%async_computation.13 | async-start | bytes 294912 | tf_op jit(solution)/shard_map/while
  777.2 92.5 %reduce-scatter.26.cloned.1.call-start = ((), (), s32[]{:S(2)}) async-start(), calls=%async_computation.14 | async-start | bytes 294912 | tf_op jit(solution)/shard_map/while
  809.3 124.6 %reduce-scatter.24.cloned.1.call-start = ((), (), s32[]{:S(2)}) async-start(), calls=%async_computation.13 | async-start | bytes 294912 | tf_op jit(solution)/shard_map/while
  935.5 92.6 %reduce-scatter.26.cloned.1.call-start = ((), (), s32[]{:S(2)}) async-start(), calls=%async_computation.14 | async-start | bytes 294912 | tf_op jit(solution)/shard_map/while
  967.6 124.7 %reduce-scatter.24.cloned.1.call-start = ((), (), s32[]{:S(2)}) async-start(), calls=%async_computation.13 | async-start | bytes 294912 | tf_op jit(solution)/shard_map/while
  1093.8 92.6 %reduce-scatter.26.cloned.1.call-start = ((), (), s32[]{:S(2)}) async-start(), calls=%async_computation.14 | async-start | bytes 294912 | tf_op jit(solution)/shard_map/while
  1126.0 124.6 %reduce-scatter.24.cloned.1.call-start = ((), (), s32[]{:S(2)}) async-start(), calls=%async_computation.13 | async-start | bytes 294912 | tf_op jit(solution)/shard_map/while
  1252.1 92.6 %reduce-scatter.26.cloned.1.call-start = ((), (), s32[]{:S(2)}) async-start(), calls=%async_computation.14 | async-start | bytes 294912 | tf_op jit(solution)/shard_map/while
  1284.2 124.5 %reduce-scatter.24.cloned.1.call-start = ((), (), s32[]{:S(2)}) async-start(), calls=%async_computation.13 | async-start | bytes 294912 | tf_op jit(solution)/shard_map/while
  1410.1 4.3 copy-start.13
  1410.1 4.3 copy-start.27
  1410.1 4.3 copy-start.35
  1410.1 600.3 %reduce-scatter.20.cloned.1.call-start = ((), (), s32[]{:S(2)}) async-start(), calls=%async_computation.11 | async-start | bytes 27033600
  1415.3 2.7 slice-start
  1415.4 2.6 copy-start.22
  1415.7 3.3 slice-start.1
  1415.7 3.9 slice-start.2
  1456.4 18.2 copy-start.9
  1456.4 2307.2 %reduce-scatter.18.cloned.1.call-start = ((), (), s32[]{:S(2)}) async-start(), calls=%async_computation.10 | async-start | bytes 86507520 | tf_op jit(solution)/shard_map/reduce_scatter | solution.py:64
  1545.3 3101.2 %reduce-scatter.22.cloned.1.call-start = ((), (), s32[]{:S(2)}) async-start(), calls=%async_computation.12 | async-start | bytes 43253760
  1603.3 7.0 copy-start.33
  1603.3 7.0 copy-start.41
  1603.3 7.0 copy-start.42
  1603.3 57.4 %copy-start.5 = (f32[128,2048]{1,0:T(8,128)S(1)}, f32[128,2048]{1,0:T(8,128)}, u32[]{:S(2)}) copy-start(f32[128,2048]{1,0:T(8,128)} %copy-done.4) | copy-start | bytes 3145732
  1610.3 52.9 %copy-start.1 = (f32[128,2048]{1,0:T(8,128)S(1)}, f32[128,2048]{1,0:T(8,128)}, u32[]{:S(2)}) copy-start(f32[128,2048]{1,0:T(8,128)} %copy-done) | copy-start | bytes 3145732
  (18 other events, 26.6 us)
Sparse Core Ops, SparseCore 0:
  11.0 78.1 all-gather.6
  92.0 72.5 all-gather.8
  167.5 133.6 all-gather.12
  304.0 132.8 all-gather.10
  439.5 132.7 all-gather.14
  652.2 59.3 reduce-scatter.25
  715.5 60.2 reduce-scatter.23
  809.5 60.2 reduce-scatter.25
  873.6 60.2 reduce-scatter.23
  967.8 60.2 reduce-scatter.25
  1032.0 60.2 reduce-scatter.23
  1126.1 60.2 reduce-scatter.25
  1190.3 60.2 reduce-scatter.23
  1284.3 60.2 reduce-scatter.25
  1348.4 60.2 reduce-scatter.23
  1456.5 553.8 reduce-scatter.19
  2012.6 1750.9 reduce-scatter.17
  3766.3 880.1 reduce-scatter.21
where the time goes:
time: 4670 us; the launch traced here: 4650 us
  waiting for transfers between devices  3830 us (82%)
  matrix products  270 us (6%)
  local copies, waits for them, and re-layouts  200 us (4%)
  blocking collectives  136 us (3%)
  loops' own time  106 us (2%)
  other arithmetic  94.1 us (2%)
    reduce_scatter x1, waiting for transfers between devices, spread_all(): lax.psum_scatter(term_fn(jnp.int32(0), share_rows * lax.axis_size(('inner...  1750 us
    unnamed x10, waiting for transfers between devices  1220 us
    while x20, waiting for transfers between devices  602 us
    all_gather x1, waiting for transfers between devices, local(): lax.all_gather(w_down, ('inner', 'outer'), axis=0, tiled=True)  124 us
    dot_general x65, matrix products, product_nt(): lax.dot_general(left, right, (((1,), (1,)), ((), ())), preferred_element_...  101 us
  transfers between devices with their start and end apart: 18, of which 16 were waited for; matrix products, arithmetic and copies ran while one was open for 7% of the time, Pallas kernels for 0%

commit v1 on v0

v1 whole, which is shorter than its diff:
```python
import functools

import jax
import jax.numpy as jnp
from jax import lax
from jax.experimental import pallas as pl
from jax.experimental.pallas import tpu as pltpu
from jax.sharding import Mesh
from jax.sharding import PartitionSpec as P

QUERY_HEADS = 20
KEY_VALUE_HEADS = 5
HEAD_DIM = 64
GROUP = QUERY_HEADS // KEY_VALUE_HEADS
QUERY_COLUMNS = QUERY_HEADS * HEAD_DIM
KEY_COLUMNS = KEY_VALUE_HEADS * HEAD_DIM
NORM_EPS = 1e-06

ALL = ("y", "core", "zh", "zl", "x")
SEQ = ("zh", "zl", "x")
TEAM = ("core", "zl", "x")
CHIPS = ("zl", "x")

bf16 = jnp.bfloat16
f32 = jnp.float32


def dot_nn(left, right):
    return jnp.dot(left, right, preferred_element_type=f32)


def dot_nt(left, right):
    return lax.dot_general(left, right, (((1,), (1,)), ((), ())), preferred_element_type=f32)


def dot_tn(left, right):
    return lax.dot_general(left, right, (((0,), (0,)), ((), ())), preferred_element_type=f32)


def row_scale(values):
    return lax.rsqrt(jnp.mean(values * values, axis=-1, keepdims=True) + NORM_EPS)


def head_norm(values):
    scale = lax.rsqrt(jnp.mean(values * values, axis=-1, keepdims=True) + NORM_EPS)
    return values * scale, scale


def turn(values):
    half = HEAD_DIM // 2
    return jnp.concatenate([-values[:, half:], values[:, :half]], axis=1)


def turn_back(values):
    half = HEAD_DIM // 2
    return jnp.concatenate([values[:, half:], -values[:, :half]], axis=1)


def heads_forward_kernel(qkv_ref, cos_ref, sin_ref, gq_ref, gk_ref, q_ref, kv_ref):
    cosine, sine = cos_ref[...], sin_ref[...]
    for head in range(QUERY_HEADS + KEY_VALUE_HEADS):
        columns = slice(head * HEAD_DIM, (head + 1) * HEAD_DIM)
        normed, _ = head_norm(qkv_ref[:, columns])
        if head < QUERY_HEADS:
            scaled = normed * gq_ref[...]
            turned = (scaled * cosine + turn(scaled) * sine) * (HEAD_DIM**-0.5)
            q_ref[:, columns] = turned.astype(bf16)
        else:
            scaled = normed * gk_ref[...]
            turned = scaled * cosine + turn(scaled) * sine
            place = slice((head - QUERY_HEADS) * HEAD_DIM, (head - QUERY_HEADS + 1) * HEAD_DIM)
            kv_ref[:, place] = turned.astype(bf16)
    kv_ref[:, KEY_COLUMNS:] = qkv_ref[:, QUERY_COLUMNS + KEY_COLUMNS :].astype(bf16)


def heads_backward_kernel(
    back, qkv_ref, cos_ref, sin_ref, gq_ref, gk_ref, dq_ref, own_ref, *refs
):
    received = refs[:back]
    grad_ref, gain_ref = refs[back:]
    cosine, sine = cos_ref[...], sin_ref[...]
    kv_grad = own_ref[...]
    for piece in received:
        kv_grad = kv_grad + piece[...].astype(f32)
    totals = [jnp.zeros((1, HEAD_DIM), f32), jnp.zeros((1, HEAD_DIM), f32)]
    for head in range(QUERY_HEADS + KEY_VALUE_HEADS):
        columns = slice(head * HEAD_DIM, (head + 1) * HEAD_DIM)
        normed, scale = head_norm(qkv_ref[:, columns])
        is_key = int(head >= QUERY_HEADS)
        if is_key:
            place = slice((head - QUERY_HEADS) * HEAD_DIM, (head - QUERY_HEADS + 1) * HEAD_DIM)
            grad = kv_grad[:, place]
            gain = gk_ref[...]
        else:
            grad = dq_ref[:, columns] * (HEAD_DIM**-0.5)
            gain = gq_ref[...]
        grad = grad * cosine + turn_back(grad * sine)
        totals[is_key] = totals[is_key] + jnp.sum(grad * normed, axis=0, keepdims=True)
        weighted = grad * gain
        inner = jnp.mean(weighted * normed, axis=-1, keepdims=True)
        grad_ref[:, columns] = (scale * (weighted - normed * inner)).astype(bf16)
    grad_ref[:, QUERY_COLUMNS + KEY_COLUMNS :] = kv_grad[:, KEY_COLUMNS:].astype(bf16)
    gain_ref[...] = jnp.concatenate(totals, axis=1)


def block_masks(back, tokens, pos_ref):
    key = lax.broadcasted_iota(jnp.int32, (tokens, GROUP * tokens), 0)
    query = lax.broadcasted_iota(jnp.int32, (tokens, GROUP * tokens), 1) % tokens
    offset = key - query
    low = -pos_ref[...]
    masks = [(offset <= 0) & (offset >= low)]
    for step in range(1, back + 1):
        masks.append(offset - step * tokens >= low)
    return masks


def stack_heads(ref, group):
    return jnp.concatenate(
        [
            ref[:, (group * GROUP + m) * HEAD_DIM : (group * GROUP + m + 1) * HEAD_DIM]
            for m in range(GROUP)
        ],
        axis=0,
    )


def key_value(ref, group):
    key = ref[:, group * HEAD_DIM : (group + 1) * HEAD_DIM]
    value = ref[:, KEY_COLUMNS + group * HEAD_DIM : KEY_COLUMNS + (group + 1) * HEAD_DIM]
    return key, value


def attend_forward_kernel(back, pos_ref, q_ref, *refs):
    kv_refs = refs[: back + 1]
    out_ref, inverse_ref = refs[back + 1 :]
    tokens = q_ref.shape[0]
    masks = block_masks(back, tokens, pos_ref)
    inverse_ref[...] = jnp.zeros_like(inverse_ref)
    for group in range(KEY_VALUE_HEADS):
        queries = stack_heads(q_ref, group)
        total = jnp.zeros((1, GROUP * tokens), f32)
        summed = jnp.zeros((HEAD_DIM, GROUP * tokens), f32)
        for step in range(back + 1):
            key, value = key_value(kv_refs[step], group)
            exponent = jnp.where(masks[step], jnp.exp(dot_nt(key, queries)), 0.0)
            total = total + jnp.sum(exponent, axis=0, keepdims=True)
            summed = summed + dot_tn(value, exponent.astype(bf16))
        inverse = 1.0 / total
        inverse_ref[group : group + 1, :] = inverse
        heads = summed * inverse
        for m in range(GROUP):
            head = group * GROUP + m
            out_ref[:, head * HEAD_DIM : (head + 1) * HEAD_DIM] = (
                heads[:, m * tokens : (m + 1) * tokens].T.astype(bf16)
            )


def attend_backward_kernel(back, pos_ref, q_ref, do_ref, inverse_ref, *refs):
    kv_refs = refs[: back + 1]
    dq_ref = refs[back + 1]
    dkv_refs = refs[back + 2 :]
    tokens = q_ref.shape[0]
    masks = block_masks(back, tokens, pos_ref)
    for group in range(KEY_VALUE_HEADS):
        queries = stack_heads(q_ref, group)
        out_grads = stack_heads(do_ref, group)
        inverse = inverse_ref[group : group + 1, :]
        chances, chance_grads = [], []
        row_dot = jnp.zeros((1, GROUP * tokens), f32)
        for step in range(back + 1):
            key, value = key_value(kv_refs[step], group)
            chance = jnp.where(masks[step], jnp.exp(dot_nt(key, queries)) * inverse, 0.0)
            chance_grad = dot_nt(value, out_grads)
            row_dot = row_dot + jnp.sum(chance * chance_grad, axis=0, keepdims=True)
            chances.append(chance)
            chance_grads.append(chance_grad)
        query_grad = jnp.zeros((HEAD_DIM, GROUP * tokens), f32)
        for step in range(back + 1):
            key, _ = key_value(kv_refs[step], group)
            score_grad = (chances[step] * (chance_grads[step] - row_dot)).astype(bf16)
            target = dkv_refs[step]
            target[:, group * HEAD_DIM : (group + 1) * HEAD_DIM] = dot_nn(
                score_grad, queries
            ).astype(target.dtype)
            target[:, KEY_COLUMNS + group * HEAD_DIM : KEY_COLUMNS + (group + 1) * HEAD_DIM] = (
                dot_nn(chances[step].astype(bf16), out_grads).astype(target.dtype)
            )
            query_grad = query_grad + dot_tn(key, score_grad)
        for m in range(GROUP):
            head = group * GROUP + m
            dq_ref[:, head * HEAD_DIM : (head + 1) * HEAD_DIM] = query_grad[
                :, m * tokens : (m + 1) * tokens
            ].T


def whole(kernel, out_shapes, name, flops, moved):
    return pl.pallas_call(
        kernel,
        out_shape=out_shapes,
        name=name,
        compiler_params=pltpu.CompilerParams(vmem_limit_bytes=48 << 20),
        cost_estimate=pl.CostEstimate(flops=flops, transcendentals=0, bytes_accessed=moved),
    )


def swap(value, axis, k):
    n = lax.axis_size(axis)
    return lax.ppermute(value, axis, [(i, i ^ k) for i in range(n)])


def shifted(value, step):
    n = lax.axis_size(SEQ)
    return lax.ppermute(value, SEQ, [(i, i + step) for i in range(n) if 0 <= i + step < n])


def spread_columns(pieces):
    team = lax.axis_size(TEAM)
    rows = pieces[0].shape[0]
    ny, nzh = lax.axis_size("y"), lax.axis_size("zh")
    blocks = jnp.concatenate([p.reshape(rows, team, -1) for p in pieces], axis=2)
    blocks = blocks.transpose(1, 0, 2)
    blocks = lax.all_to_all(blocks, TEAM, 0, 0, tiled=True)
    width = blocks.shape[2]
    nc = lax.axis_size("core")
    block = blocks.reshape(1, nc, 1, -1, width)
    full = jnp.zeros((ny, nc, nzh, block.shape[3], width), bf16)
    y, zh = lax.axis_index("y"), lax.axis_index("zh")
    far = [block] + [swap(block, "zh", b) for b in range(1, nzh)]
    for b in range(nzh):
        for a in range(ny):
            piece = far[b] if a == 0 else swap(far[b], "y", a)
            full = lax.dynamic_update_slice(full, piece, (y ^ a, 0, zh ^ b, 0, 0))
    return full.reshape(-1, width)


def reduce_rows(partial, shape):
    y, zh = lax.axis_index("y"), lax.axis_index("zh")
    ny, nzh = lax.axis_size("y"), lax.axis_size("zh")
    partial = partial.reshape(shape)
    total = lax.dynamic_index_in_dim(partial, y, 0, keepdims=False).astype(f32)
    for a in range(1, ny):
        total = total + swap(
            lax.dynamic_index_in_dim(partial, y ^ a, 0, keepdims=False), "y", a
        ).astype(f32)
    out = lax.dynamic_index_in_dim(total, zh, 1, keepdims=False)
    for b in range(1, nzh):
        out = out + swap(
            lax.dynamic_index_in_dim(total, zh ^ b, 1, keepdims=False).astype(bf16), "zh", b
        ).astype(f32)
    return out


def collect_columns(partial, count):
    ny, nzh, nc = lax.axis_size("y"), lax.axis_size("zh"), lax.axis_size("core")
    team = lax.axis_size(TEAM)
    total = reduce_rows(partial, (ny, nc, nzh, -1, partial.shape[1]))
    blocks = total.astype(bf16).reshape(team, -1, partial.shape[1])
    blocks = lax.all_to_all(blocks, TEAM, 0, 0, tiled=True)
    rows = blocks.shape[1]
    width = partial.shape[1] // count
    return [
        blocks[:, :, i * width : (i + 1) * width]
        .transpose(1, 0, 2)
        .reshape(rows, team * width)
        .astype(f32)
        for i in range(count)
    ]


def team_sum(partial):
    nc = lax.axis_size("core")
    chips = lax.axis_size(CHIPS)
    core = lax.axis_index("core")
    width = partial.shape[1]
    halves = partial.reshape(nc, -1, width)
    total = lax.dynamic_index_in_dim(halves, core, 0, keepdims=False).astype(f32)
    for k in range(1, nc):
        total = total + swap(
            lax.dynamic_index_in_dim(halves, core ^ k, 0, keepdims=False), "core", k
        ).astype(f32)
    blocks = total.astype(bf16).reshape(chips, -1, width)
    blocks = lax.all_to_all(blocks, CHIPS, 0, 0, tiled=True)
    return jnp.sum(blocks.astype(f32), axis=0)


def row_team(value):
    tokens = value.shape[0]
    ny, nc, nzh = lax.axis_size("y"), lax.axis_size("core"), lax.axis_size("zh")
    chips, team = lax.axis_size(CHIPS), lax.axis_size(TEAM)
    split = value.reshape(tokens, ny, nc, nzh, chips, -1).transpose(2, 4, 0, 1, 3, 5)
    split = split.reshape(team, tokens, -1)
    return lax.all_to_all(split, TEAM, 0, 0, tiled=True).reshape(team * tokens, -1)


def row_grads(row_side, column_side):
    ny, nzh = lax.axis_size("y"), lax.axis_size("zh")
    partial = dot_tn(row_side, column_side).astype(bf16)
    return reduce_rows(partial, (ny, 1, nzh, -1, partial.shape[1])).reshape(-1, partial.shape[1])


def sum_all(value):
    for axis in ("core", "x", "y", "zl", "zh"):
        k = 1
        while k < lax.axis_size(axis):
            value = value + swap(value, axis, k)
            k *= 2
    return value


def local(
    layer_input,
    segments,
    positions,
    query_key_value_weight,
    w_out,
    w_gate,
    w_up,
    w_down,
    g_attn,
    g_ffn,
    g_query,
    g_key,
    cotangent,
):
    tokens, model = layer_input.shape
    back = lax.axis_size(SEQ) // 2
    ff = w_gate.shape[1] // lax.axis_size(TEAM)

    inputs = layer_input.astype(f32)
    scale_in = row_scale(inputs)
    normed_in = inputs * scale_in
    normed_low = (normed_in * g_attn).astype(bf16)

    qkv_full = lax.all_gather(query_key_value_weight, ALL, axis=0, tiled=True)
    out_full = lax.all_gather(w_out, ALL, axis=0, tiled=True)
    gate_up = spread_columns([w_gate, w_up])
    down = spread_columns([w_down])
    grads_out = lax.all_gather(cotangent, TEAM, axis=0, tiled=True)

    joined = dot_nn(normed_low, qkv_full)

    half = HEAD_DIM // 2
    frequency = 10000.0 ** (-jnp.arange(half, dtype=f32) / half)
    angles = positions.astype(f32)[:, None] * frequency[None, :]
    angles = jnp.concatenate([angles, angles], axis=-1)
    cosine, sine = jnp.cos(angles), jnp.sin(angles)
    gq, gk = g_query[None, :], g_key[None, :]
    query_low, kv_low = whole(
        heads_forward_kernel,
        (
            jax.ShapeDtypeStruct((tokens, QUERY_COLUMNS), bf16),
            jax.ShapeDtypeStruct((tokens, 2 * KEY_COLUMNS), bf16),
        ),
        "heads_forward",
        tokens * 1920 * 20,
        tokens * 1920 * 6,
    )(joined, cosine, sine, gq, gk)

    kv_blocks = [kv_low] + [shifted(kv_low, step) for step in range(1, back + 1)]
    tiled_positions = jnp.tile(positions[None, :], (1, GROUP))
    attended, inverse = whole(
        functools.partial(attend_forward_kernel, back),
        (
            jax.ShapeDtypeStruct((tokens, QUERY_COLUMNS), bf16),
            jax.ShapeDtypeStruct((8, GROUP * tokens), f32),
        ),
        "attend_forward",
        4 * tokens * tokens * (back + 1) * QUERY_COLUMNS,
        tokens * 2000 * 10,
    )(tiled_positions, query_low, *kv_blocks)

    middle = inputs + dot_nt(attended, out_full)
    scale_mid = row_scale(middle)
    normed_mid = middle * scale_mid
    mid_low = (normed_mid * g_ffn).astype(bf16)
    mid_team = lax.all_gather(mid_low, TEAM, axis=0, tiled=True)

    gate_pre = dot_nn(mid_team, gate_up[:, :ff])
    up_pre = dot_nn(mid_team, gate_up[:, ff:])
    sigmoid_gate = jax.nn.sigmoid(gate_pre)
    activated = gate_pre * sigmoid_gate
    hidden = (activated * up_pre).astype(bf16)
    hidden_grad = dot_nn(grads_out, down)
    slope = sigmoid_gate * (1.0 + gate_pre * (1.0 - sigmoid_gate))
    gate_grad = (hidden_grad * up_pre * slope).astype(bf16)
    up_grad = (hidden_grad * activated).astype(bf16)
    gate_up_grad = jnp.concatenate([gate_grad, up_grad], axis=1)
    mid_grad = team_sum(dot_nt(gate_up_grad, gate_up).astype(bf16))
    branch_two = team_sum(dot_nt(hidden, down).astype(bf16))
    result = (middle + branch_two).astype(bf16)

    w_down_grad = collect_columns(dot_tn(grads_out, hidden).astype(bf16), 1)[0]
    w_gate_grad, w_up_grad = collect_columns(dot_tn(mid_team, gate_up_grad).astype(bf16), 2)

    weighted = mid_grad * g_ffn
    ffn_gain = jnp.sum(mid_grad * normed_mid, axis=0)
    middle_grad = cotangent.astype(f32) + scale_mid * (
        weighted - normed_mid * jnp.mean(weighted * normed_mid, axis=-1, keepdims=True)
    )
    branch_grad = middle_grad.astype(bf16)
    head_grads = dot_nn(branch_grad, out_full).astype(bf16)

    results = whole(
        functools.partial(attend_backward_kernel, back),
        (
            jax.ShapeDtypeStruct((tokens, QUERY_COLUMNS), f32),
            jax.ShapeDtypeStruct((tokens, 2 * KEY_COLUMNS), f32),
        )
        + (jax.ShapeDtypeStruct((tokens, 2 * KEY_COLUMNS), bf16),) * back,
        "attend_backward",
        10 * tokens * tokens * (back + 1) * QUERY_COLUMNS,
        tokens * 2000 * 20,
    )(tiled_positions, query_low, head_grads, inverse, *kv_blocks)
    query_grad, own_grad, far_grads = results[0], results[1], results[2:]
    received = [shifted(grad, -(i + 1)) for i, grad in enumerate(far_grads)]
    joined_grad, head_gains = whole(
        functools.partial(heads_backward_kernel, back),
        (
            jax.ShapeDtypeStruct((tokens, joined.shape[1]), bf16),
            jax.ShapeDtypeStruct((1, 2 * HEAD_DIM), f32),
        ),
        "heads_backward",
        tokens * 1920 * 30,
        tokens * 1920 * 16,
    )(joined, cosine, sine, gq, gk, query_grad, own_grad, *received)

    attended_team = lax.all_gather(attended, TEAM, axis=0, tiled=True)
    w_out_grad = row_grads(row_team(branch_grad), attended_team)
    joined_team = lax.all_gather(joined_grad, TEAM, axis=0, tiled=True)
    w_qkv_grad = row_grads(row_team(normed_low), joined_team)

    normed_in_grad = dot_nt(joined_grad, qkv_full)
    weighted_in = normed_in_grad * g_attn
    attn_gain = jnp.sum(normed_in_grad * normed_in, axis=0)
    input_grad = (
        middle_grad
        + scale_in
        * (weighted_in - normed_in * jnp.mean(weighted_in * normed_in, axis=-1, keepdims=True))
    ).astype(bf16)

    gains = sum_all(
        jnp.concatenate([attn_gain, ffn_gain, head_gains[0]], axis=0).reshape(-1, 128)
    ).reshape(-1)
    return (
        result,
        input_grad,
        w_qkv_grad,
        w_out_grad,
        w_gate_grad,
        w_up_grad,
        w_down_grad,
        gains[:model],
        gains[model : 2 * model],
        gains[2 * model : 2 * model + HEAD_DIM],
        gains[2 * model + HEAD_DIM :],
    )


def solution(mesh):
    inner, outer = mesh.devices.shape
    split = Mesh(mesh.devices.reshape(inner // 2, 2, 2, 2, outer // 4), ALL)
    rows, whole_array = P(ALL, None), P()
    in_specs = (rows, P(ALL), P(ALL)) + (rows,) * 5 + (whole_array,) * 4 + (rows,)
    out_specs = (rows,) * 7 + (whole_array,) * 4
    return jax.shard_map(local, mesh=split, in_specs=in_specs, out_specs=out_specs, check_vma=False)
```

time: 4670 us -> 672 us (0.14)
  waiting for transfers between devices: 3830 us -> 361 us
  matrix products: 270 us -> 77.3 us
  blocking collectives: 136 us -> 0 us
  local copies, waits for them, and re-layouts: 200 us -> 77.1 us
  loops' own time: 106 us -> 0 us
  starting transfers between devices: 1.01 us -> 72.4 us
  other arithmetic: 94.1 us -> 34.3 us
    reduce_scatter x1 -> x0, waiting for transfers between devices: 1750 us -> none  [spread_all(): lax.psum_scatter(term_fn(jnp.int32(0), share_rows * lax.axis_size(('inner...]
    unnamed x10 -> x6, waiting for transfers between devices: 1220 us -> 2.62 us
    while x20 -> x0, waiting for transfers between devices: 602 us -> none
    ppermute x0 -> x29, waiting for transfers between devices: none -> 199 us  [the longest x21 171 us: swap(): return lax.ppermute(value, axis, [(i, i ^ k) for i in range(n)])]
    dot_general x155 -> x13, matrix products: 270 us -> 77.3 us  [the longest x4 28.7 us: dot_nt(): lax.dot_general(left, right, (((1,), (1,)), ((), ())), preferred_element_...]
    all_gather x5 -> x6, waiting for transfers between devices: 262 us -> 114 us  [the longest x1 76.2 us: local(): qkv_full = lax.all_gather(query_key_value_weight, ALL, axis=0, tiled=True)]
    another operation x7 -> x0, loops' own time: 106 us -> none  [the longest x1 78.9 us: attend_forward(): return lax.map(one_head, jnp.arange(QUERY_HEADS))]
    all_gather x3 -> x0, blocking collectives: 85.5 us -> none  [the longest x1 33.4 us: local(): lax.all_gather(value_low, 'outer', axis=0, tiled=True)]
  transfers between devices with their start and end apart: 18 -> 43, of which waited for: 16 -> 16; matrix products, arithmetic and copies ran while one was open for 7% -> 24% of each run, Pallas kernels for 0% -> 4%
where the time goes in v1:
time: 672 us; the launch traced here: 662 us
  waiting for transfers between devices  361 us (54%)
  matrix products  77.3 us (12%)
  local copies, waits for them, and re-layouts  77.1 us (11%)
  starting transfers between devices  72.4 us (11%)
  other arithmetic  34.3 us (5%)
  Pallas kernels  24.4 us (4%)
  between operations  15.4 us (2%)
    ppermute x21, waiting for transfers between devices, swap(): return lax.ppermute(value, axis, [(i, i ^ k) for i in range(n)])  171 us
    all_gather x1, waiting for transfers between devices, local(): qkv_full = lax.all_gather(query_key_value_weight, ALL, axis=0, tiled=True)  76.2 us
    all_to_all x2, waiting for transfers between devices, spread_columns(): blocks = lax.all_to_all(blocks, TEAM, 0, 0, tiled=True)  39.4 us
    all_gather x1, waiting for transfers between devices, local(): out_full = lax.all_gather(w_out, ALL, axis=0, tiled=True)  38.1 us
    dot_general x4, matrix products, dot_nt(): lax.dot_general(left, right, (((1,), (1,)), ((), ())), preferred_element_...  28.7 us
    dot_general x5, matrix products, dot_nn(): return jnp.dot(left, right, preferred_element_type=f32)  28.2 us
    ppermute x8, waiting for transfers between devices, shifted(): lax.ppermute(value, SEQ, [(i, i + step) for i in range(n) if 0 <= i + ste...  27.6 us
    dot_general x4, matrix products, dot_tn(): lax.dot_general(left, right, (((0,), (0,)), ((), ())), preferred_element_...  20.3 us
  transfers between devices with their start and end apart: 43, of which 16 were waited for; matrix products, arithmetic and copies ran while one was open for 24% of the time, Pallas kernels for 4%

profile of v1, /device:TPU:0, one launch (start us, length us, event | category | flops | bytes accessed | tf_op | source)
XLA Modules:
  0.0 662.3 jit_solution(9070302019061866709)
XLA Ops:
  13.0 76.2 %all-gather.7.cloned.1.call-done = bf16[2048,1920]{1,0:T(8,128)(2,1)} async-done(((bf16[64,1920]{1,0:T(8,128)(2,1)}), bf16[2048,1920]{1,0:T(8,128)(2,1)}) %all-gather.7.cloned.1.call-update) | async-done | bytes 7864336 | tf_op jit(solution)/shard_map/all_gather | solution.py:334
  89.2 4.6 fusion.38.qkv_ref
  93.8 4.9 heads_forward.1
  102.0 3.4 collective-permute-start.1
  111.2 4.2 all-to-all-start.1
  118.8 6.1 attend_forward.1
  124.9 38.1 %all-gather.9.cloned.1.call-done = bf16[2048,1280]{1,0:T(8,128)(2,1)} async-done(((bf16[64,1280]{1,0:T(8,128)(2,1)}), bf16[2048,1280]{1,0:T(8,128)(2,1)}) %all-gather.9.cloned.1.call-update) | async-done | bytes 5242896 | tf_op jit(solution)/shard_map/all_gather | solution.py:335
  163.0 4.6 multiply_reduce_fusion.2
  172.4 4.5 all-to-all-start
  180.7 39.4 %all-to-all-done = bf16[8,64,1280]{2,1,0:T(8,128)(2,1)} async-done(((bf16[8,64,1280]{2,1,0:T(8,128)(2,1)}), bf16[8,64,1280]{2,1,0:T(8,128)(2,1)}, u32[]{:S(2)}, u32[]{:S(2)}) %all-to-all-start) | async-done | bytes 1310752 | tf_op jit(solution)/shard_map/all_to_all | solution.py:222
  231.0 48.6 %collective-permute-done.5 = bf16[1,2,1,256,1280]{4,3,1,2,0:T(8,128)(2,1)} collective-permute-done((bf16[1,2,1,256,1280]{4,3,1,2,0:T(8,128)(2,1)}, bf16[1,2,1,256,1280]{4,3,1,2,0:T(8,128)(2,1)}, u32[]{:S(2)}, u32[]{:S(2)}) %collective-permute-start.5) | collective-permute-done | bytes 1310752 | tf_op jit(solution)/shard_map/ppermute | solution.py:208
  281.1 3.4 bitcast_dynamic-update-slice_fusion.2
  287.1 23.4 %collective-permute-done.6 = bf16[1,2,1,256,1280]{4,3,1,2,0:T(8,128)(2,1)S(1)} collective-permute-done((bf16[1,2,1,256,1280]{4,3,1,2,0:T(8,128)(2,1)}, bf16[1,2,1,256,1280]{4,3,1,2,0:T(8,128)(2,1)S(1)}, u32[]{:S(2)}, u32[]{:S(2)}) %collective-permute-start.6) | collective-permute-done | bytes 1310752 | tf_op jit(solution)/shard_map/ppermute | solution.py:208
  311.7 7.5 %fusion.39 = f32[640,1024]{1,0:T(8,128)} fusion(bf16[2048,640]{1,0:T(8,128)(2,1)} %bitcast.192, bf16[1024,2048]{1,0:T(8,128)(2,1)} %all-gather.13.cloned.1.call-done), kind=kOutput, calls=%fused_computation.105 | convolution fusion | flops 2684354560 | bytes 9437184 | tf_op jit(solution)/shard_map/dot_general | solution.py:29
  319.2 5.7 fusion.5
  324.9 6.9 %fusion.9 = (bf16[1024,640]{0,1:T(8,128)(2,1)S(1)}, bf16[1024,640]{0,1:T(8,128)(2,1)S(1)}, bf16[1024,640]{0,1:T(8,128)(2,1)}) fusion(f32[640,1024]{1,0:T(8,128)S(1)} %copy-done.23, f32[1024,640]{0,1:T(8,128)S(1)} %fusion.5, bf16[1024,2048]{1,0:T(8,128)(2,1)S(1)} %copy-done.21, bf16[2048,1280]{1,0:T(8,128)(2,1)} %bitcast.9), kind=kOutput, calls=%fused_computation.23 | convolution fusion | flops 2694184960 | bytes 15990784 | tf_op jit(solution)/shard_map/dot_general | solution.py:29
  331.8 9.3 %convolution_convert_fusion.1 = bf16[1024,2048]{1,0:T(8,128)(2,1)S(1)} fusion(bf16[2048,1280]{1,0:T(8,128)(2,1)} %bitcast.9, bf16[1024,640]{0,1:T(8,128)(2,1)S(1)} %get-tuple-element.40, bf16[1024,640]{0,1:T(8,128)(2,1)S(1)} %get-tuple-element.39), kind=kOutput, calls=%fused_computation.8 | convolution fusion | flops 5376049152 | bytes 12058624 | tf_op jit(solution)/shard_map/dot_general | solution.py:33
  348.7 4.2 all-to-all-start.4
  353.4 6.9 %fusion.2 = bf16[2048,640]{0,1:T(8,128)(2,1)} fusion(bf16[1024,640]{0,1:T(8,128)(2,1)} %get-tuple-element.41, bf16[1024,2048]{1,0:T(8,128)(2,1)} %all-gather.13.cloned.1.call-done), kind=kOutput, calls=%fused_computation.11 | convolution fusion | flops 2685665280 | bytes 8126464 | tf_op jit(solution)/shard_map/dot_general | solution.py:37
  360.4 13.6 %reshape.240 = bf16[2,2,2,256,640]{3,2,1,0,4:T(2,128)(2,1)} reshape(bf16[2048,640]{0,1:T(8,128)(2,1)} %fusion.2) | data formatting | bytes 5242880 | tf_op jit(solution)/shard_map/reshape | solution.py:239
  374.0 5.0 constant_dynamic-slice_fusion.1
  379.0 4.3 copy.100
  384.8 7.7 %convolution_convert_fusion.2 = bf16[1024,2048]{1,0:T(8,128)(2,1)} fusion(bf16[1024,640]{0,1:T(8,128)(2,1)} %get-tuple-element.41, bf16[2048,640]{1,0:T(8,128)(2,1)} %bitcast.193), kind=kOutput, calls=%fused_computation.9 | convolution fusion | flops 2686451712 | bytes 8126464 | tf_op jit(solution)/shard_map/dot_general | solution.py:33
  392.4 4.3 copy.102
  396.7 3.4 dynamic-slice_bitcast_fusion.2
  400.2 3.7 fusion
  404.0 4.5 all-to-all-start.3
  408.5 6.3 collective-permute-done.22
  416.9 7.2 %convolution_convert_fusion = bf16[2048,1280]{1,0:T(8,128)(2,1)S(1)} fusion(bf16[1024,2048]{1,0:T(8,128)(2,1)S(1)} %copy-done.22, bf16[1024,640]{0,1:T(8,128)(2,1)} %copy-done.26, bf16[1024,640]{0,1:T(8,128)(2,1)S(1)} %copy-done.25), kind=kOutput, calls=%fused_computation | convolution fusion | flops 5376573440 | bytes 12058624 | tf_op jit(solution)/shard_map/dot_general | solution.py:37
  429.5 16.4 %collective-permute-done.23 = bf16[2,256,640]{2,1,0:T(8,128)(2,1)S(1)} collective-permute-done((bf16[2,256,640]{2,1,0:T(8,128)(2,1)S(1)}, bf16[2,256,640]{2,1,0:T(8,128)(2,1)S(1)}, u32[]{:S(2)}, u32[]{:S(2)}) %collective-permute-start.23) | collective-permute-done | bytes 655392 | tf_op jit(solution)/shard_map/ppermute | solution.py:208
  446.9 3.8 fusion.1
  450.6 5.1 all-to-all-start.7
  460.0 6.5 all-to-all-done.7
  466.5 4.5 all-to-all-start.2
  471.0 3.5 convolution_convert_fusion.6.do_ref
  474.5 6.2 attend_backward.1
  486.2 13.8 %collective-permute-done.12.refs_0_ = bf16[128,640]{1,0:T(8,128)(2,1)S(1)} collective-permute-done((bf16[128,640]{1,0:T(8,128)(2,1)S(1)}, bf16[128,640]{1,0:T(8,128)(2,1)S(1)}, u32[]{:S(2)}, u32[]{:S(2)}) %collective-permute-start.12) | collective-permute-done | bytes 163872 | tf_op jit(solution)/shard_map/ppermute | solution.py:213
  500.0 10.6 %collective-permute-done.13.refs_1_ = bf16[128,640]{1,0:T(8,128)(2,1)S(1)} collective-permute-done((bf16[128,640]{1,0:T(8,128)(2,1)S(1)}, bf16[128,640]{1,0:T(8,128)(2,1)S(1)}, u32[]{:S(2)}, u32[]{:S(2)}) %collective-permute-start.13) | collective-permute-done | bytes 163872 | tf_op jit(solution)/shard_map/ppermute | solution.py:213
  510.6 7.2 %heads_backward.1 = (bf16[128,1920]{1,0:T(8,128)(2,1)}, f32[1,128]{1,0:T(1,128)S(1)}) custom-call(f32[128,1920]{1,0:T(8,128)S(1)} %fusion.38.qkv_ref, f32[128,64]{1,0:T(8,128)S(1)} %get-tuple-element.49.cos_ref, f32[128,64]{1,0:T(8,128)S(1)} %get-tuple-element.48.sin_ref, f32[1,64]{1,0:T(1,128)S(1)} %bitcast.176, f32[1,64]{1,0:T(1,128)S(1)} %bitcast.178, ...), custom_call_target="tpu_custom_call" | custom-call | flops 7372800 | bytes 3932160 | tf_op jit(solution)/shard_map/heads_backward/pallas_call | solution.py:416
  527.9 3.8 all-to-all-start.5
  531.7 7.1 %fusion.24 = (f32[2048]{0:T(1024)S(1)}, f32[128]{0:T(128)S(1)}, f32[128,2048]{1,0:T(8,128)}) fusion(bf16[128,2048]{1,0:T(8,128)(2,1)S(1)} %copy-done.5, f32[128]{0:T(128)S(1)} %add_rsqrt_fusion.1, f32[2048]{0:T(1024)S(1)} %copy-done.19, bf16[128,1920]{1,0:T(8,128)(2,1)} %get-tuple-element.33, bf16[2048,1920]{1,0:T(8,128)(2,1)} %all-gather.7.cloned.1.call-done), kind=kOutput, calls=%fused_computation.59 | convolution fusion | flops 1008465792 | bytes 9946112 | tf_op jit(solution)/shard_map/dot_general | solution.py:33
  539.3 44.7 %collective-permute-done.21 = bf16[2,256,1280]{2,1,0:T(8,128)(2,1)} collective-permute-done((bf16[2,256,1280]{2,1,0:T(8,128)(2,1)}, bf16[2,256,1280]{2,1,0:T(8,128)(2,1)}, u32[]{:S(2)}, u32[]{:S(2)}) %collective-permute-start.21) | collective-permute-done | bytes 1310752 | tf_op jit(solution)/shard_map/ppermute | solution.py:208
  584.0 3.5 fusion.7
  587.6 4.6 all-to-all-start.6
  601.6 8.2 %collective-permute-done.27 = f32[33,128]{1,0:T(8,128)S(1)} collective-permute-done((f32[33,128]{1,0:T(8,128)S(1)}, f32[33,128]{1,0:T(8,128)S(1)}, u32[]{:S(2)}, u32[]{:S(2)}) %collective-permute-start.27) | collective-permute-done | bytes 16928 | tf_op jit(solution)/shard_map/ppermute | solution.py:208
  627.0 3.6 convolution_convert_fusion.5
  631.8 10.5 %collective-permute-done.16 = bf16[1,2,64,1920]{3,2,1,0:T(8,128)(2,1)S(1)} collective-permute-done((bf16[1,2,64,1920]{3,2,1,0:T(8,128)(2,1)S(1)}, bf16[1,2,64,1920]{3,2,1,0:T(8,128)(2,1)S(1)}, u32[]{:S(2)}, u32[]{:S(2)}) %collective-permute-start.16) | collective-permute-done | bytes 491552 | tf_op jit(solution)/shard_map/ppermute | solution.py:208
  643.7 10.4 %collective-permute-done.17 = bf16[1,64,1920]{2,1,0:T(8,128)(2,1)S(1)} collective-permute-done((bf16[1,64,1920]{2,1,0:T(8,128)(2,1)S(1)}, bf16[1,64,1920]{2,1,0:T(8,128)(2,1)S(1)}, u32[]{:S(2)}, u32[]{:S(2)}) %collective-permute-start.17) | collective-permute-done | bytes 245792 | tf_op jit(solution)/shard_map/ppermute | solution.py:208
  (190 shorter events, 111.2 us)
Async XLA Ops:
  7.2 82.0 %all-gather.7.cloned.1.call-start = ((), (), s32[]{:S(2)}) async-start(), calls=%async_computation.8 | async-start | bytes 8110080 | tf_op jit(solution)/shard_map/all_gather | solution.py:334
  7.9 155.1 %all-gather.9.cloned.1.call-start = ((), (), s32[]{:S(2)}) async-start(), calls=%async_computation.9 | async-start | bytes 5406720 | tf_op jit(solution)/shard_map/all_gather | solution.py:335
  8.7 303.0 %all-gather.13.cloned.1.call-start = ((), (), s32[]{:S(2)}) async-start(), calls=%async_computation.11 | async-start | bytes 4718592 | tf_op jit(solution)/shard_map/all_gather | solution.py:338
  13.0 80.8 %copy-start.6 = (bf16[128,2048]{1,0:T(8,128)(2,1)}, bf16[128,2048]{1,0:T(8,128)(2,1)S(1)}, u32[]{:S(2)}) copy-start(bf16[128,2048]{1,0:T(8,128)(2,1)S(1)} %fusion.18) | copy-start | bytes 1572868
  13.0 80.8 %copy-start = (f32[64]{0:T(128)S(1)}, f32[64]{0:T(128)}, u32[]{:S(2)}) copy-start(f32[64]{0:T(128)} %param.22) | copy-start | bytes 772
  13.0 80.8 %copy-start.1 = (f32[64]{0:T(128)S(1)}, f32[64]{0:T(128)}, u32[]{:S(2)}) copy-start(f32[64]{0:T(128)} %param.23) | copy-start | bytes 772
  93.8 25.0 %copy-start.20 = (s32[128]{0:T(128)S(1)}, s32[128]{0:T(128)}, u32[]{:S(2)}) copy-start(s32[128]{0:T(128)} %param.14) | copy-start | bytes 1540
  98.7 16.8 %collective-permute-start = (bf16[128,640]{1,0:T(8,128)(2,1)S(1)}, bf16[128,640]{1,0:T(8,128)(2,1)S(1)}, u32[]{:S(2)}, u32[]{:S(2)}) collective-permute-start(bf16[128,640]{1,0:T(8,128)(2,1)S(1)} %get-tuple-element.24.refs_0_), channel_id=1, source_target_pairs={{0,1},{1,2},{2,3},{3,4},{4,5},{5,6},{6,7},{8,9},{9,10},{10,11},{11... | collective-permute-start | bytes 491528 | tf_op jit(solution)/shard_map/ppermute | solution.py:213
  102.0 13.5 %collective-permute-start.1 = (bf16[128,640]{1,0:T(8,128)(2,1)S(1)}, bf16[128,640]{1,0:T(8,128)(2,1)S(1)}, u32[]{:S(2)}, u32[]{:S(2)}) collective-permute-start(bf16[128,640]{1,0:T(8,128)(2,1)S(1)} %get-tuple-element.24.refs_0_), channel_id=1, source_target_pairs={{0,2},{1,3},{2,4},{3,5},{4,6},{5,7},{8,10},{9,11},{10,12},{11,13},... | collective-permute-start | bytes 491528 | tf_op jit(solution)/shard_map/ppermute | solution.py:213
  105.5 10.1 %collective-permute-start.2 = (bf16[128,640]{1,0:T(8,128)(2,1)S(1)}, bf16[128,640]{1,0:T(8,128)(2,1)S(1)}, u32[]{:S(2)}, u32[]{:S(2)}) collective-permute-start(bf16[128,640]{1,0:T(8,128)(2,1)S(1)} %get-tuple-element.24.refs_0_), channel_id=1, source_target_pairs={{0,3},{1,4},{2,5},{3,6},{4,7},{8,11},{9,12},{10,13},{11,14},{12,15... | collective-permute-start | bytes 491528 | tf_op jit(solution)/shard_map/ppermute | solution.py:213
  108.3 10.4 %collective-permute-start.3 = (bf16[128,640]{1,0:T(8,128)(2,1)S(1)}, bf16[128,640]{1,0:T(8,128)(2,1)S(1)}, u32[]{:S(2)}, u32[]{:S(2)}) collective-permute-start(bf16[128,640]{1,0:T(8,128)(2,1)S(1)} %get-tuple-element.24.refs_0_), channel_id=1, source_target_pairs={{0,4},{1,5},{2,6},{3,7},{8,12},{9,13},{10,14},{11,15},{16,20},{17,... | collective-permute-start | bytes 491528 | tf_op jit(solution)/shard_map/ppermute | solution.py:213
  111.2 61.1 %all-to-all-start.1 = ((bf16[8,64,640]{2,1,0:T(8,128)(2,1)}), bf16[8,64,640]{2,1,0:T(8,128)(2,1)}, u32[]{:S(2)}, u32[]{:S(2)}) async-start(bf16[8,64,640]{2,1,0:T(8,128)(2,1)} %copy.84), calls=%async_computation.1 | async-start | bytes 1310720 | tf_op jit(solution)/shard_map/all_to_all | solution.py:222
  115.5 203.7 %all-gather.11.cloned.1.call-start = ((), (), s32[]{:S(2)}) async-start(), calls=%async_computation.10 | async-start | bytes 4718592 | tf_op jit(solution)/shard_map/all_gather | solution.py:376
  172.4 47.6 %all-to-all-start = ((bf16[8,64,1280]{2,1,0:T(8,128)(2,1)}), bf16[8,64,1280]{2,1,0:T(8,128)(2,1)}, u32[]{:S(2)}, u32[]{:S(2)}) async-start(bf16[8,64,1280]{2,1,0:T(8,128)(2,1)} %copy.79), calls=%async_computation | async-start | bytes 2621440 | tf_op jit(solution)/shard_map/all_to_all | solution.py:222
  176.9 46.0 %collective-permute-start.8 = (bf16[1,2,1,256,640]{4,3,1,2,0:T(8,128)(2,1)}, bf16[1,2,1,256,640]{4,3,1,2,0:T(8,128)(2,1)}, u32[]{:S(2)}, u32[]{:S(2)}) collective-permute-start(bf16[1,2,1,256,640]{4,3,1,2,0:T(8,128)(2,1)} %bitcast.11), channel_id=1, source_target_pairs={{0,4},{4,0},{1,5},{5,1},{2,6},{6,2},{3,7},{7,3},{8,12},{12,8},{9,1... | collective-permute-start | bytes 1966088 | tf_op jit(solution)/shard_map/ppermute | solution.py:208
  179.2 44.4 %collective-permute-start.7 = (bf16[1,2,1,256,640]{4,3,1,2,0:T(8,128)(2,1)}, bf16[1,2,1,256,640]{4,3,1,2,0:T(8,128)(2,1)}, u32[]{:S(2)}, u32[]{:S(2)}) collective-permute-start(bf16[1,2,1,256,640]{4,3,1,2,0:T(8,128)(2,1)} %bitcast.11), channel_id=1, source_target_pairs={{0,16},{16,0},{1,17},{17,1},{2,18},{18,2},{3,19},{19,3},{4,20},{20... | collective-permute-start | bytes 1966088 | tf_op jit(solution)/shard_map/ppermute | solution.py:208
  220.0 59.5 %collective-permute-start.5 = (bf16[1,2,1,256,1280]{4,3,1,2,0:T(8,128)(2,1)}, bf16[1,2,1,256,1280]{4,3,1,2,0:T(8,128)(2,1)}, u32[]{:S(2)}, u32[]{:S(2)}) collective-permute-start(bf16[1,2,1,256,1280]{4,3,1,2,0:T(8,128)(2,1)} %bitcast.4), channel_id=1, source_target_pairs={{0,4},{4,0},{1,5},{5,1},{2,6},{6,2},{3,7},{7,3},{8,12},{12,8},{9,1... | collective-permute-start | bytes 3932168 | tf_op jit(solution)/shard_map/ppermute | solution.py:208
  220.0 61.1 %collective-permute-start.4 = (bf16[1,2,1,256,1280]{4,3,1,2,0:T(8,128)(2,1)}, bf16[1,2,1,256,1280]{4,3,1,2,0:T(8,128)(2,1)}, u32[]{:S(2)}, u32[]{:S(2)}) collective-permute-start(bf16[1,2,1,256,1280]{4,3,1,2,0:T(8,128)(2,1)} %bitcast.4), channel_id=1, source_target_pairs={{0,16},{16,0},{1,17},{17,1},{2,18},{18,2},{3,19},{19,3},{4,20},{20... | collective-permute-start | bytes 3932168 | tf_op jit(solution)/shard_map/ppermute | solution.py:208
  222.9 58.1 %collective-permute-start.9 = (bf16[1,2,1,256,640]{4,3,1,2,0:T(8,128)(2,1)}, bf16[1,2,1,256,640]{4,3,1,2,0:T(8,128)(2,1)S(1)}, u32[]{:S(2)}, u32[]{:S(2)}) collective-permute-start(bf16[1,2,1,256,640]{4,3,1,2,0:T(8,128)(2,1)} %collective-permute-done.8), channel_id=1, source_target_pairs={{0,16},{16,0},{1,17},{17,1},{2,18},{18,2},{3,19},{19,3},{4,20},{20... | collective-permute-start | bytes 1966088 | tf_op jit(solution)/shard_map/ppermute | solution.py:208
  279.5 30.9 %collective-permute-start.6 = (bf16[1,2,1,256,1280]{4,3,1,2,0:T(8,128)(2,1)}, bf16[1,2,1,256,1280]{4,3,1,2,0:T(8,128)(2,1)S(1)}, u32[]{:S(2)}, u32[]{:S(2)}) collective-permute-start(bf16[1,2,1,256,1280]{4,3,1,2,0:T(8,128)(2,1)} %collective-permute-done.5), channel_id=1, source_target_pairs={{0,16},{16,0},{1,17},{17,1},{2,18},{18,2},{3,19},{19,3},{4,20},{20... | collective-permute-start | bytes 3932168 | tf_op jit(solution)/shard_map/ppermute | solution.py:208
  344.8 55.5 %collective-permute-start.11 = (bf16[512,2048]{1,0:T(8,128)(2,1)}, bf16[512,2048]{1,0:T(8,128)(2,1)}, u32[]{:S(2)}, u32[]{:S(2)}) collective-permute-start(bf16[512,2048]{1,0:T(8,128)(2,1)} %dynamic-slice_bitcast_fusion.1), channel_id=1, source_target_pairs={{0,8},{8,0},{1,9},{9,1},{2,10},{10,2},{3,11},{11,3},{4,12},{12,4},... | collective-permute-start | bytes 6291464 | tf_op jit(solution)/shard_map/ppermute | solution.py:208
  348.7 55.3 %all-to-all-start.4 = ((bf16[8,128,256]{1,2,0:T(8,128)(2,1)}), bf16[8,128,256]{1,2,0:T(8,128)(2,1)}, u32[]{:S(2)}, u32[]{:S(2)}) async-start(bf16[8,128,256]{1,2,0:T(8,128)(2,1)} %bitcast.196), calls=%async_computation.4 | async-start | bytes 1048576 | tf_op jit(solution)/shard_map/all_to_all | solution.py:292
  352.8 264.2 %all-gather.17.cloned.1.call-start = ((), (), s32[]{:S(2)}) async-start(), calls=%async_computation.13 | async-start | bytes 2949120 | tf_op jit(solution)/shard_map/all_gather | solution.py:427
  383.3 31.4 %collective-permute-start.22 = (bf16[2,2,256,640]{3,2,0,1:T(8,128)(2,1)}, bf16[2,2,256,640]{3,2,0,1:T(8,128)(2,1)}, u32[]{:S(2)}, u32[]{:S(2)}) collective-permute-start(bf16[2,2,256,640]{3,2,0,1:T(8,128)(2,1)} %bitcast.202), channel_id=1, source_target_pairs={{0,16},{16,0},{1,17},{17,1},{2,18},{18,2},{3,19},{19,3},{4,20},{20... | collective-permute-start | bytes 3932168 | tf_op jit(solution)/shard_map/ppermute | solution.py:208
  400.1 46.8 %collective-permute-start.10 = (bf16[512,2048]{1,0:T(8,128)(2,1)}, bf16[512,2048]{1,0:T(8,128)(2,1)}, u32[]{:S(2)}, u32[]{:S(2)}) collective-permute-start(bf16[512,2048]{1,0:T(8,128)(2,1)} %dynamic-slice_bitcast_fusion.2), channel_id=1, source_target_pairs={{0,8},{8,0},{1,9},{9,1},{2,10},{10,2},{3,11},{11,3},{4,12},{12,4},... | collective-permute-start | bytes 6291464 | tf_op jit(solution)/shard_map/ppermute | solution.py:208
  404.0 46.7 %all-to-all-start.3 = ((bf16[4,128,2048]{2,1,0:T(8,128)(2,1)}), bf16[4,128,2048]{2,1,0:T(8,128)(2,1)}, u32[]{:S(2)}, u32[]{:S(2)}) async-start(bf16[4,128,2048]{2,1,0:T(8,128)(2,1)} %bitcast.182), calls=%async_computation.3 | async-start | bytes 4194304 | tf_op jit(solution)/shard_map/all_to_all | solution.py:282
  416.8 29.1 %collective-permute-start.23 = (bf16[2,256,640]{2,1,0:T(8,128)(2,1)S(1)}, bf16[2,256,640]{2,1,0:T(8,128)(2,1)S(1)}, u32[]{:S(2)}, u32[]{:S(2)}) collective-permute-start(bf16[2,256,640]{2,1,0:T(8,128)(2,1)S(1)} %fusion.26), channel_id=1, source_target_pairs={{0,4},{4,0},{1,5},{5,1},{2,6},{6,2},{3,7},{7,3},{8,12},{12,8},{9,1... | collective-permute-start | bytes 1966088 | tf_op jit(solution)/shard_map/ppermute | solution.py:208
  424.2 22.7 %copy-start.13 = (bf16[1024,2048]{1,0:T(8,128)(2,1)S(1)}, bf16[1024,2048]{1,0:T(8,128)(2,1)}, u32[]{:S(2)}) copy-start(bf16[1024,2048]{1,0:T(8,128)(2,1)} %convolution_convert_fusion.2) | copy-start | bytes 12582916
  428.1 89.7 %collective-permute-start.20 = (bf16[2,2,256,1280]{3,2,1,0:T(8,128)(2,1)}, bf16[2,2,256,1280]{3,2,1,0:T(8,128)(2,1)}, u32[]{:S(2)}, u32[]{:S(2)}) collective-permute-start(bf16[2,2,256,1280]{3,2,1,0:T(8,128)(2,1)} %dynamic-slice_bitcast_fusion), channel_id=1, source_target_pairs={{0,16},{16,0},{1,17},{17,1},{2,18},{18,2},{3,19},{19,3},{4,20},{20... | collective-permute-start | bytes 7864328 | tf_op jit(solution)/shard_map/ppermute | solution.py:208
  450.6 15.8 %all-to-all-start.7 = ((bf16[8,64,640]{2,1,0:T(8,128)(2,1)}), bf16[8,64,640]{2,1,0:T(8,128)(2,1)}, u32[]{:S(2)}, u32[]{:S(2)}) async-start(bf16[8,64,640]{2,1,0:T(8,128)(2,1)} %bitcast.195), calls=%async_computation.7 | async-start | bytes 1310720 | tf_op jit(solution)/shard_map/all_to_all | solution.py:258
  466.5 61.4 %all-to-all-start.2 = ((bf16[4,128,2048]{2,1,0:T(8,128)(2,1)}), bf16[4,128,2048]{2,1,0:T(8,128)(2,1)}, u32[]{:S(2)}, u32[]{:S(2)}) async-start(bf16[4,128,2048]{2,1,0:T(8,128)(2,1)} %bitcast.181), calls=%async_computation.2 | async-start | bytes 4194304 | tf_op jit(solution)/shard_map/all_to_all | solution.py:282
  471.0 156.0 %all-gather.15.cloned.1.call-start = ((), (), s32[]{:S(2)}) async-start(), calls=%async_computation.12 | async-start | bytes 4423680 | tf_op jit(solution)/shard_map/all_gather | solution.py:429
  480.8 19.2 %collective-permute-start.12 = (bf16[128,640]{1,0:T(8,128)(2,1)S(1)}, bf16[128,640]{1,0:T(8,128)(2,1)S(1)}, u32[]{:S(2)}, u32[]{:S(2)}) collective-permute-start(bf16[128,640]{1,0:T(8,128)(2,1)S(1)} %get-tuple-element.29), channel_id=1, source_target_pairs={{1,0},{2,1},{3,2},{4,3},{5,4},{6,5},{7,6},{9,8},{10,9},{11,10},{12... | collective-permute-start | bytes 491528 | tf_op jit(solution)/shard_map/ppermute | solution.py:213
  482.1 28.5 %collective-permute-start.13 = (bf16[128,640]{1,0:T(8,128)(2,1)S(1)}, bf16[128,640]{1,0:T(8,128)(2,1)S(1)}, u32[]{:S(2)}, u32[]{:S(2)}) collective-permute-start(bf16[128,640]{1,0:T(8,128)(2,1)S(1)} %get-tuple-element.30), channel_id=1, source_target_pairs={{2,0},{3,1},{4,2},{5,3},{6,4},{7,5},{10,8},{11,9},{12,10},{13,11},... | collective-permute-start | bytes 491528 | tf_op jit(solution)/shard_map/ppermute | solution.py:213
  483.4 27.2 %collective-permute-start.14 = (bf16[128,640]{1,0:T(8,128)(2,1)S(1)}, bf16[128,640]{1,0:T(8,128)(2,1)S(1)}, u32[]{:S(2)}, u32[]{:S(2)}) collective-permute-start(bf16[128,640]{1,0:T(8,128)(2,1)S(1)} %get-tuple-element.31), channel_id=1, source_target_pairs={{3,0},{4,1},{5,2},{6,3},{7,4},{11,8},{12,9},{13,10},{14,11},{15,12... | collective-permute-start | bytes 491528 | tf_op jit(solution)/shard_map/ppermute | solution.py:213
  484.7 25.9 %collective-permute-start.15 = (bf16[128,640]{1,0:T(8,128)(2,1)S(1)}, bf16[128,640]{1,0:T(8,128)(2,1)S(1)}, u32[]{:S(2)}, u32[]{:S(2)}) collective-permute-start(bf16[128,640]{1,0:T(8,128)(2,1)S(1)} %get-tuple-element.32), channel_id=1, source_target_pairs={{4,0},{5,1},{6,2},{7,3},{12,8},{13,9},{14,10},{15,11},{20,16},{21,... | collective-permute-start | bytes 491528 | tf_op jit(solution)/shard_map/ppermute | solution.py:213
  524.5 59.5 %collective-permute-start.21 = (bf16[2,256,1280]{2,1,0:T(8,128)(2,1)}, bf16[2,256,1280]{2,1,0:T(8,128)(2,1)}, u32[]{:S(2)}, u32[]{:S(2)}) collective-permute-start(bf16[2,256,1280]{2,1,0:T(8,128)(2,1)} %fusion.16), channel_id=1, source_target_pairs={{0,4},{4,0},{1,5},{5,1},{2,6},{6,2},{3,7},{7,3},{8,12},{12,8},{9,1... | collective-permute-start | bytes 3932168 | tf_op jit(solution)/shard_map/ppermute | solution.py:208
  527.9 59.7 %all-to-all-start.5 = ((bf16[8,128,256]{1,2,0:T(8,128)(2,1)}), bf16[8,128,256]{1,2,0:T(8,128)(2,1)S(1)}, u32[]{:S(2)}, u32[]{:S(2)}) async-start(bf16[8,128,256]{1,2,0:T(8,128)(2,1)} %bitcast.39), calls=%async_computation.5 | async-start | bytes 1048576 | tf_op jit(solution)/shard_map/all_to_all | solution.py:292
  538.8 48.7 %collective-permute-start.24 = (f32[33,128]{1,0:T(8,128)S(1)}, f32[33,128]{1,0:T(8,128)S(1)}, u32[]{:S(2)}, u32[]{:S(2)}) collective-permute-start(f32[33,128]{1,0:T(8,128)S(1)} %maximum_bitcast_fusion.1), channel_id=1, source_target_pairs={{0,8},{8,0},{1,9},{9,1},{2,10},{10,2},{3,11},{11,3},{4,12},{12,4},... | collective-permute-start | bytes 50696 | tf_op jit(solution)/shard_map/ppermute | solution.py:208
  587.5 7.1 %collective-permute-start.25 = (f32[33,128]{1,0:T(8,128)S(1)}, f32[33,128]{1,0:T(8,128)S(1)}, u32[]{:S(2)}, u32[]{:S(2)}) collective-permute-start(f32[33,128]{1,0:T(8,128)S(1)} %fusion.35), channel_id=1, source_target_pairs={{0,1},{1,0},{2,3},{3,2},{4,5},{5,4},{6,7},{7,6},{8,9},{9,8},{10,11... | collective-permute-start | bytes 50696 | tf_op jit(solution)/shard_map/ppermute | solution.py:208
  587.6 35.5 %all-to-all-start.6 = ((bf16[8,64,1280]{2,1,0:T(8,128)(2,1)}), bf16[8,64,1280]{2,1,0:T(8,128)(2,1)}, u32[]{:S(2)}, u32[]{:S(2)}) async-start(bf16[8,64,1280]{2,1,0:T(8,128)(2,1)} %bitcast.183), calls=%async_computation.6 | async-start | bytes 2621440 | tf_op jit(solution)/shard_map/all_to_all | solution.py:258
  594.6 5.0 collective-permute-start.26
  599.6 10.3 %collective-permute-start.27 = (f32[33,128]{1,0:T(8,128)S(1)}, f32[33,128]{1,0:T(8,128)S(1)}, u32[]{:S(2)}, u32[]{:S(2)}) collective-permute-start(f32[33,128]{1,0:T(8,128)S(1)} %add.162), channel_id=1, source_target_pairs={{0,2},{2,0},{1,3},{3,1},{4,6},{6,4},{5,7},{7,5},{8,10},{10,8},{9,1... | collective-permute-start | bytes 50696 | tf_op jit(solution)/shard_map/ppermute | solution.py:208
  609.8 4.7 collective-permute-start.28
  620.4 10.3 %collective-permute-start.18 = (bf16[1,2,64,1280]{3,2,1,0:T(8,128)(2,1)}, bf16[1,2,64,1280]{3,2,1,0:T(8,128)(2,1)}, u32[]{:S(2)}, u32[]{:S(2)}) collective-permute-start(bf16[1,2,64,1280]{3,2,1,0:T(8,128)(2,1)} %dynamic-slice_bitcast_fusion.4), channel_id=1, source_target_pairs={{0,16},{16,0},{1,17},{17,1},{2,18},{18,2},{3,19},{19,3},{4,20},{20... | collective-permute-start | bytes 983048 | tf_op jit(solution)/shard_map/ppermute | solution.py:208
  630.6 11.7 %collective-permute-start.16 = (bf16[1,2,64,1920]{3,2,1,0:T(8,128)(2,1)S(1)}, bf16[1,2,64,1920]{3,2,1,0:T(8,128)(2,1)S(1)}, u32[]{:S(2)}, u32[]{:S(2)}) collective-permute-start(bf16[1,2,64,1920]{3,2,1,0:T(8,128)(2,1)S(1)} %dynamic-slice_bitcast_fusion.3), channel_id=1, source_target_pairs={{0,16},{16,0},{1,17},{17,1},{2,18},{18,2},{3,19},{19,3},{4,20},{20... | collective-permute-start | bytes 1474568 | tf_op jit(solution)/shard_map/ppermute | solution.py:208
  631.8 11.2 %collective-permute-start.19 = (bf16[1,64,1280]{2,1,0:T(8,128)(2,1)S(1)}, bf16[1,64,1280]{2,1,0:T(8,128)(2,1)S(1)}, u32[]{:S(2)}, u32[]{:S(2)}) collective-permute-start(bf16[1,64,1280]{2,1,0:T(8,128)(2,1)S(1)} %fusion.30), channel_id=1, source_target_pairs={{0,4},{4,0},{1,5},{5,1},{2,6},{6,2},{3,7},{7,3},{8,12},{12,8},{9,1... | collective-permute-start | bytes 491528 | tf_op jit(solution)/shard_map/ppermute | solution.py:208
  642.5 11.7 %collective-permute-start.17 = (bf16[1,64,1920]{2,1,0:T(8,128)(2,1)S(1)}, bf16[1,64,1920]{2,1,0:T(8,128)(2,1)S(1)}, u32[]{:S(2)}, u32[]{:S(2)}) collective-permute-start(bf16[1,64,1920]{2,1,0:T(8,128)(2,1)S(1)} %fusion.29), channel_id=1, source_target_pairs={{0,4},{4,0},{1,5},{5,1},{2,6},{6,2},{3,7},{7,3},{8,12},{12,8},{9,1... | collective-permute-start | bytes 737288 | tf_op jit(solution)/shard_map/ppermute | solution.py:208
  (22 other events, 168.3 us)
Sparse Core Ops, SparseCore 0:
  11.0 78.1 all-gather.6
  92.0 70.9 all-gather.8
  164.6 52.6 all-gather.12
  219.3 43.8 all-gather.10
  355.5 22.4 all-gather.16
  517.9 49.1 all-gather.14

commit v2 on v1

--- a/solution.py
+++ b/solution.py
@@ -56,11 +56,21 @@
     return jnp.concatenate([values[:, half:], -values[:, :half]], axis=1)
 
 
+def block_head(ref, head):
+    block, start = divmod(head * HEAD_DIM, ref.shape[2])
+    return ref[block, :, start : start + HEAD_DIM].astype(f32)
+
+
+def block_store(ref, head, value):
+    block, start = divmod(head * HEAD_DIM, ref.shape[2])
+    ref[block, :, start : start + HEAD_DIM] = value
+
+
 def heads_forward_kernel(qkv_ref, cos_ref, sin_ref, gq_ref, gk_ref, q_ref, kv_ref):
     cosine, sine = cos_ref[...], sin_ref[...]
     for head in range(QUERY_HEADS + KEY_VALUE_HEADS):
         columns = slice(head * HEAD_DIM, (head + 1) * HEAD_DIM)
-        normed, _ = head_norm(qkv_ref[:, columns])
+        normed, _ = head_norm(block_head(qkv_ref, head))
         if head < QUERY_HEADS:
             scaled = normed * gq_ref[...]
             turned = (scaled * cosine + turn(scaled) * sine) * (HEAD_DIM**-0.5)
@@ -70,7 +80,10 @@
             turned = scaled * cosine + turn(scaled) * sine
             place = slice((head - QUERY_HEADS) * HEAD_DIM, (head - QUERY_HEADS + 1) * HEAD_DIM)
             kv_ref[:, place] = turned.astype(bf16)
-    kv_ref[:, KEY_COLUMNS:] = qkv_ref[:, QUERY_COLUMNS + KEY_COLUMNS :].astype(bf16)
+    for head in range(KEY_VALUE_HEADS):
+        place = slice(KEY_COLUMNS + head * HEAD_DIM, KEY_COLUMNS + (head + 1) * HEAD_DIM)
+        value = block_head(qkv_ref, QUERY_HEADS + KEY_VALUE_HEADS + head)
+        kv_ref[:, place] = value.astype(bf16)
 
 
 def heads_backward_kernel(
@@ -85,7 +98,7 @@
     totals = [jnp.zeros((1, HEAD_DIM), f32), jnp.zeros((1, HEAD_DIM), f32)]
     for head in range(QUERY_HEADS + KEY_VALUE_HEADS):
         columns = slice(head * HEAD_DIM, (head + 1) * HEAD_DIM)
-        normed, scale = head_norm(qkv_ref[:, columns])
+        normed, scale = head_norm(block_head(qkv_ref, head))
         is_key = int(head >= QUERY_HEADS)
         if is_key:
             place = slice((head - QUERY_HEADS) * HEAD_DIM, (head - QUERY_HEADS + 1) * HEAD_DIM)
@@ -98,8 +111,13 @@
         totals[is_key] = totals[is_key] + jnp.sum(grad * normed, axis=0, keepdims=True)
         weighted = grad * gain
         inner = jnp.mean(weighted * normed, axis=-1, keepdims=True)
-        grad_ref[:, columns] = (scale * (weighted - normed * inner)).astype(bf16)
-    grad_ref[:, QUERY_COLUMNS + KEY_COLUMNS :] = kv_grad[:, KEY_COLUMNS:].astype(bf16)
+        block_store(grad_ref, head, (scale * (weighted - normed * inner)).astype(bf16))
+    for head in range(KEY_VALUE_HEADS):
+        place = slice(KEY_COLUMNS + head * HEAD_DIM, KEY_COLUMNS + (head + 1) * HEAD_DIM)
+        block_store(grad_ref, QUERY_HEADS + KEY_VALUE_HEADS + head, kv_grad[:, place].astype(bf16))
+    count, tokens, width = grad_ref.shape
+    for head in range(QUERY_HEADS + 2 * KEY_VALUE_HEADS, count * width // HEAD_DIM):
+        block_store(grad_ref, head, jnp.zeros((tokens, HEAD_DIM), bf16))
     gain_ref[...] = jnp.concatenate(totals, axis=1)
 
 
@@ -193,6 +211,111 @@
             ].T
 
 
+def ffn_dz_kernel(count, offsets, grads_ref, *refs):
+    blocks, out_ref = refs[:-1], refs[-1]
+    total = jnp.zeros(out_ref.shape, f32)
+    for i, column, piece in pieces_of(blocks, offsets, count):
+        total = total + dot_nn(grads_ref[:, column], piece[...])
+    out_ref[...] = total
+
+
+def ffn_mid_kernel(count, offsets, mid_ref, dz_ref, *refs):
+    blocks = len(refs) // 2 - 2
+    gates, ups = refs[:blocks], refs[blocks : 2 * blocks]
+    hidden_ref, gate_grad_ref, up_grad_ref, out_ref = refs[2 * blocks :]
+    gate = jnp.zeros(dz_ref.shape, f32)
+    up = jnp.zeros(dz_ref.shape, f32)
+    for i, column, piece in pieces_of(gates, offsets, count):
+        gate = gate + dot_nn(mid_ref[:, column], piece[...])
+    for i, column, piece in pieces_of(ups, offsets, count):
+        up = up + dot_nn(mid_ref[:, column], piece[...])
+    sigmoid = 1.0 / (1.0 + jnp.exp(-gate))
+    activated = gate * sigmoid
+    hidden_ref[...] = (activated * up).astype(bf16)
+    hidden_grad = dz_ref[...]
+    slope = sigmoid * (1.0 + gate * (1.0 - sigmoid))
+    gate_grad = (hidden_grad * up * slope).astype(bf16)
+    up_grad = (hidden_grad * activated).astype(bf16)
+    gate_grad_ref[...] = gate_grad
+    up_grad_ref[...] = up_grad
+    up_pieces = list(pieces_of(ups, offsets, count))
+    for i, column, piece in pieces_of(gates, offsets, count):
+        out_ref[:, column] = (
+            dot_nt(gate_grad, piece[...]) + dot_nt(up_grad, up_pieces[i][2][...])
+        ).astype(bf16)
+
+
+def ffn_out_kernel(count, offsets, hidden_ref, *refs):
+    blocks, out_ref = refs[:-1], refs[-1]
+    for i, column, piece in pieces_of(blocks, offsets, count):
+        out_ref[:, column] = dot_nt(hidden_ref[...], piece[...]).astype(bf16)
+
+
+def weight_grad_kernel(rows_ref, columns_ref, out_ref):
+    out_ref[...] = dot_tn(rows_ref[...], columns_ref[...]).astype(bf16)
+
+
+def weight_grad(row_side, column_side, name):
+    tokens, model = row_side.shape
+    width = column_side.shape[1]
+    ny, nc, nzh = lax.axis_size("y"), lax.axis_size("core"), lax.axis_size("zh")
+    rows = model // (ny * nc * nzh)
+
+    def put(r):
+        y, rest = r // (nc * nzh), r % (nc * nzh)
+        return ((y * nzh + rest % nzh) * nc + rest // nzh, 0)
+
+    return pl.pallas_call(
+        weight_grad_kernel,
+        out_shape=jax.ShapeDtypeStruct((model, width), bf16),
+        grid=(model // rows,),
+        in_specs=[
+            pl.BlockSpec((tokens, rows), lambda r: (0, r)),
+            pl.BlockSpec((tokens, width), lambda r: (0, 0)),
+        ],
+        out_specs=pl.BlockSpec((rows, width), put),
+        name=name,
+        compiler_params=pltpu.CompilerParams(vmem_limit_bytes=32 << 20),
+        cost_estimate=pl.CostEstimate(
+            flops=2 * tokens * model * width,
+            transcendentals=0,
+            bytes_accessed=2 * (tokens * model + tokens * width + model * width),
+        ),
+    )(row_side, column_side)
+
+
+def pieces_of(blocks, offsets, count):
+    i = 0
+    for block in blocks:
+        rows = block.shape[0] // count
+        for c in range(count):
+            column = pl.ds(pl.multiple_of(offsets[i], 128), rows)
+            yield i, column, block.at[c * rows : (c + 1) * rows, :]
+            i += 1
+
+
+def by_tokens(kernel, offsets, token_arrays, blocks, outs, name, flops):
+    tokens = token_arrays[0].shape[0]
+    chunk = min(256, tokens)
+    blocks = [block.reshape(-1, block.shape[-1]) for block in blocks]
+    moved = 2 * sum(b.size for b in blocks) + 2 * sum(t.size for t in token_arrays)
+    row = lambda width: pl.BlockSpec((chunk, width), lambda t, o: (t, 0))
+    return pl.pallas_call(
+        functools.partial(kernel, lax.axis_size("core")),
+        out_shape=tuple(jax.ShapeDtypeStruct((tokens, width), kind) for width, kind in outs),
+        grid_spec=pltpu.PrefetchScalarGridSpec(
+            num_scalar_prefetch=1,
+            grid=(tokens // chunk,),
+            in_specs=[row(t.shape[1]) for t in token_arrays]
+            + [pl.BlockSpec(b.shape, lambda t, o: (0, 0)) for b in blocks],
+            out_specs=tuple(row(width) for width, _ in outs),
+        ),
+        name=name,
+        compiler_params=pltpu.CompilerParams(vmem_limit_bytes=48 << 20),
+        cost_estimate=pl.CostEstimate(flops=flops, transcendentals=0, bytes_accessed=moved),
+    )(offsets, *token_arrays, *blocks)
+
+
 def whole(kernel, out_shapes, name, flops, moved):
     return pl.pallas_call(
         kernel,
@@ -213,74 +336,93 @@
     return lax.ppermute(value, SEQ, [(i, i + step) for i in range(n) if 0 <= i + step < n])
 
 
-def spread_columns(pieces):
-    team = lax.axis_size(TEAM)
+def tie(*values):
+    return lax.optimization_barrier(values)
+
+
+def team_columns(pieces):
+    team, nc = lax.axis_size(TEAM), lax.axis_size("core")
     rows = pieces[0].shape[0]
-    ny, nzh = lax.axis_size("y"), lax.axis_size("zh")
     blocks = jnp.concatenate([p.reshape(rows, team, -1) for p in pieces], axis=2)
-    blocks = blocks.transpose(1, 0, 2)
-    blocks = lax.all_to_all(blocks, TEAM, 0, 0, tiled=True)
-    width = blocks.shape[2]
-    nc = lax.axis_size("core")
-    block = blocks.reshape(1, nc, 1, -1, width)
-    full = jnp.zeros((ny, nc, nzh, block.shape[3], width), bf16)
+    blocks = lax.all_to_all(blocks.transpose(1, 0, 2), TEAM, 0, 0, tiled=True)
+    return blocks.reshape(1, nc, 1, -1, blocks.shape[2])
+
+
+def exchange(block, axis):
+    return [block] + [swap(block, axis, k) for k in range(1, lax.axis_size(axis))]
+
+
+def place(pieces):
     y, zh = lax.axis_index("y"), lax.axis_index("zh")
-    far = [block] + [swap(block, "zh", b) for b in range(1, nzh)]
-    for b in range(nzh):
-        for a in range(ny):
-            piece = far[b] if a == 0 else swap(far[b], "y", a)
+    _, nc, _, rest, width = pieces[0][0].shape
+    full = jnp.zeros((lax.axis_size("y"), nc, lax.axis_size("zh"), rest, width), bf16)
+    for b, row in enumerate(pieces):
+        for a, piece in enumerate(row):
             full = lax.dynamic_update_slice(full, piece, (y ^ a, 0, zh ^ b, 0, 0))
     return full.reshape(-1, width)
 
 
-def reduce_rows(partial, shape):
-    y, zh = lax.axis_index("y"), lax.axis_index("zh")
-    ny, nzh = lax.axis_size("y"), lax.axis_size("zh")
-    partial = partial.reshape(shape)
+def reduce_y(partial):
+    y = lax.axis_index("y")
     total = lax.dynamic_index_in_dim(partial, y, 0, keepdims=False).astype(f32)
-    for a in range(1, ny):
+    for a in range(1, lax.axis_size("y")):
         total = total + swap(
             lax.dynamic_index_in_dim(partial, y ^ a, 0, keepdims=False), "y", a
         ).astype(f32)
+    return total
+
+
+def reduce_zh(total):
+    zh = lax.axis_index("zh")
     out = lax.dynamic_index_in_dim(total, zh, 1, keepdims=False)
-    for b in range(1, nzh):
+    for b in range(1, lax.axis_size("zh")):
         out = out + swap(
             lax.dynamic_index_in_dim(total, zh ^ b, 1, keepdims=False).astype(bf16), "zh", b
         ).astype(f32)
     return out
 
 
-def collect_columns(partial, count):
-    ny, nzh, nc = lax.axis_size("y"), lax.axis_size("zh"), lax.axis_size("core")
+def return_columns(totals):
     team = lax.axis_size(TEAM)
-    total = reduce_rows(partial, (ny, nc, nzh, -1, partial.shape[1]))
-    blocks = total.astype(bf16).reshape(team, -1, partial.shape[1])
-    blocks = lax.all_to_all(blocks, TEAM, 0, 0, tiled=True)
-    rows = blocks.shape[1]
-    width = partial.shape[1] // count
-    return [
-        blocks[:, :, i * width : (i + 1) * width]
-        .transpose(1, 0, 2)
-        .reshape(rows, team * width)
-        .astype(f32)
-        for i in range(count)
-    ]
-
-
-def team_sum(partial):
+    parts = [total.astype(bf16).reshape(team, -1, total.shape[-1]) for total in totals]
+    blocks = lax.all_to_all(jnp.concatenate(parts, axis=2), TEAM, 0, 0, tiled=True)
+    grads, start = [], 0
+    for part in parts:
+        width = part.shape[2]
+        grad = blocks[:, :, start : start + width].transpose(1, 0, 2)
+        grads.append(grad.reshape(grad.shape[0], -1).astype(f32))
+        start += width
+    return grads
+
+
+def team_core(partial):
     nc = lax.axis_size("core")
-    chips = lax.axis_size(CHIPS)
     core = lax.axis_index("core")
-    width = partial.shape[1]
-    halves = partial.reshape(nc, -1, width)
+    halves = partial.reshape(nc, -1, partial.shape[1])
     total = lax.dynamic_index_in_dim(halves, core, 0, keepdims=False).astype(f32)
     for k in range(1, nc):
         total = total + swap(
             lax.dynamic_index_in_dim(halves, core ^ k, 0, keepdims=False), "core", k
         ).astype(f32)
-    blocks = total.astype(bf16).reshape(chips, -1, width)
-    blocks = lax.all_to_all(blocks, CHIPS, 0, 0, tiled=True)
-    return jnp.sum(blocks.astype(f32), axis=0)
+    return total.astype(bf16)
+
+
+def team_chips(total):
+    chips, chip = lax.axis_size(CHIPS), lax.axis_index(CHIPS)
+    blocks = total.reshape(chips, -1, total.shape[1])
+    block = lambda i: lax.dynamic_index_in_dim(blocks, i, 0, keepdims=False)
+    far = [
+        lax.ppermute(block(chip ^ k), CHIPS, [(i, i ^ k) for i in range(chips)])
+        for k in range(1, chips)
+    ]
+    out = block(chip).astype(f32)
+    for piece in far:
+        out = out + piece.astype(f32)
+    return out
+
+
+def team_sum(partial):
+    return team_chips(team_core(partial))
 
 
 def row_team(value):
@@ -292,14 +434,16 @@
     return lax.all_to_all(split, TEAM, 0, 0, tiled=True).reshape(team * tokens, -1)
 
 
-def row_grads(row_side, column_side):
-    ny, nzh = lax.axis_size("y"), lax.axis_size("zh")
-    partial = dot_tn(row_side, column_side).astype(bf16)
-    return reduce_rows(partial, (ny, 1, nzh, -1, partial.shape[1])).reshape(-1, partial.shape[1])
-
-
-def sum_all(value):
-    for axis in ("core", "x", "y", "zl", "zh"):
+def own_rows(value):
+    ny, nc, nzh = lax.axis_size("y"), lax.axis_size("core"), lax.axis_size("zh")
+    split = value.reshape(value.shape[0], ny, nc, nzh, lax.axis_size(CHIPS), -1)
+    split = lax.dynamic_index_in_dim(split, lax.axis_index("core"), 2, keepdims=False)
+    split = lax.dynamic_index_in_dim(split, lax.axis_index(CHIPS), 3, keepdims=False)
+    return split.reshape(value.shape[0], -1)
+
+
+def sum_over(value, axes):
+    for axis in axes:
         k = 1
         while k < lax.axis_size(axis):
             value = value + swap(value, axis, k)
@@ -331,13 +475,50 @@
     normed_in = inputs * scale_in
     normed_low = (normed_in * g_attn).astype(bf16)
 
-    qkv_full = lax.all_gather(query_key_value_weight, ALL, axis=0, tiled=True)
-    out_full = lax.all_gather(w_out, ALL, axis=0, tiled=True)
-    gate_up = spread_columns([w_gate, w_up])
-    down = spread_columns([w_down])
-    grads_out = lax.all_gather(cotangent, TEAM, axis=0, tiled=True)
-
-    joined = dot_nn(normed_low, qkv_full)
+    team = lax.axis_size(TEAM)
+    joined_columns = query_key_value_weight.shape[1]
+    padded = -(-joined_columns // (128 * team)) * 128 * team
+
+    y, zh = lax.axis_index("y"), lax.axis_index("zh")
+    ny, nc, nzh = lax.axis_size("y"), lax.axis_size("core"), lax.axis_size("zh")
+    width = model // (ny * nc * nzh)
+    offsets = jnp.stack(
+        [
+            (((y ^ a) * nc + c) * nzh + (zh ^ b)) * width
+            for b in range(nzh)
+            for a in range(ny)
+            for c in range(nc)
+        ]
+    ).astype(jnp.int32)
+
+    normed_team = lax.all_gather(normed_low, TEAM, axis=0, tiled=True)
+    qkv_block = team_columns([jnp.pad(query_key_value_weight, ((0, 0), (0, padded - joined_columns)))])
+    qkv_block, w_down, w_out = tie(qkv_block, w_down, w_out)
+    qkv_near, qkv_far = exchange(qkv_block, "y"), exchange(qkv_block, "zh")
+    out_near = exchange(w_out[None, None], "zh")
+    down_block = team_columns([w_down])
+    out_part = [exchange(piece, "y") for piece in out_near]
+    qkv_part = place([qkv_near] + [exchange(piece, "y") for piece in qkv_far[1:]])
+    out_rows = jnp.zeros((ny, nzh) + w_out.shape, bf16)
+    for b, row in enumerate(out_part):
+        for a, piece in enumerate(row):
+            out_rows = lax.dynamic_update_slice(out_rows, piece, (y ^ a, zh ^ b, 0, 0))
+
+    normed_team, qkv_part, out_rows, down_block, w_gate = tie(
+        normed_team, qkv_part, out_rows, down_block, w_gate
+    )
+    out_full = lax.all_gather(out_rows, TEAM, axis=0, tiled=False)
+    out_full = (
+        out_full.reshape((nc, lax.axis_size(CHIPS)) + out_rows.shape)
+        .transpose(2, 0, 3, 1, 4, 5)
+        .reshape(model, -1)
+    )
+    down_far, down_near = exchange(down_block, "zh"), exchange(down_block, "y")
+    joined_team = dot_nn(normed_team, qkv_part).astype(bf16)
+    joined = lax.all_to_all(
+        joined_team.reshape(team, tokens, -1), TEAM, 0, 0, tiled=True
+    )
+    joined, down_near = tie(joined, down_near)
 
     half = HEAD_DIM // 2
     frequency = 10000.0 ** (-jnp.arange(half, dtype=f32) / half)
@@ -357,6 +538,10 @@
     )(joined, cosine, sine, gq, gk)
 
     kv_blocks = [kv_low] + [shifted(kv_low, step) for step in range(1, back + 1)]
+    kv_blocks, down_far, w_gate, cotangent_in = tie(kv_blocks, down_far, w_gate, cotangent)
+    gate_block = team_columns([w_gate])
+    down_blocks = down_near + sum([exchange(piece, "y") for piece in down_far[1:]], [])
+    grads_out = lax.all_gather(cotangent_in, TEAM, axis=0, tiled=True)
     tiled_positions = jnp.tile(positions[None, :], (1, GROUP))
     attended, inverse = whole(
         functools.partial(attend_forward_kernel, back),
@@ -369,28 +554,54 @@
         tokens * 2000 * 10,
     )(tiled_positions, query_low, *kv_blocks)
 
+    attended, out_full, gate_block, w_up = tie(attended, out_full, gate_block, w_up)
+    gate_far, gate_near = exchange(gate_block, "zh"), exchange(gate_block, "y")
+    up_block = team_columns([w_up])
     middle = inputs + dot_nt(attended, out_full)
     scale_mid = row_scale(middle)
     normed_mid = middle * scale_mid
     mid_low = (normed_mid * g_ffn).astype(bf16)
     mid_team = lax.all_gather(mid_low, TEAM, axis=0, tiled=True)
 
-    gate_pre = dot_nn(mid_team, gate_up[:, :ff])
-    up_pre = dot_nn(mid_team, gate_up[:, ff:])
-    sigmoid_gate = jax.nn.sigmoid(gate_pre)
-    activated = gate_pre * sigmoid_gate
-    hidden = (activated * up_pre).astype(bf16)
-    hidden_grad = dot_nn(grads_out, down)
-    slope = sigmoid_gate * (1.0 + gate_pre * (1.0 - sigmoid_gate))
-    gate_grad = (hidden_grad * up_pre * slope).astype(bf16)
-    up_grad = (hidden_grad * activated).astype(bf16)
-    gate_up_grad = jnp.concatenate([gate_grad, up_grad], axis=1)
-    mid_grad = team_sum(dot_nt(gate_up_grad, gate_up).astype(bf16))
-    branch_two = team_sum(dot_nt(hidden, down).astype(bf16))
-    result = (middle + branch_two).astype(bf16)
-
-    w_down_grad = collect_columns(dot_tn(grads_out, hidden).astype(bf16), 1)[0]
-    w_gate_grad, w_up_grad = collect_columns(dot_tn(mid_team, gate_up_grad).astype(bf16), 2)
+    products = 2 * mid_team.shape[0] * model * ff
+    grads_out, down_blocks, gate_far, gate_near, up_block = tie(
+        grads_out, down_blocks, gate_far, gate_near, up_block
+    )
+    up_far, up_near = exchange(up_block, "zh"), exchange(up_block, "y")
+    gate_blocks = gate_near + sum([exchange(piece, "y") for piece in gate_far[1:]], [])
+    (hidden_grad,) = by_tokens(
+        ffn_dz_kernel, offsets, [grads_out], down_blocks, [(ff, f32)], "ffn_dz", products
+    )
+    mid_team, hidden_grad, gate_blocks, up_far, up_near, attended_in = tie(
+        mid_team, hidden_grad, gate_blocks, up_far, up_near, attended
+    )
+    up_blocks = up_near + sum([exchange(piece, "y") for piece in up_far[1:]], [])
+    attended_team = lax.all_gather(attended_in, TEAM, axis=0, tiled=True)
+    hidden, gate_grad, up_grad, mid_part = by_tokens(
+        ffn_mid_kernel,
+        offsets,
+        [mid_team, hidden_grad],
+        gate_blocks + up_blocks,
+        [(ff, bf16), (ff, bf16), (ff, bf16), (model, bf16)],
+        "ffn_mid",
+        4 * products,
+    )
+
+    scatter = lambda part: lax.psum_scatter(part, ("y", "zh"), scatter_dimension=0, tiled=True)
+    mid_part, attended_team, hidden = tie(mid_part, attended_team, hidden)
+    mid_half = team_core(mid_part)
+    down_part = weight_grad(grads_out, hidden, "down_grad")
+    down_sum = scatter(down_part)
+    mid_half, hidden, _ = tie(mid_half, hidden, down_part)
+    mid_grad = team_chips(mid_half)
+    branch_half = team_core(
+        by_tokens(
+            ffn_out_kernel, offsets, [hidden], down_blocks, [(model, bf16)], "ffn_out", products
+        )[0]
+    )
+    mid_grad, branch_half, mid_team, gate_grad, up_grad = tie(
+        mid_grad, branch_half, mid_team, gate_grad, up_grad
+    )
 
     weighted = mid_grad * g_ffn
     ffn_gain = jnp.sum(mid_grad * normed_mid, axis=0)
@@ -399,7 +610,6 @@
     )
     branch_grad = middle_grad.astype(bf16)
     head_grads = dot_nn(branch_grad, out_full).astype(bf16)
-
     results = whole(
         functools.partial(attend_backward_kernel, back),
         (
@@ -412,11 +622,15 @@
         tokens * 2000 * 20,
     )(tiled_positions, query_low, head_grads, inverse, *kv_blocks)
     query_grad, own_grad, far_grads = results[0], results[1], results[2:]
+    far_grads, gate_grad, mid_team_in = tie(far_grads, gate_grad, mid_team)
+    gate_part = weight_grad(mid_team_in, gate_grad, "gate_grad")
     received = [shifted(grad, -(i + 1)) for i, grad in enumerate(far_grads)]
+    received, down_sum, gate_part, up_grad = tie(received, down_sum, gate_part, up_grad)
+    gate_sum = scatter(gate_part)
     joined_grad, head_gains = whole(
         functools.partial(heads_backward_kernel, back),
         (
-            jax.ShapeDtypeStruct((tokens, joined.shape[1]), bf16),
+            jax.ShapeDtypeStruct(joined.shape, bf16),
             jax.ShapeDtypeStruct((1, 2 * HEAD_DIM), f32),
         ),
         "heads_backward",
@@ -424,12 +638,24 @@
         tokens * 1920 * 16,
     )(joined, cosine, sine, gq, gk, query_grad, own_grad, *received)
 
-    attended_team = lax.all_gather(attended, TEAM, axis=0, tiled=True)
-    w_out_grad = row_grads(row_team(branch_grad), attended_team)
-    joined_team = lax.all_gather(joined_grad, TEAM, axis=0, tiled=True)
-    w_qkv_grad = row_grads(row_team(normed_low), joined_team)
-
-    normed_in_grad = dot_nt(joined_grad, qkv_full)
+    joined_grad, up_grad, mid_team = tie(joined_grad, up_grad, mid_team)
+    up_part = weight_grad(mid_team, up_grad, "up_grad")
+    joined_grad = lax.all_to_all(joined_grad, TEAM, 0, 0, tiled=True).reshape(-1, padded // team)
+    joined_grad, up_part, down_sum = tie(joined_grad, up_part, down_sum)
+    up_sum = scatter(up_part)
+    normed_in_grad = team_sum(dot_nt(joined_grad, qkv_part).astype(bf16))
+    normed_in_grad, gate_sum, joined_grad, down_sum, branch_grad, branch_half = tie(
+        normed_in_grad, gate_sum, joined_grad, down_sum, branch_grad, branch_half
+    )
+    qkv_sum = reduce_zh(
+        reduce_y(
+            dot_tn(normed_team, joined_grad).astype(bf16).reshape(ny, nc, nzh, -1, padded // team)
+        )
+    )
+    w_down_grad, w_gate_grad = return_columns([down_sum, gate_sum])
+    out_part = dot_tn(row_team(branch_grad), attended_team).astype(bf16)
+    out_sum = reduce_y(out_part.reshape(ny, 1, nzh, -1, out_part.shape[1]))
+    branch_two = team_chips(branch_half)
     weighted_in = normed_in_grad * g_attn
     attn_gain = jnp.sum(normed_in_grad * normed_in, axis=0)
     input_grad = (
@@ -438,9 +664,18 @@
         * (weighted_in - normed_in * jnp.mean(weighted_in * normed_in, axis=-1, keepdims=True))
     ).astype(bf16)
 
-    gains = sum_all(
-        jnp.concatenate([attn_gain, ffn_gain, head_gains[0]], axis=0).reshape(-1, 128)
-    ).reshape(-1)
+    gains = sum_over(
+        jnp.concatenate([attn_gain, ffn_gain, head_gains[0]], axis=0).reshape(-1, 128),
+        ("core", "x", "y"),
+    )
+    gains, up_sum, qkv_sum, out_sum, branch_two = tie(
+        gains, up_sum, qkv_sum, out_sum, branch_two
+    )
+    w_up_grad, w_qkv_grad = return_columns([up_sum, qkv_sum])
+    w_qkv_grad = w_qkv_grad[:, :joined_columns]
+    gains = sum_over(gains, ("zl", "zh")).reshape(-1)
+    w_out_grad = reduce_zh(out_sum).reshape(-1, out_sum.shape[-1])
+    result = (middle + branch_two).astype(bf16)
     return (
         result,
         input_grad,

time: 672 us -> 563 us (0.84)
  waiting for transfers between devices: 361 us -> 256 us
  matrix products: 77.3 us -> 17.3 us
  Pallas kernels: 24.4 us -> 75.4 us
  starting transfers between devices: 72.4 us -> 101 us
  local copies, waits for them, and re-layouts: 77.1 us -> 52.7 us
    all_gather x5 -> x4, waiting for transfers between devices: 114 us -> 1.07 us  [the longest x1 1.05 us: local(): normed_team = lax.all_gather(normed_low, TEAM, axis=0, tiled=True)]
    ppermute x0 -> x9, waiting for transfers between devices: none -> 68.8 us  [team_chips(): lax.ppermute(block(chip ^ k), CHIPS, [(i, i ^ k) for i in range(chips)])]
    ppermute x21 -> x27, waiting for transfers between devices: 171 us -> 118 us  [swap(): return lax.ppermute(value, axis, [(i, i ^ k) for i in range(n)])]
    pallas_call x0 -> x6, Pallas kernels: none -> 51 us  [the longest x3 31.1 us: by_tokens(): pl.pallas_call(functools.partial(kernel, lax.axis_size('core')), out_shap...]
    dot_general x5 -> x2, matrix products: 28.2 us -> 5.17 us  [dot_nn(): return jnp.dot(left, right, preferred_element_type=f32)]
    dot_general x4 -> x2, matrix products: 28.7 us -> 5.88 us  [dot_nt(): lax.dot_general(left, right, (((1,), (1,)), ((), ())), preferred_element_...]
    all_to_all x6 -> x8, waiting for transfers between devices: 45.9 us -> 23.5 us  [the longest x1 8.93 us: local(): lax.all_to_all(joined_team.reshape(team, tokens, -1), TEAM, 0, 0, tiled=T...]
    all_to_all x2 -> x1, waiting for transfers between devices: 0.01 us -> 20.8 us  [row_team(): lax.all_to_all(split, TEAM, 0, 0, tiled=True).reshape(team * tokens, -1)]
  transfers between devices with their start and end apart: 43 -> 61, of which waited for: 16 -> 31; matrix products, arithmetic and copies ran while one was open for 24% -> 14% of each run, Pallas kernels for 4% -> 14%
where the time goes in v2:
time: 563 us; the launch traced here: 555 us
  waiting for transfers between devices  256 us (45%)
  starting transfers between devices  101 us (18%)
  Pallas kernels  75.4 us (13%)
  local copies, waits for them, and re-layouts  52.7 us (9%)
  other arithmetic  37.3 us (7%)
  matrix products  17.3 us (3%)
  between operations  15.4 us (3%)
    ppermute x27, waiting for transfers between devices, swap(): return lax.ppermute(value, axis, [(i, i ^ k) for i in range(n)])  118 us
    ppermute x9, waiting for transfers between devices, team_chips(): lax.ppermute(block(chip ^ k), CHIPS, [(i, i ^ k) for i in range(chips)])  68.8 us
    ppermute x27, starting transfers between devices, swap(): return lax.ppermute(value, axis, [(i, i ^ k) for i in range(n)])  34.5 us
    pallas_call x3, Pallas kernels, by_tokens(): pl.pallas_call(functools.partial(kernel, lax.axis_size('core')), out_shap...  31.1 us
    ppermute x8, waiting for transfers between devices, shifted(): lax.ppermute(value, SEQ, [(i, i + step) for i in range(n) if 0 <= i + ste...  23.1 us
    all_to_all x1, waiting for transfers between devices, row_team(): lax.all_to_all(split, TEAM, 0, 0, tiled=True).reshape(team * tokens, -1)  20.8 us
    pallas_call x3, Pallas kernels, weight_grad(): pl.pallas_call(weight_grad_kernel, out_shape=jax.ShapeDtypeStruct((model,...  19.9 us
    all_to_all x4, starting transfers between devices, team_columns(): blocks = lax.all_to_all(blocks.transpose(1, 0, 2), TEAM, 0, 0, tiled=True)  19.3 us
  transfers between devices with their start and end apart: 61, of which 31 were waited for; matrix products, arithmetic and copies ran while one was open for 14% of the time, Pallas kernels for 14%

profile of v2, /device:TPU:0, one launch (start us, length us, event | category | flops | bytes accessed | tf_op | source)
XLA Modules:
  0.0 555.4 jit_solution(3082576529726771642)
XLA Ops:
  11.5 5.2 all-to-all-start
  16.7 6.6 %all-to-all-done = bf16[8,64,256]{2,1,0:T(8,128)(2,1)S(1)} async-done(((bf16[8,64,256]{2,1,0:T(8,128)(2,1)}), bf16[8,64,256]{2,1,0:T(8,128)(2,1)S(1)}, u32[]{:S(2)}, u32[]{:S(2)}) %all-to-all-start) | async-done | bytes 262176 | tf_op jit(solution)/shard_map/all_to_all | solution.py:347
  33.1 13.3 %collective-permute-done.4 = bf16[1,1,64,1280]{3,2,1,0:T(8,128)(2,1)} collective-permute-done((bf16[1,1,64,1280]{3,2,1,0:T(8,128)(2,1)S(1)}, bf16[1,1,64,1280]{3,2,1,0:T(8,128)(2,1)}, u32[]{:S(2)}, u32[]{:S(2)}) %collective-permute-start.4) | collective-permute-done | bytes 163872 | tf_op jit(solution)/shard_map/ppermute | solution.py:331
  53.6 3.9 collective-permute-done.2
  58.7 4.3 convolution_convert_fusion.4
  70.6 12.9 %collective-permute-done.6 = bf16[1,2,1,256,640]{4,3,1,2,0:T(8,128)(2,1)S(1)} collective-permute-done((bf16[1,2,1,256,640]{4,3,1,2,0:T(8,128)(2,1)S(1)}, bf16[1,2,1,256,640]{4,3,1,2,0:T(8,128)(2,1)S(1)}, u32[]{:S(2)}, u32[]{:S(2)}) %collective-permute-start.6) | collective-permute-done | bytes 655392 | tf_op jit(solution)/shard_map/ppermute | solution.py:331
  83.5 8.9 %all-to-all-done.2.qkv_ref = bf16[8,128,256]{2,1,0:T(8,128)(2,1)S(1)} async-done(((bf16[8,128,256]{2,1,0:T(8,128)(2,1)}), bf16[8,128,256]{2,1,0:T(8,128)(2,1)S(1)}, u32[]{:S(2)}, u32[]{:S(2)}) %all-to-all-start.2) | async-done | bytes 524320 | tf_op jit(solution)/shard_map/all_to_all | solution.py:518
  92.4 4.9 heads_forward.1
  102.2 3.9 collective-permute-start.8
  109.4 4.8 collective-permute-done.8.refs_2_
  114.8 3.9 collective-permute-done.9.refs_3_
  121.6 6.4 %all-to-all-start.3 = ((bf16[8,64,640]{2,1,0:T(8,128)(2,1)}), bf16[8,64,640]{2,1,0:T(8,128)(2,1)S(1)}, u32[]{:S(2)}, u32[]{:S(2)}) async-start(bf16[8,64,640]{2,1,0:T(8,128)(2,1)} %copy.79), calls=%async_computation.3 | async-start | bytes 1310720 | tf_op jit(solution)/shard_map/all_to_all | solution.py:347
  130.0 6.1 %attend_forward.1 = (bf16[128,1280]{1,0:T(8,128)(2,1)}, f32[8,512]{1,0:T(8,128)S(1)}) custom-call(s32[1,512]{1,0:T(1,128)S(1)} %bitcast.196, bf16[128,1280]{1,0:T(8,128)(2,1)S(1)} %get-tuple-element.116.q_ref, bf16[128,640]{1,0:T(8,128)(2,1)S(1)} %get-tuple-element.119.refs_0_, bf16[128,640]{1,0:T(8,128)(2,1)S(1)} %collective-permute-done.7.refs_1_, ...), custom_call_target="tpu_custom_call" | custom-call | flops 419430400 | bytes 2560000 | tf_op jit(solution)/shard_map/attend_forward/pallas_call | solution.py:546
  136.2 5.4 copy.78
  141.6 4.6 multiply_reduce_fusion.2
  149.2 4.2 all-to-all-start.4
  154.9 5.1 collective-permute-start.13
  160.6 10.7 %collective-permute-done.12 = bf16[1,2,1,256,640]{4,3,1,2,0:T(8,128)(2,1)S(1)} collective-permute-done((bf16[1,2,1,256,640]{4,3,1,2,0:T(8,128)(2,1)}, bf16[1,2,1,256,640]{4,3,1,2,0:T(8,128)(2,1)S(1)}, u32[]{:S(2)}, u32[]{:S(2)}) %collective-permute-start.12) | collective-permute-done | bytes 655392 | tf_op jit(solution)/shard_map/ppermute | solution.py:331
  172.1 15.5 %collective-permute-done.13 = bf16[1,2,1,256,640]{4,3,1,2,0:T(8,128)(2,1)} collective-permute-done((bf16[1,2,1,256,640]{4,3,1,2,0:T(8,128)(2,1)S(1)}, bf16[1,2,1,256,640]{4,3,1,2,0:T(8,128)(2,1)}, u32[]{:S(2)}, u32[]{:S(2)}) %collective-permute-start.13) | collective-permute-done | bytes 655392 | tf_op jit(solution)/shard_map/ppermute | solution.py:331
  187.6 3.8 collective-permute-start.16
  194.3 6.1 %ffn_dz.1.dz_ref = f32[1024,640]{1,0:T(8,128)S(1)} custom-call(s32[8]{0:T(128)S(1)} %stack.35.offsets, bf16[1024,2048]{1,0:T(8,128)(2,1)} %all-gather.11.cloned.1.call-done.grads_ref.rows_ref, bf16[512,640]{1,0:T(8,128)(2,1)S(1)} %bitcast.185, bf16[512,640]{1,0:T(8,128)(2,1)S(1)} %bitcast.202, bf16[512,640]{1,0:T(8,128)(2,1)S(1)} %bitcast.204, ...), custom_call_target="tpu_custom_call" | custom-call | flops 2684354560 | bytes 6815744 | tf_op jit(solution)/shard_map/ffn_dz/pallas_call | solution.py:303
  201.9 3.7 collective-permute-done.15
  205.6 14.3 %collective-permute-done.16 = bf16[1,2,1,256,640]{4,3,1,2,0:T(8,128)(2,1)} collective-permute-done((bf16[1,2,1,256,640]{4,3,1,2,0:T(8,128)(2,1)S(1)}, bf16[1,2,1,256,640]{4,3,1,2,0:T(8,128)(2,1)}, u32[]{:S(2)}, u32[]{:S(2)}) %collective-permute-start.16) | collective-permute-done | bytes 655392 | tf_op jit(solution)/shard_map/ppermute | solution.py:331
  220.7 15.1 %collective-permute-done.18 = bf16[1,2,1,256,640]{4,3,1,2,0:T(8,128)(2,1)} collective-permute-done((bf16[1,2,1,256,640]{4,3,1,2,0:T(8,128)(2,1)}, bf16[1,2,1,256,640]{4,3,1,2,0:T(8,128)(2,1)}, u32[]{:S(2)}, u32[]{:S(2)}) %collective-permute-start.18) | collective-permute-done | bytes 655392 | tf_op jit(solution)/shard_map/ppermute | solution.py:331
  235.8 19.2 %ffn_mid.1 = (bf16[1024,640]{1,0:T(8,128)(2,1)}, bf16[1024,640]{1,0:T(8,128)(2,1)}, bf16[1024,640]{1,0:T(8,128)(2,1)}, bf16[1024,2048]{1,0:T(8,128)(2,1)}) custom-call(s32[8]{0:T(128)S(1)} %stack.35.offsets, bf16[1024,2048]{1,0:T(8,128)(2,1)} %all-gather.9.cloned.1.call-done.mid_ref.rows_ref, f32[1024,640]{1,0:T(8,128)} %copy-done.23, ...), custom_call_target="tpu_custom_call" | custom-call | flops 10737418240 | bytes 10747904 | tf_op jit(solution)/shard_map/ffn_mid/pallas_call | solution.py:303
  260.4 6.6 %down_grad.1 = bf16[2048,640]{1,0:T(8,128)(2,1)} custom-call(bf16[1024,2048]{1,0:T(8,128)(2,1)S(1)} %copy-done.4, bf16[1024,640]{1,0:T(8,128)(2,1)S(1)} %copy-done.24), custom_call_target="tpu_custom_call" | custom-call | flops 2684354560 | bytes 8126464 | tf_op jit(solution)/shard_map/down_grad/pallas_call | solution.py:268
  267.3 4.5 fusion.2
  271.8 5.8 %ffn_out.1 = bf16[1024,2048]{1,0:T(8,128)(2,1)} custom-call(s32[8]{0:T(128)S(1)} %stack.35.offsets, bf16[1024,640]{1,0:T(8,128)(2,1)S(1)} %copy-done.24, bf16[512,640]{1,0:T(8,128)(2,1)S(1)} %bitcast.186, bf16[512,640]{1,0:T(8,128)(2,1)S(1)} %bitcast.203, bf16[512,640]{1,0:T(8,128)(2,1)S(1)} %bitcast.205, bf16[512,640]{1,0:T(8,128)(2,1)S(1)} %bitcast.207), custom_call_target="tpu_custom_call" | custom-call | flops 2684354560 | bytes 3932160 | tf_op jit(solution)/shard_map/ffn_out/pallas_call | solution.py:303
  286.4 10.3 %collective-permute-done.20 = bf16[128,2048]{1,0:T(8,128)(2,1)S(1)} collective-permute-done((bf16[128,2048]{1,0:T(8,128)(2,1)S(1)}, bf16[128,2048]{1,0:T(8,128)(2,1)S(1)}, u32[]{:S(2)}, u32[]{:S(2)}) %collective-permute-start.20) | collective-permute-done | bytes 524320 | tf_op jit(solution)/shard_map/ppermute | solution.py:415
  296.7 13.8 %collective-permute-done.21 = bf16[128,2048]{1,0:T(8,128)(2,1)} collective-permute-done((bf16[128,2048]{1,0:T(8,128)(2,1)S(1)}, bf16[128,2048]{1,0:T(8,128)(2,1)}, u32[]{:S(2)}, u32[]{:S(2)}) %collective-permute-start.21) | collective-permute-done | bytes 524320 | tf_op jit(solution)/shard_map/ppermute | solution.py:415
  310.6 14.4 %collective-permute-done.22 = bf16[128,2048]{1,0:T(8,128)(2,1)} collective-permute-done((bf16[128,2048]{1,0:T(8,128)(2,1)S(1)}, bf16[128,2048]{1,0:T(8,128)(2,1)}, u32[]{:S(2)}, u32[]{:S(2)}) %collective-permute-start.22) | collective-permute-done | bytes 524320 | tf_op jit(solution)/shard_map/ppermute | solution.py:415
  326.8 4.9 fusion.1
  334.6 6.2 %attend_backward.1 = (f32[128,1280]{1,0:T(8,128)S(1)}, f32[128,640]{1,0:T(8,128)S(1)}, bf16[128,640]{1,0:T(8,128)(2,1)S(1)}, bf16[128,640]{1,0:T(8,128)(2,1)S(1)...) custom-call(s32[1,512]{1,0:T(1,128)S(1)} %bitcast.197, bf16[128,1280]{1,0:T(8,128)(2,1)S(1)} %copy-done.12, ...), custom_call_target="tpu_custom_call" | custom-call | flops 1048576000 | bytes 5120000 | tf_op jit(solution)/shard_map/attend_backward/pallas_call | solution.py:613
  346.4 6.6 %gate_grad.1 = bf16[2048,640]{1,0:T(8,128)(2,1)} custom-call(bf16[1024,2048]{1,0:T(8,128)(2,1)S(1)} %copy-done.2, bf16[1024,640]{1,0:T(8,128)(2,1)S(1)} %copy-done.26), custom_call_target="tpu_custom_call" | custom-call | flops 2684354560 | bytes 8126464 | tf_op jit(solution)/shard_map/gate_grad/pallas_call | solution.py:268
  355.9 11.2 %collective-permute-done.27.refs_3_ = bf16[128,640]{1,0:T(8,128)(2,1)S(1)} collective-permute-done((bf16[128,640]{1,0:T(8,128)(2,1)S(1)}, bf16[128,640]{1,0:T(8,128)(2,1)S(1)}, u32[]{:S(2)}, u32[]{:S(2)}) %collective-permute-start.27) | collective-permute-done | bytes 163872 | tf_op jit(solution)/shard_map/ppermute | solution.py:336
  367.0 7.2 %heads_backward.1 = (bf16[8,128,256]{2,1,0:T(8,128)(2,1)}, f32[1,128]{1,0:T(1,128)S(1)}) custom-call(bf16[8,128,256]{2,1,0:T(8,128)(2,1)S(1)} %all-to-all-done.2.qkv_ref, f32[128,64]{1,0:T(8,128)S(1)} %get-tuple-element.225.cos_ref, f32[128,64]{1,0:T(8,128)S(1)} %get-tuple-element.224.sin_ref, f32[1,64]{1,0:T(1,128)S(1)} %bitcast.199, ...), custom_call_target="tpu_custom_call" | custom-call | flops 7372800 | bytes 3932160 | tf_op jit(solution)/shard_map/heads_backward/pallas_call | solution.py:630
  381.3 6.6 %up_grad.1 = bf16[2048,640]{1,0:T(8,128)(2,1)} custom-call(bf16[1024,2048]{1,0:T(8,128)(2,1)S(1)} %copy-done.3, bf16[1024,640]{1,0:T(8,128)(2,1)S(1)} %copy-done.25), custom_call_target="tpu_custom_call" | custom-call | flops 2684354560 | bytes 8126464 | tf_op jit(solution)/shard_map/up_grad/pallas_call | solution.py:268
  387.9 4.4 all-to-all-done.5
  394.4 3.8 collective-permute-done.28
  404.2 10.7 %collective-permute-done.29 = bf16[128,2048]{1,0:T(8,128)(2,1)S(1)} collective-permute-done((bf16[128,2048]{1,0:T(8,128)(2,1)S(1)}, bf16[128,2048]{1,0:T(8,128)(2,1)S(1)}, u32[]{:S(2)}, u32[]{:S(2)}) %collective-permute-start.29) | collective-permute-done | bytes 524320 | tf_op jit(solution)/shard_map/ppermute | solution.py:415
  414.9 7.3 %collective-permute-done.30 = bf16[128,2048]{1,0:T(8,128)(2,1)} collective-permute-done((bf16[128,2048]{1,0:T(8,128)(2,1)S(1)}, bf16[128,2048]{1,0:T(8,128)(2,1)}, u32[]{:S(2)}, u32[]{:S(2)}) %collective-permute-start.30) | collective-permute-done | bytes 524320 | tf_op jit(solution)/shard_map/ppermute | solution.py:415
  422.2 12.2 %collective-permute-done.31 = bf16[128,2048]{1,0:T(8,128)(2,1)} collective-permute-done((bf16[128,2048]{1,0:T(8,128)(2,1)S(1)}, bf16[128,2048]{1,0:T(8,128)(2,1)}, u32[]{:S(2)}, u32[]{:S(2)}) %collective-permute-start.31) | collective-permute-done | bytes 524320 | tf_op jit(solution)/shard_map/ppermute | solution.py:415
  449.9 3.7 convolution_convert_fusion.2
  460.4 8.7 %collective-permute-done.34 = f32[33,128]{1,0:T(8,128)S(1)} collective-permute-done((f32[33,128]{1,0:T(8,128)S(1)}, f32[33,128]{1,0:T(8,128)S(1)}, u32[]{:S(2)}, u32[]{:S(2)}) %collective-permute-start.34) | collective-permute-done | bytes 16928 | tf_op jit(solution)/shard_map/ppermute | solution.py:331
  469.2 20.8 %all-to-all-done.6 = bf16[8,128,256]{1,2,0:T(8,128)(2,1)S(1)} async-done(((bf16[8,128,256]{1,2,0:T(8,128)(2,1)}), bf16[8,128,256]{1,2,0:T(8,128)(2,1)S(1)}, u32[]{:S(2)}, u32[]{:S(2)}) %all-to-all-start.6) | async-done | bytes 524320 | tf_op jit(solution)/shard_map/all_to_all | solution.py:434
  489.9 4.4 all-to-all-start.8
  502.6 12.6 %collective-permute-done.36 = bf16[2,256,256]{2,1,0:T(8,128)(2,1)} collective-permute-done((bf16[2,256,256]{2,1,0:T(8,128)(2,1)}, bf16[2,256,256]{2,1,0:T(8,128)(2,1)}, u32[]{:S(2)}, u32[]{:S(2)}) %collective-permute-start.36) | collective-permute-done | bytes 262176 | tf_op jit(solution)/shard_map/ppermute | solution.py:331
  526.5 4.2 all-to-all-start.7
  (287 shorter events, 156.2 us)
Async XLA Ops:
  7.2 51.4 %all-gather.7.cloned.1.call-start = ((), (), s32[]{:S(2)}) async-start(), calls=%async_computation.12 | async-start | bytes 4718592 | tf_op jit(solution)/shard_map/all_gather | solution.py:494
  23.3 27.0 %collective-permute-start = (bf16[1,2,1,256,256]{4,3,1,2,0:T(8,128)(2,1)S(1)}, bf16[1,2,1,256,256]{4,3,1,2,0:T(8,128)(2,1)S(1)}, u32[]{:S(2)}, u32[]{:S(2)}) collective-permute-start(bf16[1,2,1,256,256]{4,3,1,2,0:T(8,128)(2,1)S(1)} %bitcast.240), channel_id=1, source_target_pairs={{0,16},{16,0},{1,17},{17,1},{2,18},{18,2},{3,19},{19,3},{4,20},{20... | collective-permute-start | bytes 786440 | tf_op jit(solution)/shard_map/ppermute | solution.py:331
  24.8 24.3 %collective-permute-start.1 = (bf16[1,2,1,256,256]{4,3,1,2,0:T(8,128)(2,1)S(1)}, bf16[1,2,1,256,256]{4,3,1,2,0:T(8,128)(2,1)S(1)}, u32[]{:S(2)}, u32[]{:S(2)}) collective-permute-start(bf16[1,2,1,256,256]{4,3,1,2,0:T(8,128)(2,1)S(1)} %bitcast.241), channel_id=1, source_target_pairs={{0,4},{4,0},{1,5},{5,1},{2,6},{6,2},{3,7},{7,3},{8,12},{12,8},{9,1... | collective-permute-start | bytes 786440 | tf_op jit(solution)/shard_map/ppermute | solution.py:331
  27.4 19.8 %collective-permute-start.3 = (bf16[1,1,64,1280]{3,2,1,0:T(8,128)(2,1)S(1)}, bf16[1,1,64,1280]{3,2,1,0:T(8,128)(2,1)}, u32[]{:S(2)}, u32[]{:S(2)}) collective-permute-start(bf16[1,1,64,1280]{3,2,1,0:T(8,128)(2,1)S(1)} %bitcast.255), channel_id=1, source_target_pairs={{0,16},{16,0},{1,17},{17,1},{2,18},{18,2},{3,19},{19,3},{4,20},{20... | collective-permute-start | bytes 491528 | tf_op jit(solution)/shard_map/ppermute | solution.py:331
  27.9 18.4 %collective-permute-start.4 = (bf16[1,1,64,1280]{3,2,1,0:T(8,128)(2,1)S(1)}, bf16[1,1,64,1280]{3,2,1,0:T(8,128)(2,1)}, u32[]{:S(2)}, u32[]{:S(2)}) collective-permute-start(bf16[1,1,64,1280]{3,2,1,0:T(8,128)(2,1)S(1)} %bitcast.256), channel_id=1, source_target_pairs={{0,4},{4,0},{1,5},{5,1},{2,6},{6,2},{3,7},{7,3},{8,12},{12,8},{9,1... | collective-permute-start | bytes 491528 | tf_op jit(solution)/shard_map/ppermute | solution.py:331
  29.3 28.3 %all-to-all-start.1 = ((bf16[8,64,640]{2,1,0:T(8,128)(2,1)}), bf16[8,64,640]{2,1,0:T(8,128)(2,1)S(1)}, u32[]{:S(2)}, u32[]{:S(2)}) async-start(bf16[8,64,640]{2,1,0:T(8,128)(2,1)} %copy.77), calls=%async_computation.1 | async-start | bytes 1310720 | tf_op jit(solution)/shard_map/all_to_all | solution.py:347
  32.8 103.3 %all-gather.15.cloned.1.call-start = ((), (), s32[]{:S(2)}) async-start(), calls=%async_computation.19 | async-start | bytes 5898240 | tf_op jit(solution)/shard_map/all_gather | solution.py:510
  62.9 29.5 %all-to-all-start.2 = ((bf16[8,128,256]{2,1,0:T(8,128)(2,1)}), bf16[8,128,256]{2,1,0:T(8,128)(2,1)S(1)}, u32[]{:S(2)}, u32[]{:S(2)}) async-start(bf16[8,128,256]{2,1,0:T(8,128)(2,1)} %bitcast.11), calls=%async_computation.2 | async-start | bytes 1048576 | tf_op jit(solution)/shard_map/all_to_all | solution.py:518
  66.4 105.7 %all-gather.11.cloned.1.call-start = ((), (), s32[]{:S(2)}) async-start(), calls=%async_computation.14 | async-start | bytes 4718592 | tf_op jit(solution)/shard_map/all_gather | solution.py:544
  66.5 17.0 %collective-permute-start.6 = (bf16[1,2,1,256,640]{4,3,1,2,0:T(8,128)(2,1)S(1)}, bf16[1,2,1,256,640]{4,3,1,2,0:T(8,128)(2,1)S(1)}, u32[]{:S(2)}, u32[]{:S(2)}) collective-permute-start(bf16[1,2,1,256,640]{4,3,1,2,0:T(8,128)(2,1)S(1)} %bitcast.183), channel_id=1, source_target_pairs={{0,16},{16,0},{1,17},{17,1},{2,18},{18,2},{3,19},{19,3},{4,20},{20... | collective-permute-start | bytes 1966088 | tf_op jit(solution)/shard_map/ppermute | solution.py:331
  68.0 40.9 %collective-permute-start.11 = (bf16[1,2,1,256,640]{4,3,1,2,0:T(8,128)(2,1)S(1)}, bf16[1,2,1,256,640]{4,3,1,2,0:T(8,128)(2,1)S(1)}, u32[]{:S(2)}, u32[]{:S(2)}) collective-permute-start(bf16[1,2,1,256,640]{4,3,1,2,0:T(8,128)(2,1)S(1)} %bitcast.184), channel_id=1, source_target_pairs={{0,4},{4,0},{1,5},{5,1},{2,6},{6,2},{3,7},{7,3},{8,12},{12,8},{9,1... | collective-permute-start | bytes 1966088 | tf_op jit(solution)/shard_map/ppermute | solution.py:331
  102.2 11.9 %collective-permute-start.8 = (bf16[128,640]{1,0:T(8,128)(2,1)S(1)}, bf16[128,640]{1,0:T(8,128)(2,1)S(1)}, u32[]{:S(2)}, u32[]{:S(2)}) collective-permute-start(bf16[128,640]{1,0:T(8,128)(2,1)S(1)} %get-tuple-element.119.refs_0_), channel_id=1, source_target_pairs={{0,2},{1,3},{2,4},{3,5},{4,6},{5,7},{8,10},{9,11},{10,12},{11,13},... | collective-permute-start | bytes 491528 | tf_op jit(solution)/shard_map/ppermute | solution.py:336
  106.2 12.6 %collective-permute-start.9 = (bf16[128,640]{1,0:T(8,128)(2,1)S(1)}, bf16[128,640]{1,0:T(8,128)(2,1)S(1)}, u32[]{:S(2)}, u32[]{:S(2)}) collective-permute-start(bf16[128,640]{1,0:T(8,128)(2,1)S(1)} %get-tuple-element.119.refs_0_), channel_id=1, source_target_pairs={{0,3},{1,4},{2,5},{3,6},{4,7},{8,11},{9,12},{10,13},{11,14},{12,15... | collective-permute-start | bytes 491528 | tf_op jit(solution)/shard_map/ppermute | solution.py:336
  121.6 20.0 %all-to-all-start.3 = ((bf16[8,64,640]{2,1,0:T(8,128)(2,1)}), bf16[8,64,640]{2,1,0:T(8,128)(2,1)S(1)}, u32[]{:S(2)}, u32[]{:S(2)}) async-start(bf16[8,64,640]{2,1,0:T(8,128)(2,1)} %copy.79), calls=%async_computation.3 | async-start | bytes 1310720 | tf_op jit(solution)/shard_map/all_to_all | solution.py:347
  127.9 91.9 %all-gather.9.cloned.1.call-start = ((), (), s32[]{:S(2)}) async-start(), calls=%async_computation.13 | async-start | bytes 4718592 | tf_op jit(solution)/shard_map/all_gather | solution.py:564
  149.2 38.4 %all-to-all-start.4 = ((bf16[8,64,640]{2,1,0:T(8,128)(2,1)}), bf16[8,64,640]{2,1,0:T(8,128)(2,1)S(1)}, u32[]{:S(2)}, u32[]{:S(2)}) async-start(bf16[8,64,640]{2,1,0:T(8,128)(2,1)} %copy.80), calls=%async_computation.4 | async-start | bytes 1310720 | tf_op jit(solution)/shard_map/all_to_all | solution.py:347
  153.4 101.6 %all-gather.13.cloned.1.call-start = ((), (), s32[]{:S(2)}) async-start(), calls=%async_computation.15 | async-start | bytes 2949120 | tf_op jit(solution)/shard_map/all_gather | solution.py:579
  153.4 17.8 %collective-permute-start.12 = (bf16[1,2,1,256,640]{4,3,1,2,0:T(8,128)(2,1)}, bf16[1,2,1,256,640]{4,3,1,2,0:T(8,128)(2,1)S(1)}, u32[]{:S(2)}, u32[]{:S(2)}) collective-permute-start(bf16[1,2,1,256,640]{4,3,1,2,0:T(8,128)(2,1)} %copy-done.5), channel_id=1, source_target_pairs={{0,16},{16,0},{1,17},{17,1},{2,18},{18,2},{3,19},{19,3},{4,20},{20... | collective-permute-start | bytes 1966088 | tf_op jit(solution)/shard_map/ppermute | solution.py:331
  154.9 32.7 %collective-permute-start.13 = (bf16[1,2,1,256,640]{4,3,1,2,0:T(8,128)(2,1)S(1)}, bf16[1,2,1,256,640]{4,3,1,2,0:T(8,128)(2,1)}, u32[]{:S(2)}, u32[]{:S(2)}) collective-permute-start(bf16[1,2,1,256,640]{4,3,1,2,0:T(8,128)(2,1)S(1)} %bitcast.187), channel_id=1, source_target_pairs={{0,4},{4,0},{1,5},{5,1},{2,6},{6,2},{3,7},{7,3},{8,12},{12,8},{9,1... | collective-permute-start | bytes 1966088 | tf_op jit(solution)/shard_map/ppermute | solution.py:331
  160.0 27.6 %collective-permute-start.14 = (bf16[1,2,1,256,640]{4,3,1,2,0:T(8,128)(2,1)S(1)}, bf16[1,2,1,256,640]{4,3,1,2,0:T(8,128)(2,1)}, u32[]{:S(2)}, u32[]{:S(2)}) collective-permute-start(bf16[1,2,1,256,640]{4,3,1,2,0:T(8,128)(2,1)S(1)} %bitcast.188), channel_id=1, source_target_pairs={{0,16},{16,0},{1,17},{17,1},{2,18},{18,2},{3,19},{19,3},{4,20},{20... | collective-permute-start | bytes 1966088 | tf_op jit(solution)/shard_map/ppermute | solution.py:331
  187.6 18.0 %collective-permute-start.15 = (bf16[1,2,1,256,640]{4,3,1,2,0:T(8,128)(2,1)}, bf16[1,2,1,256,640]{4,3,1,2,0:T(8,128)(2,1)}, u32[]{:S(2)}, u32[]{:S(2)}) collective-permute-start(bf16[1,2,1,256,640]{4,3,1,2,0:T(8,128)(2,1)} %collective-permute-done.13), channel_id=1, source_target_pairs={{0,16},{16,0},{1,17},{17,1},{2,18},{18,2},{3,19},{19,3},{4,20},{20... | collective-permute-start | bytes 1966088 | tf_op jit(solution)/shard_map/ppermute | solution.py:331
  187.6 32.3 %collective-permute-start.16 = (bf16[1,2,1,256,640]{4,3,1,2,0:T(8,128)(2,1)S(1)}, bf16[1,2,1,256,640]{4,3,1,2,0:T(8,128)(2,1)}, u32[]{:S(2)}, u32[]{:S(2)}) collective-permute-start(bf16[1,2,1,256,640]{4,3,1,2,0:T(8,128)(2,1)S(1)} %bitcast.190), channel_id=1, source_target_pairs={{0,4},{4,0},{1,5},{5,1},{2,6},{6,2},{3,7},{7,3},{8,12},{12,8},{9,1... | collective-permute-start | bytes 1966088 | tf_op jit(solution)/shard_map/ppermute | solution.py:331
  191.4 28.4 %collective-permute-start.17 = (bf16[1,2,1,256,640]{4,3,1,2,0:T(8,128)(2,1)S(1)}, bf16[1,2,1,256,640]{4,3,1,2,0:T(8,128)(2,1)}, u32[]{:S(2)}, u32[]{:S(2)}) collective-permute-start(bf16[1,2,1,256,640]{4,3,1,2,0:T(8,128)(2,1)S(1)} %bitcast.191), channel_id=1, source_target_pairs={{0,16},{16,0},{1,17},{17,1},{2,18},{18,2},{3,19},{19,3},{4,20},{20... | collective-permute-start | bytes 1966088 | tf_op jit(solution)/shard_map/ppermute | solution.py:331
  219.9 147.1 %reduce-scatter.4.cloned.1.call-start = ((), (), s32[]{:S(2)}) async-start(), calls=%async_computation.16 | async-start | bytes 3276800 | tf_op jit(solution)/shard_map/reduce_scatter | solution.py:590
  219.9 15.8 %collective-permute-start.18 = (bf16[1,2,1,256,640]{4,3,1,2,0:T(8,128)(2,1)}, bf16[1,2,1,256,640]{4,3,1,2,0:T(8,128)(2,1)}, u32[]{:S(2)}, u32[]{:S(2)}) collective-permute-start(bf16[1,2,1,256,640]{4,3,1,2,0:T(8,128)(2,1)} %collective-permute-done.16), channel_id=1, source_target_pairs={{0,16},{16,0},{1,17},{17,1},{2,18},{18,2},{3,19},{19,3},{4,20},{20... | collective-permute-start | bytes 1966088 | tf_op jit(solution)/shard_map/ppermute | solution.py:331
  267.0 169.1 %reduce-scatter.6.cloned.1.call-start = ((), (), s32[]{:S(2)}) async-start(), calls=%async_computation.17 | async-start | bytes 3276800 | tf_op jit(solution)/shard_map/reduce_scatter | solution.py:590
  280.8 46.0 %collective-permute-start.23 = (bf16[512,2048]{1,0:T(8,128)(2,1)}, bf16[512,2048]{1,0:T(8,128)(2,1)}, u32[]{:S(2)}, u32[]{:S(2)}) collective-permute-start(bf16[512,2048]{1,0:T(8,128)(2,1)} %dynamic-slice_bitcast_fusion.1), channel_id=1, source_target_pairs={{0,8},{8,0},{1,9},{9,1},{2,10},{10,2},{3,11},{11,3},{4,12},{12,4},... | collective-permute-start | bytes 6291464 | tf_op jit(solution)/shard_map/ppermute | solution.py:331
  282.8 13.9 %collective-permute-start.20 = (bf16[128,2048]{1,0:T(8,128)(2,1)S(1)}, bf16[128,2048]{1,0:T(8,128)(2,1)S(1)}, u32[]{:S(2)}, u32[]{:S(2)}) collective-permute-start(bf16[128,2048]{1,0:T(8,128)(2,1)S(1)} %get-tuple-element.217), channel_id=1, source_target_pairs={{0,1},{1,0},{2,3},{3,2},{4,5},{5,4},{6,7},{7,6},{8,9},{9,8},{10,11... | collective-permute-start | bytes 1572872 | tf_op jit(solution)/shard_map/ppermute | solution.py:415
  283.9 26.6 %collective-permute-start.21 = (bf16[128,2048]{1,0:T(8,128)(2,1)S(1)}, bf16[128,2048]{1,0:T(8,128)(2,1)}, u32[]{:S(2)}, u32[]{:S(2)}) collective-permute-start(bf16[128,2048]{1,0:T(8,128)(2,1)S(1)} %get-tuple-element.219), channel_id=1, source_target_pairs={{0,2},{1,3},{2,0},{3,1},{4,6},{5,7},{6,4},{7,5},{8,10},{9,11},{10,... | collective-permute-start | bytes 1572872 | tf_op jit(solution)/shard_map/ppermute | solution.py:415
  285.4 39.6 %collective-permute-start.22 = (bf16[128,2048]{1,0:T(8,128)(2,1)S(1)}, bf16[128,2048]{1,0:T(8,128)(2,1)}, u32[]{:S(2)}, u32[]{:S(2)}) collective-permute-start(bf16[128,2048]{1,0:T(8,128)(2,1)S(1)} %get-tuple-element.218), channel_id=1, source_target_pairs={{0,3},{1,2},{2,1},{3,0},{4,7},{5,6},{6,5},{7,4},{8,11},{9,10},{10,... | collective-permute-start | bytes 1572872 | tf_op jit(solution)/shard_map/ppermute | solution.py:415
  340.8 12.3 %collective-permute-start.24 = (bf16[128,640]{1,0:T(8,128)(2,1)S(1)}, bf16[128,640]{1,0:T(8,128)(2,1)S(1)}, u32[]{:S(2)}, u32[]{:S(2)}) collective-permute-start(bf16[128,640]{1,0:T(8,128)(2,1)S(1)} %get-tuple-element.172), channel_id=1, source_target_pairs={{1,0},{2,1},{3,2},{4,3},{5,4},{6,5},{7,6},{9,8},{10,9},{11,10},{12... | collective-permute-start | bytes 491528 | tf_op jit(solution)/shard_map/ppermute | solution.py:336
  343.4 12.5 %collective-permute-start.26 = (bf16[128,640]{1,0:T(8,128)(2,1)S(1)}, bf16[128,640]{1,0:T(8,128)(2,1)S(1)}, u32[]{:S(2)}, u32[]{:S(2)}) collective-permute-start(bf16[128,640]{1,0:T(8,128)(2,1)S(1)} %get-tuple-element.174), channel_id=1, source_target_pairs={{3,0},{4,1},{5,2},{6,3},{7,4},{11,8},{12,9},{13,10},{14,11},{15,12... | collective-permute-start | bytes 491528 | tf_op jit(solution)/shard_map/ppermute | solution.py:336
  344.7 22.3 %collective-permute-start.27 = (bf16[128,640]{1,0:T(8,128)(2,1)S(1)}, bf16[128,640]{1,0:T(8,128)(2,1)S(1)}, u32[]{:S(2)}, u32[]{:S(2)}) collective-permute-start(bf16[128,640]{1,0:T(8,128)(2,1)S(1)} %get-tuple-element.175), channel_id=1, source_target_pairs={{4,0},{5,1},{6,2},{7,3},{12,8},{13,9},{14,10},{15,11},{20,16},{21,... | collective-permute-start | bytes 491528 | tf_op jit(solution)/shard_map/ppermute | solution.py:336
  374.2 18.1 %all-to-all-start.5 = ((bf16[8,128,256]{2,1,0:T(8,128)(2,1)}), bf16[8,128,256]{2,1,0:T(8,128)(2,1)S(1)}, u32[]{:S(2)}, u32[]{:S(2)}) async-start(bf16[8,128,256]{2,1,0:T(8,128)(2,1)} %get-tuple-element.185), calls=%async_computation.6 | async-start | bytes 1048576 | tf_op jit(solution)/shard_map/all_to_all | solution.py:643
  377.7 139.4 %reduce-scatter.8.cloned.1.call-start = ((), (), s32[]{:S(2)}) async-start(), calls=%async_computation.18 | async-start | bytes 3276800 | tf_op jit(solution)/shard_map/reduce_scatter | solution.py:590
  400.6 14.3 %collective-permute-start.29 = (bf16[128,2048]{1,0:T(8,128)(2,1)S(1)}, bf16[128,2048]{1,0:T(8,128)(2,1)S(1)}, u32[]{:S(2)}, u32[]{:S(2)}) collective-permute-start(bf16[128,2048]{1,0:T(8,128)(2,1)S(1)} %get-tuple-element.214), channel_id=1, source_target_pairs={{0,1},{1,0},{2,3},{3,2},{4,5},{5,4},{6,7},{7,6},{8,9},{9,8},{10,11... | collective-permute-start | bytes 1572872 | tf_op jit(solution)/shard_map/ppermute | solution.py:415
  400.7 21.5 %collective-permute-start.30 = (bf16[128,2048]{1,0:T(8,128)(2,1)S(1)}, bf16[128,2048]{1,0:T(8,128)(2,1)}, u32[]{:S(2)}, u32[]{:S(2)}) collective-permute-start(bf16[128,2048]{1,0:T(8,128)(2,1)S(1)} %get-tuple-element.216), channel_id=1, source_target_pairs={{0,2},{1,3},{2,0},{3,1},{4,6},{5,7},{6,4},{7,5},{8,10},{9,11},{10,... | collective-permute-start | bytes 1572872 | tf_op jit(solution)/shard_map/ppermute | solution.py:415
  401.1 33.4 %collective-permute-start.31 = (bf16[128,2048]{1,0:T(8,128)(2,1)S(1)}, bf16[128,2048]{1,0:T(8,128)(2,1)}, u32[]{:S(2)}, u32[]{:S(2)}) collective-permute-start(bf16[128,2048]{1,0:T(8,128)(2,1)S(1)} %get-tuple-element.215), channel_id=1, source_target_pairs={{0,3},{1,2},{2,1},{3,0},{4,7},{5,6},{6,5},{7,4},{8,11},{9,10},{10,... | collective-permute-start | bytes 1572872 | tf_op jit(solution)/shard_map/ppermute | solution.py:415
  439.1 60.6 %collective-permute-start.38 = (bf16[128,2048]{1,0:T(8,128)(2,1)}, bf16[128,2048]{1,0:T(8,128)(2,1)}, u32[]{:S(2)}, u32[]{:S(2)}) collective-permute-start(bf16[128,2048]{1,0:T(8,128)(2,1)} %get-tuple-element.211), channel_id=1, source_target_pairs={{0,1},{1,0},{2,3},{3,2},{4,5},{5,4},{6,7},{7,6},{8,9},{9,8},{10,11... | collective-permute-start | bytes 1572872 | tf_op jit(solution)/shard_map/ppermute | solution.py:415
  439.8 59.9 %collective-permute-start.39 = (bf16[128,2048]{1,0:T(8,128)(2,1)}, bf16[128,2048]{1,0:T(8,128)(2,1)}, u32[]{:S(2)}, u32[]{:S(2)}) collective-permute-start(bf16[128,2048]{1,0:T(8,128)(2,1)} %get-tuple-element.213), channel_id=1, source_target_pairs={{0,2},{1,3},{2,0},{3,1},{4,6},{5,7},{6,4},{7,5},{8,10},{9,11},{10,... | collective-permute-start | bytes 1572872 | tf_op jit(solution)/shard_map/ppermute | solution.py:415
  439.8 59.9 %collective-permute-start.40 = (bf16[128,2048]{1,0:T(8,128)(2,1)}, bf16[128,2048]{1,0:T(8,128)(2,1)}, u32[]{:S(2)}, u32[]{:S(2)}) collective-permute-start(bf16[128,2048]{1,0:T(8,128)(2,1)} %get-tuple-element.212), channel_id=1, source_target_pairs={{0,3},{1,2},{2,1},{3,0},{4,7},{5,6},{6,5},{7,4},{8,11},{9,10},{10,... | collective-permute-start | bytes 1572872 | tf_op jit(solution)/shard_map/ppermute | solution.py:415
  445.4 44.5 %all-to-all-start.6 = ((bf16[8,128,256]{1,2,0:T(8,128)(2,1)}), bf16[8,128,256]{1,2,0:T(8,128)(2,1)S(1)}, u32[]{:S(2)}, u32[]{:S(2)}) async-start(bf16[8,128,256]{1,2,0:T(8,128)(2,1)} %bitcast.232), calls=%async_computation.9 | async-start | bytes 1048576 | tf_op jit(solution)/shard_map/all_to_all | solution.py:434
  454.5 39.9 %collective-permute-start.35 = (bf16[2,2,256,256]{3,2,1,0:T(8,128)(2,1)}, bf16[2,2,256,256]{3,2,1,0:T(8,128)(2,1)S(1)}, u32[]{:S(2)}, u32[]{:S(2)}) collective-permute-start(bf16[2,2,256,256]{3,2,1,0:T(8,128)(2,1)} %dynamic-slice_bitcast_fusion.6), channel_id=1, source_target_pairs={{0,16},{16,0},{1,17},{17,1},{2,18},{18,2},{3,19},{19,3},{4,20},{20... | collective-permute-start | bytes 1572872 | tf_op jit(solution)/shard_map/ppermute | solution.py:331
  489.9 36.6 %all-to-all-start.8 = ((bf16[8,64,1280]{2,1,0:T(8,128)(2,1)}), bf16[8,64,1280]{2,1,0:T(8,128)(2,1)}, u32[]{:S(2)}, u32[]{:S(2)}) async-start(bf16[8,64,1280]{2,1,0:T(8,128)(2,1)} %pad_maximum_fusion), calls=%async_computation.11 | async-start | bytes 2621440 | tf_op jit(solution)/shard_map/all_to_all | solution.py:388
  496.4 18.8 %collective-permute-start.36 = (bf16[2,256,256]{2,1,0:T(8,128)(2,1)}, bf16[2,256,256]{2,1,0:T(8,128)(2,1)}, u32[]{:S(2)}, u32[]{:S(2)}) collective-permute-start(bf16[2,256,256]{2,1,0:T(8,128)(2,1)} %fusion.22), channel_id=1, source_target_pairs={{0,4},{4,0},{1,5},{5,1},{2,6},{6,2},{3,7},{7,3},{8,12},{12,8},{9,1... | collective-permute-start | bytes 786440 | tf_op jit(solution)/shard_map/ppermute | solution.py:331
  499.7 16.6 %collective-permute-start.37 = (bf16[1,2,64,1280]{3,2,1,0:T(8,128)(2,1)S(1)}, bf16[1,2,64,1280]{3,2,1,0:T(8,128)(2,1)S(1)}, u32[]{:S(2)}, u32[]{:S(2)}) collective-permute-start(bf16[1,2,64,1280]{3,2,1,0:T(8,128)(2,1)S(1)} %dynamic-slice_bitcast_fusion.13), channel_id=1, source_target_pairs={{0,16},{16,0},{1,17},{17,1},{2,18},{18,2},{3,19},{19,3},{4,20},{20... | collective-permute-start | bytes 983048 | tf_op jit(solution)/shard_map/ppermute | solution.py:331
  521.4 13.8 %collective-permute-start.41 = (bf16[1,64,1280]{2,1,0:T(8,128)(2,1)}, bf16[1,64,1280]{2,1,0:T(8,128)(2,1)}, u32[]{:S(2)}, u32[]{:S(2)}) collective-permute-start(bf16[1,64,1280]{2,1,0:T(8,128)(2,1)} %fusion.23), channel_id=1, source_target_pairs={{0,4},{4,0},{1,5},{5,1},{2,6},{6,2},{3,7},{7,3},{8,12},{12,8},{9,1... | collective-permute-start | bytes 491528 | tf_op jit(solution)/shard_map/ppermute | solution.py:331
  526.5 17.7 %all-to-all-start.7 = ((bf16[8,64,896]{2,1,0:T(8,128)(2,1)}), bf16[8,64,896]{2,1,0:T(8,128)(2,1)}, u32[]{:S(2)}, u32[]{:S(2)}) async-start(bf16[8,64,896]{2,1,0:T(8,128)(2,1)} %pad_maximum_fusion.1), calls=%async_computation.10 | async-start | bytes 1835008 | tf_op jit(solution)/shard_map/all_to_all | solution.py:388
  (68 other events, 561.2 us)
Sparse Core Ops, SparseCore 0:
  10.8 47.7 all-gather.6
  60.8 55.6 all-gather.14
  119.6 37.8 all-gather.10
  159.5 44.9 all-gather.8
  220.0 24.1 all-gather.12
  267.1 62.9 reduce-scatter.3
  367.2 57.0 reduce-scatter.5
  427.2 61.6 reduce-scatter.7

commit v3 on v2

--- a/solution.py
+++ b/solution.py
@@ -643,9 +643,12 @@
     joined_grad = lax.all_to_all(joined_grad, TEAM, 0, 0, tiled=True).reshape(-1, padded // team)
     joined_grad, up_part, down_sum = tie(joined_grad, up_part, down_sum)
     up_sum = scatter(up_part)
-    normed_in_grad = team_sum(dot_nt(joined_grad, qkv_part).astype(bf16))
-    normed_in_grad, gate_sum, joined_grad, down_sum, branch_grad, branch_half = tie(
-        normed_in_grad, gate_sum, joined_grad, down_sum, branch_grad, branch_half
+    normed_half = team_core(dot_nt(joined_grad, qkv_part).astype(bf16))
+    normed_half, branch_grad = tie(normed_half, branch_grad)
+    normed_in_grad = team_chips(normed_half)
+    branch_rows = row_team(branch_grad)
+    normed_in_grad, gate_sum, joined_grad, down_sum, branch_rows, branch_half = tie(
+        normed_in_grad, gate_sum, joined_grad, down_sum, branch_rows, branch_half
     )
     qkv_sum = reduce_zh(
         reduce_y(
@@ -653,7 +656,7 @@
         )
     )
     w_down_grad, w_gate_grad = return_columns([down_sum, gate_sum])
-    out_part = dot_tn(row_team(branch_grad), attended_team).astype(bf16)
+    out_part = dot_tn(branch_rows, attended_team).astype(bf16)
     out_sum = reduce_y(out_part.reshape(ny, 1, nzh, -1, out_part.shape[1]))
     branch_two = team_chips(branch_half)
     weighted_in = normed_in_grad * g_attn
@@ -666,14 +669,14 @@
 
     gains = sum_over(
         jnp.concatenate([attn_gain, ffn_gain, head_gains[0]], axis=0).reshape(-1, 128),
-        ("core", "x", "y"),
+        ("core", "x"),
     )
     gains, up_sum, qkv_sum, out_sum, branch_two = tie(
         gains, up_sum, qkv_sum, out_sum, branch_two
     )
     w_up_grad, w_qkv_grad = return_columns([up_sum, qkv_sum])
     w_qkv_grad = w_qkv_grad[:, :joined_columns]
-    gains = sum_over(gains, ("zl", "zh")).reshape(-1)
+    gains = sum_over(gains, ("y", "zl", "zh")).reshape(-1)
     w_out_grad = reduce_zh(out_sum).reshape(-1, out_sum.shape[-1])
     result = (middle + branch_two).astype(bf16)
     return (

time: 563 us -> 553 us (0.982)
  waiting for transfers between devices: 256 us -> 246 us
    all_to_all x1, waiting for transfers between devices: 20.8 us -> 4.5 us  [row_team(): lax.all_to_all(split, TEAM, 0, 0, tiled=True).reshape(team * tokens, -1)]
    ppermute x27, waiting for transfers between devices: 118 us -> 128 us  [swap(): return lax.ppermute(value, axis, [(i, i ^ k) for i in range(n)])]
    unnamed x115 -> x119, local copies, waits for them, and re-layouts: 19.3 us -> 19.6 us
  transfers between devices with their start and end apart: 61 -> 61, of which waited for: 31 -> 33; matrix products, arithmetic and copies ran while one was open for 14% -> 14% of each run, Pallas kernels for 14% -> 14%
where the time goes in v3:
time: 553 us; the launch traced here: 546 us
  waiting for transfers between devices  246 us (44%)
  starting transfers between devices  106 us (19%)
  Pallas kernels  75.5 us (14%)
  local copies, waits for them, and re-layouts  51.1 us (9%)
  other arithmetic  36.5 us (7%)
  matrix products  15.6 us (3%)
  between operations  15.4 us (3%)
    ppermute x27, waiting for transfers between devices, swap(): return lax.ppermute(value, axis, [(i, i ^ k) for i in range(n)])  128 us
    ppermute x9, waiting for transfers between devices, team_chips(): lax.ppermute(block(chip ^ k), CHIPS, [(i, i ^ k) for i in range(chips)])  65 us
    ppermute x27, starting transfers between devices, swap(): return lax.ppermute(value, axis, [(i, i ^ k) for i in range(n)])  37.7 us
    pallas_call x3, Pallas kernels, by_tokens(): pl.pallas_call(functools.partial(kernel, lax.axis_size('core')), out_shap...  31.1 us
    ppermute x8, waiting for transfers between devices, shifted(): lax.ppermute(value, SEQ, [(i, i + step) for i in range(n) if 0 <= i + ste...  23.1 us
    pallas_call x3, Pallas kernels, weight_grad(): pl.pallas_call(weight_grad_kernel, out_shape=jax.ShapeDtypeStruct((model,...  19.9 us
    unnamed x119, local copies, waits for them, and re-layouts  19.6 us
    all_to_all x4, starting transfers between devices, team_columns(): blocks = lax.all_to_all(blocks.transpose(1, 0, 2), TEAM, 0, 0, tiled=True)  19.3 us
  transfers between devices with their start and end apart: 61, of which 33 were waited for; matrix products, arithmetic and copies ran while one was open for 14% of the time, Pallas kernels for 14%

profile of v3, /device:TPU:0, one launch (start us, length us, event | category | flops | bytes accessed | tf_op | source)
XLA Modules:
  0.0 545.7 jit_solution(6677310683914950632)
XLA Ops:
  11.5 5.2 all-to-all-start
  16.7 6.6 %all-to-all-done = bf16[8,64,256]{2,1,0:T(8,128)(2,1)S(1)} async-done(((bf16[8,64,256]{2,1,0:T(8,128)(2,1)}), bf16[8,64,256]{2,1,0:T(8,128)(2,1)S(1)}, u32[]{:S(2)}, u32[]{:S(2)}) %all-to-all-start) | async-done | bytes 262176 | tf_op jit(solution)/shard_map/all_to_all | solution.py:347
  33.1 13.3 %collective-permute-done.4 = bf16[1,1,64,1280]{3,2,1,0:T(8,128)(2,1)} collective-permute-done((bf16[1,1,64,1280]{3,2,1,0:T(8,128)(2,1)S(1)}, bf16[1,1,64,1280]{3,2,1,0:T(8,128)(2,1)}, u32[]{:S(2)}, u32[]{:S(2)}) %collective-permute-start.4) | collective-permute-done | bytes 163872 | tf_op jit(solution)/shard_map/ppermute | solution.py:331
  53.6 3.9 collective-permute-done.2
  58.7 4.3 convolution_convert_fusion.4
  70.6 12.9 %collective-permute-done.6 = bf16[1,2,1,256,640]{4,3,1,2,0:T(8,128)(2,1)S(1)} collective-permute-done((bf16[1,2,1,256,640]{4,3,1,2,0:T(8,128)(2,1)S(1)}, bf16[1,2,1,256,640]{4,3,1,2,0:T(8,128)(2,1)S(1)}, u32[]{:S(2)}, u32[]{:S(2)}) %collective-permute-start.6) | collective-permute-done | bytes 655392 | tf_op jit(solution)/shard_map/ppermute | solution.py:331
  83.5 8.9 %all-to-all-done.2.qkv_ref = bf16[8,128,256]{2,1,0:T(8,128)(2,1)S(1)} async-done(((bf16[8,128,256]{2,1,0:T(8,128)(2,1)}), bf16[8,128,256]{2,1,0:T(8,128)(2,1)S(1)}, u32[]{:S(2)}, u32[]{:S(2)}) %all-to-all-start.2) | async-done | bytes 524320 | tf_op jit(solution)/shard_map/all_to_all | solution.py:518
  92.4 4.9 heads_forward.1
  102.2 3.9 collective-permute-start.8
  109.4 4.8 collective-permute-done.8.refs_2_
  114.9 3.9 collective-permute-done.9.refs_3_
  121.6 6.4 %all-to-all-start.3 = ((bf16[8,64,640]{2,1,0:T(8,128)(2,1)}), bf16[8,64,640]{2,1,0:T(8,128)(2,1)S(1)}, u32[]{:S(2)}, u32[]{:S(2)}) async-start(bf16[8,64,640]{2,1,0:T(8,128)(2,1)} %copy.79), calls=%async_computation.3 | async-start | bytes 1310720 | tf_op jit(solution)/shard_map/all_to_all | solution.py:347
  130.0 6.1 %attend_forward.1 = (bf16[128,1280]{1,0:T(8,128)(2,1)}, f32[8,512]{1,0:T(8,128)S(1)}) custom-call(s32[1,512]{1,0:T(1,128)S(1)} %bitcast.196, bf16[128,1280]{1,0:T(8,128)(2,1)S(1)} %get-tuple-element.118.q_ref, bf16[128,640]{1,0:T(8,128)(2,1)S(1)} %get-tuple-element.121.refs_0_, bf16[128,640]{1,0:T(8,128)(2,1)S(1)} %collective-permute-done.7.refs_1_, ...), custom_call_target="tpu_custom_call" | custom-call | flops 419430400 | bytes 2560000 | tf_op jit(solution)/shard_map/attend_forward/pallas_call | solution.py:546
  136.2 5.5 copy.78
  141.6 4.6 multiply_reduce_fusion.2
  149.2 4.2 all-to-all-start.4
  155.0 5.0 collective-permute-start.13
  160.6 10.7 %collective-permute-done.12 = bf16[1,2,1,256,640]{4,3,1,2,0:T(8,128)(2,1)S(1)} collective-permute-done((bf16[1,2,1,256,640]{4,3,1,2,0:T(8,128)(2,1)}, bf16[1,2,1,256,640]{4,3,1,2,0:T(8,128)(2,1)S(1)}, u32[]{:S(2)}, u32[]{:S(2)}) %collective-permute-start.12) | collective-permute-done | bytes 655392 | tf_op jit(solution)/shard_map/ppermute | solution.py:331
  172.1 15.4 %collective-permute-done.13 = bf16[1,2,1,256,640]{4,3,1,2,0:T(8,128)(2,1)} collective-permute-done((bf16[1,2,1,256,640]{4,3,1,2,0:T(8,128)(2,1)S(1)}, bf16[1,2,1,256,640]{4,3,1,2,0:T(8,128)(2,1)}, u32[]{:S(2)}, u32[]{:S(2)}) %collective-permute-start.13) | collective-permute-done | bytes 655392 | tf_op jit(solution)/shard_map/ppermute | solution.py:331
  187.6 3.9 collective-permute-start.16
  194.3 6.1 %ffn_dz.1.dz_ref = f32[1024,640]{1,0:T(8,128)S(1)} custom-call(s32[8]{0:T(128)S(1)} %stack.35.offsets, bf16[1024,2048]{1,0:T(8,128)(2,1)} %all-gather.11.cloned.1.call-done.grads_ref.rows_ref, bf16[512,640]{1,0:T(8,128)(2,1)S(1)} %bitcast.185, bf16[512,640]{1,0:T(8,128)(2,1)S(1)} %bitcast.202, bf16[512,640]{1,0:T(8,128)(2,1)S(1)} %bitcast.204, ...), custom_call_target="tpu_custom_call" | custom-call | flops 2684354560 | bytes 6815744 | tf_op jit(solution)/shard_map/ffn_dz/pallas_call | solution.py:303
  205.6 14.3 %collective-permute-done.16 = bf16[1,2,1,256,640]{4,3,1,2,0:T(8,128)(2,1)} collective-permute-done((bf16[1,2,1,256,640]{4,3,1,2,0:T(8,128)(2,1)S(1)}, bf16[1,2,1,256,640]{4,3,1,2,0:T(8,128)(2,1)}, u32[]{:S(2)}, u32[]{:S(2)}) %collective-permute-start.16) | collective-permute-done | bytes 655392 | tf_op jit(solution)/shard_map/ppermute | solution.py:331
  220.7 15.0 %collective-permute-done.18 = bf16[1,2,1,256,640]{4,3,1,2,0:T(8,128)(2,1)} collective-permute-done((bf16[1,2,1,256,640]{4,3,1,2,0:T(8,128)(2,1)}, bf16[1,2,1,256,640]{4,3,1,2,0:T(8,128)(2,1)}, u32[]{:S(2)}, u32[]{:S(2)}) %collective-permute-start.18) | collective-permute-done | bytes 655392 | tf_op jit(solution)/shard_map/ppermute | solution.py:331
  235.8 19.2 %ffn_mid.1 = (bf16[1024,640]{1,0:T(8,128)(2,1)}, bf16[1024,640]{1,0:T(8,128)(2,1)}, bf16[1024,640]{1,0:T(8,128)(2,1)}, bf16[1024,2048]{1,0:T(8,128)(2,1)}) custom-call(s32[8]{0:T(128)S(1)} %stack.35.offsets, bf16[1024,2048]{1,0:T(8,128)(2,1)} %all-gather.9.cloned.1.call-done.mid_ref.rows_ref, f32[1024,640]{1,0:T(8,128)} %copy-done.23, ...), custom_call_target="tpu_custom_call" | custom-call | flops 10737418240 | bytes 10747904 | tf_op jit(solution)/shard_map/ffn_mid/pallas_call | solution.py:303
  260.4 6.6 %down_grad.1 = bf16[2048,640]{1,0:T(8,128)(2,1)} custom-call(bf16[1024,2048]{1,0:T(8,128)(2,1)S(1)} %copy-done.4, bf16[1024,640]{1,0:T(8,128)(2,1)S(1)} %copy-done.24), custom_call_target="tpu_custom_call" | custom-call | flops 2684354560 | bytes 8126464 | tf_op jit(solution)/shard_map/down_grad/pallas_call | solution.py:268
  267.4 4.5 fusion.2
  271.9 5.8 %ffn_out.1 = bf16[1024,2048]{1,0:T(8,128)(2,1)} custom-call(s32[8]{0:T(128)S(1)} %stack.35.offsets, bf16[1024,640]{1,0:T(8,128)(2,1)S(1)} %copy-done.24, bf16[512,640]{1,0:T(8,128)(2,1)S(1)} %bitcast.186, bf16[512,640]{1,0:T(8,128)(2,1)S(1)} %bitcast.203, bf16[512,640]{1,0:T(8,128)(2,1)S(1)} %bitcast.205, bf16[512,640]{1,0:T(8,128)(2,1)S(1)} %bitcast.207), custom_call_target="tpu_custom_call" | custom-call | flops 2684354560 | bytes 3932160 | tf_op jit(solution)/shard_map/ffn_out/pallas_call | solution.py:303
  286.5 10.3 %collective-permute-done.20 = bf16[128,2048]{1,0:T(8,128)(2,1)S(1)} collective-permute-done((bf16[128,2048]{1,0:T(8,128)(2,1)S(1)}, bf16[128,2048]{1,0:T(8,128)(2,1)S(1)}, u32[]{:S(2)}, u32[]{:S(2)}) %collective-permute-start.20) | collective-permute-done | bytes 524320 | tf_op jit(solution)/shard_map/ppermute | solution.py:415
  296.8 13.9 %collective-permute-done.21 = bf16[128,2048]{1,0:T(8,128)(2,1)} collective-permute-done((bf16[128,2048]{1,0:T(8,128)(2,1)S(1)}, bf16[128,2048]{1,0:T(8,128)(2,1)}, u32[]{:S(2)}, u32[]{:S(2)}) %collective-permute-start.21) | collective-permute-done | bytes 524320 | tf_op jit(solution)/shard_map/ppermute | solution.py:415
  310.7 14.4 %collective-permute-done.22 = bf16[128,2048]{1,0:T(8,128)(2,1)} collective-permute-done((bf16[128,2048]{1,0:T(8,128)(2,1)S(1)}, bf16[128,2048]{1,0:T(8,128)(2,1)}, u32[]{:S(2)}, u32[]{:S(2)}) %collective-permute-start.22) | collective-permute-done | bytes 524320 | tf_op jit(solution)/shard_map/ppermute | solution.py:415
  326.9 4.9 fusion.1
  334.7 6.2 %attend_backward.1 = (f32[128,1280]{1,0:T(8,128)S(1)}, f32[128,640]{1,0:T(8,128)S(1)}, bf16[128,640]{1,0:T(8,128)(2,1)S(1)}, bf16[128,640]{1,0:T(8,128)(2,1)S(1)...) custom-call(s32[1,512]{1,0:T(1,128)S(1)} %bitcast.197, bf16[128,1280]{1,0:T(8,128)(2,1)S(1)} %copy-done.12, ...), custom_call_target="tpu_custom_call" | custom-call | flops 1048576000 | bytes 5120000 | tf_op jit(solution)/shard_map/attend_backward/pallas_call | solution.py:613
  346.5 6.7 %gate_grad.1 = bf16[2048,640]{1,0:T(8,128)(2,1)} custom-call(bf16[1024,2048]{1,0:T(8,128)(2,1)S(1)} %copy-done.2, bf16[1024,640]{1,0:T(8,128)(2,1)S(1)} %copy-done.26), custom_call_target="tpu_custom_call" | custom-call | flops 2684354560 | bytes 8126464 | tf_op jit(solution)/shard_map/gate_grad/pallas_call | solution.py:268
  356.0 11.2 %collective-permute-done.27.refs_3_ = bf16[128,640]{1,0:T(8,128)(2,1)S(1)} collective-permute-done((bf16[128,640]{1,0:T(8,128)(2,1)S(1)}, bf16[128,640]{1,0:T(8,128)(2,1)S(1)}, u32[]{:S(2)}, u32[]{:S(2)}) %collective-permute-start.27) | collective-permute-done | bytes 163872 | tf_op jit(solution)/shard_map/ppermute | solution.py:336
  367.2 7.2 %heads_backward.1 = (bf16[8,128,256]{2,1,0:T(8,128)(2,1)}, f32[1,128]{1,0:T(1,128)S(1)}) custom-call(bf16[8,128,256]{2,1,0:T(8,128)(2,1)S(1)} %all-to-all-done.2.qkv_ref, f32[128,64]{1,0:T(8,128)S(1)} %get-tuple-element.229.cos_ref, f32[128,64]{1,0:T(8,128)S(1)} %get-tuple-element.228.sin_ref, f32[1,64]{1,0:T(1,128)S(1)} %bitcast.199, ...), custom_call_target="tpu_custom_call" | custom-call | flops 7372800 | bytes 3932160 | tf_op jit(solution)/shard_map/heads_backward/pallas_call | solution.py:630
  381.4 6.6 %up_grad.1 = bf16[2048,640]{1,0:T(8,128)(2,1)} custom-call(bf16[1024,2048]{1,0:T(8,128)(2,1)S(1)} %copy-done.3, bf16[1024,640]{1,0:T(8,128)(2,1)S(1)} %copy-done.25), custom_call_target="tpu_custom_call" | custom-call | flops 2684354560 | bytes 8126464 | tf_op jit(solution)/shard_map/up_grad/pallas_call | solution.py:268
  388.0 4.4 all-to-all-done.5
  394.6 3.8 collective-permute-done.28
  409.7 6.9 %collective-permute-done.29 = bf16[128,2048]{1,0:T(8,128)(2,1)} collective-permute-done((bf16[128,2048]{1,0:T(8,128)(2,1)}, bf16[128,2048]{1,0:T(8,128)(2,1)}, u32[]{:S(2)}, u32[]{:S(2)}) %collective-permute-start.29) | collective-permute-done | bytes 524320 | tf_op jit(solution)/shard_map/ppermute | solution.py:415
  416.6 6.8 %collective-permute-done.30 = bf16[128,2048]{1,0:T(8,128)(2,1)} collective-permute-done((bf16[128,2048]{1,0:T(8,128)(2,1)S(1)}, bf16[128,2048]{1,0:T(8,128)(2,1)}, u32[]{:S(2)}, u32[]{:S(2)}) %collective-permute-start.30) | collective-permute-done | bytes 524320 | tf_op jit(solution)/shard_map/ppermute | solution.py:415
  423.4 12.7 %collective-permute-done.31 = bf16[128,2048]{1,0:T(8,128)(2,1)} collective-permute-done((bf16[128,2048]{1,0:T(8,128)(2,1)S(1)}, bf16[128,2048]{1,0:T(8,128)(2,1)}, u32[]{:S(2)}, u32[]{:S(2)}) %collective-permute-start.31) | collective-permute-done | bytes 524320 | tf_op jit(solution)/shard_map/ppermute | solution.py:415
  438.0 4.5 all-to-all-done.6
  453.3 4.4 all-to-all-start.8
  463.6 4.8 collective-permute-done.33
  472.0 17.0 %collective-permute-done.34 = bf16[2,2,256,256]{3,2,1,0:T(8,128)(2,1)S(1)} collective-permute-done((bf16[2,2,256,256]{3,2,1,0:T(8,128)(2,1)S(1)}, bf16[2,2,256,256]{3,2,1,0:T(8,128)(2,1)S(1)}, u32[]{:S(2)}, u32[]{:S(2)}) %collective-permute-start.34) | collective-permute-done | bytes 524320 | tf_op jit(solution)/shard_map/ppermute | solution.py:331
  489.1 6.0 %collective-permute-start.35 = (bf16[2,256,256]{2,1,0:T(8,128)(2,1)S(1)}, bf16[2,256,256]{2,1,0:T(8,128)(2,1)S(1)}, u32[]{:S(2)}, u32[]{:S(2)}) collective-permute-start(bf16[2,256,256]{2,1,0:T(8,128)(2,1)S(1)} %fusion.22), channel_id=1, source_target_pairs={{0,4},{4,0},{1,5},{5,1},{2,6},{6,2},{3,7},{7,3},{8,12},{12,8},{9,1... | collective-permute-start | bytes 786440 | tf_op jit(solution)/shard_map/ppermute | solution.py:331
  497.9 8.2 %collective-permute-done.35 = bf16[2,256,256]{2,1,0:T(8,128)(2,1)S(1)} collective-permute-done((bf16[2,256,256]{2,1,0:T(8,128)(2,1)S(1)}, bf16[2,256,256]{2,1,0:T(8,128)(2,1)S(1)}, u32[]{:S(2)}, u32[]{:S(2)}) %collective-permute-start.35) | collective-permute-done | bytes 262176 | tf_op jit(solution)/shard_map/ppermute | solution.py:331
  516.1 4.8 all-to-all-start.7
  (291 shorter events, 158.7 us)
Async XLA Ops:
  7.2 51.4 %all-gather.7.cloned.1.call-start = ((), (), s32[]{:S(2)}) async-start(), calls=%async_computation.12 | async-start | bytes 4718592 | tf_op jit(solution)/shard_map/all_gather | solution.py:494
  23.3 27.0 %collective-permute-start = (bf16[1,2,1,256,256]{4,3,1,2,0:T(8,128)(2,1)S(1)}, bf16[1,2,1,256,256]{4,3,1,2,0:T(8,128)(2,1)S(1)}, u32[]{:S(2)}, u32[]{:S(2)}) collective-permute-start(bf16[1,2,1,256,256]{4,3,1,2,0:T(8,128)(2,1)S(1)} %bitcast.239), channel_id=1, source_target_pairs={{0,16},{16,0},{1,17},{17,1},{2,18},{18,2},{3,19},{19,3},{4,20},{20... | collective-permute-start | bytes 786440 | tf_op jit(solution)/shard_map/ppermute | solution.py:331
  24.8 24.3 %collective-permute-start.1 = (bf16[1,2,1,256,256]{4,3,1,2,0:T(8,128)(2,1)S(1)}, bf16[1,2,1,256,256]{4,3,1,2,0:T(8,128)(2,1)S(1)}, u32[]{:S(2)}, u32[]{:S(2)}) collective-permute-start(bf16[1,2,1,256,256]{4,3,1,2,0:T(8,128)(2,1)S(1)} %bitcast.240), channel_id=1, source_target_pairs={{0,4},{4,0},{1,5},{5,1},{2,6},{6,2},{3,7},{7,3},{8,12},{12,8},{9,1... | collective-permute-start | bytes 786440 | tf_op jit(solution)/shard_map/ppermute | solution.py:331
  27.4 19.8 %collective-permute-start.3 = (bf16[1,1,64,1280]{3,2,1,0:T(8,128)(2,1)S(1)}, bf16[1,1,64,1280]{3,2,1,0:T(8,128)(2,1)}, u32[]{:S(2)}, u32[]{:S(2)}) collective-permute-start(bf16[1,1,64,1280]{3,2,1,0:T(8,128)(2,1)S(1)} %bitcast.254), channel_id=1, source_target_pairs={{0,16},{16,0},{1,17},{17,1},{2,18},{18,2},{3,19},{19,3},{4,20},{20... | collective-permute-start | bytes 491528 | tf_op jit(solution)/shard_map/ppermute | solution.py:331
  27.9 18.4 %collective-permute-start.4 = (bf16[1,1,64,1280]{3,2,1,0:T(8,128)(2,1)S(1)}, bf16[1,1,64,1280]{3,2,1,0:T(8,128)(2,1)}, u32[]{:S(2)}, u32[]{:S(2)}) collective-permute-start(bf16[1,1,64,1280]{3,2,1,0:T(8,128)(2,1)S(1)} %bitcast.255), channel_id=1, source_target_pairs={{0,4},{4,0},{1,5},{5,1},{2,6},{6,2},{3,7},{7,3},{8,12},{12,8},{9,1... | collective-permute-start | bytes 491528 | tf_op jit(solution)/shard_map/ppermute | solution.py:331
  29.3 28.3 %all-to-all-start.1 = ((bf16[8,64,640]{2,1,0:T(8,128)(2,1)}), bf16[8,64,640]{2,1,0:T(8,128)(2,1)S(1)}, u32[]{:S(2)}, u32[]{:S(2)}) async-start(bf16[8,64,640]{2,1,0:T(8,128)(2,1)} %copy.77), calls=%async_computation.1 | async-start | bytes 1310720 | tf_op jit(solution)/shard_map/all_to_all | solution.py:347
  32.8 103.3 %all-gather.15.cloned.1.call-start = ((), (), s32[]{:S(2)}) async-start(), calls=%async_computation.19 | async-start | bytes 5898240 | tf_op jit(solution)/shard_map/all_gather | solution.py:510
  62.9 29.5 %all-to-all-start.2 = ((bf16[8,128,256]{2,1,0:T(8,128)(2,1)}), bf16[8,128,256]{2,1,0:T(8,128)(2,1)S(1)}, u32[]{:S(2)}, u32[]{:S(2)}) async-start(bf16[8,128,256]{2,1,0:T(8,128)(2,1)} %bitcast.11), calls=%async_computation.2 | async-start | bytes 1048576 | tf_op jit(solution)/shard_map/all_to_all | solution.py:518
  66.4 105.7 %all-gather.11.cloned.1.call-start = ((), (), s32[]{:S(2)}) async-start(), calls=%async_computation.14 | async-start | bytes 4718592 | tf_op jit(solution)/shard_map/all_gather | solution.py:544
  66.5 17.0 %collective-permute-start.6 = (bf16[1,2,1,256,640]{4,3,1,2,0:T(8,128)(2,1)S(1)}, bf16[1,2,1,256,640]{4,3,1,2,0:T(8,128)(2,1)S(1)}, u32[]{:S(2)}, u32[]{:S(2)}) collective-permute-start(bf16[1,2,1,256,640]{4,3,1,2,0:T(8,128)(2,1)S(1)} %bitcast.183), channel_id=1, source_target_pairs={{0,16},{16,0},{1,17},{17,1},{2,18},{18,2},{3,19},{19,3},{4,20},{20... | collective-permute-start | bytes 1966088 | tf_op jit(solution)/shard_map/ppermute | solution.py:331
  68.0 40.9 %collective-permute-start.11 = (bf16[1,2,1,256,640]{4,3,1,2,0:T(8,128)(2,1)S(1)}, bf16[1,2,1,256,640]{4,3,1,2,0:T(8,128)(2,1)S(1)}, u32[]{:S(2)}, u32[]{:S(2)}) collective-permute-start(bf16[1,2,1,256,640]{4,3,1,2,0:T(8,128)(2,1)S(1)} %bitcast.184), channel_id=1, source_target_pairs={{0,4},{4,0},{1,5},{5,1},{2,6},{6,2},{3,7},{7,3},{8,12},{12,8},{9,1... | collective-permute-start | bytes 1966088 | tf_op jit(solution)/shard_map/ppermute | solution.py:331
  102.2 11.9 %collective-permute-start.8 = (bf16[128,640]{1,0:T(8,128)(2,1)S(1)}, bf16[128,640]{1,0:T(8,128)(2,1)S(1)}, u32[]{:S(2)}, u32[]{:S(2)}) collective-permute-start(bf16[128,640]{1,0:T(8,128)(2,1)S(1)} %get-tuple-element.121.refs_0_), channel_id=1, source_target_pairs={{0,2},{1,3},{2,4},{3,5},{4,6},{5,7},{8,10},{9,11},{10,12},{11,13},... | collective-permute-start | bytes 491528 | tf_op jit(solution)/shard_map/ppermute | solution.py:336
  106.2 12.6 %collective-permute-start.9 = (bf16[128,640]{1,0:T(8,128)(2,1)S(1)}, bf16[128,640]{1,0:T(8,128)(2,1)S(1)}, u32[]{:S(2)}, u32[]{:S(2)}) collective-permute-start(bf16[128,640]{1,0:T(8,128)(2,1)S(1)} %get-tuple-element.121.refs_0_), channel_id=1, source_target_pairs={{0,3},{1,4},{2,5},{3,6},{4,7},{8,11},{9,12},{10,13},{11,14},{12,15... | collective-permute-start | bytes 491528 | tf_op jit(solution)/shard_map/ppermute | solution.py:336
  121.6 20.1 %all-to-all-start.3 = ((bf16[8,64,640]{2,1,0:T(8,128)(2,1)}), bf16[8,64,640]{2,1,0:T(8,128)(2,1)S(1)}, u32[]{:S(2)}, u32[]{:S(2)}) async-start(bf16[8,64,640]{2,1,0:T(8,128)(2,1)} %copy.79), calls=%async_computation.3 | async-start | bytes 1310720 | tf_op jit(solution)/shard_map/all_to_all | solution.py:347
  127.9 92.0 %all-gather.9.cloned.1.call-start = ((), (), s32[]{:S(2)}) async-start(), calls=%async_computation.13 | async-start | bytes 4718592 | tf_op jit(solution)/shard_map/all_gather | solution.py:564
  149.2 38.4 %all-to-all-start.4 = ((bf16[8,64,640]{2,1,0:T(8,128)(2,1)}), bf16[8,64,640]{2,1,0:T(8,128)(2,1)S(1)}, u32[]{:S(2)}, u32[]{:S(2)}) async-start(bf16[8,64,640]{2,1,0:T(8,128)(2,1)} %copy.80), calls=%async_computation.4 | async-start | bytes 1310720 | tf_op jit(solution)/shard_map/all_to_all | solution.py:347
  153.4 101.6 %all-gather.13.cloned.1.call-start = ((), (), s32[]{:S(2)}) async-start(), calls=%async_computation.15 | async-start | bytes 2949120 | tf_op jit(solution)/shard_map/all_gather | solution.py:579
  153.5 17.8 %collective-permute-start.12 = (bf16[1,2,1,256,640]{4,3,1,2,0:T(8,128)(2,1)}, bf16[1,2,1,256,640]{4,3,1,2,0:T(8,128)(2,1)S(1)}, u32[]{:S(2)}, u32[]{:S(2)}) collective-permute-start(bf16[1,2,1,256,640]{4,3,1,2,0:T(8,128)(2,1)} %copy-done.5), channel_id=1, source_target_pairs={{0,16},{16,0},{1,17},{17,1},{2,18},{18,2},{3,19},{19,3},{4,20},{20... | collective-permute-start | bytes 1966088 | tf_op jit(solution)/shard_map/ppermute | solution.py:331
  155.0 32.6 %collective-permute-start.13 = (bf16[1,2,1,256,640]{4,3,1,2,0:T(8,128)(2,1)S(1)}, bf16[1,2,1,256,640]{4,3,1,2,0:T(8,128)(2,1)}, u32[]{:S(2)}, u32[]{:S(2)}) collective-permute-start(bf16[1,2,1,256,640]{4,3,1,2,0:T(8,128)(2,1)S(1)} %bitcast.187), channel_id=1, source_target_pairs={{0,4},{4,0},{1,5},{5,1},{2,6},{6,2},{3,7},{7,3},{8,12},{12,8},{9,1... | collective-permute-start | bytes 1966088 | tf_op jit(solution)/shard_map/ppermute | solution.py:331
  160.0 27.6 %collective-permute-start.14 = (bf16[1,2,1,256,640]{4,3,1,2,0:T(8,128)(2,1)S(1)}, bf16[1,2,1,256,640]{4,3,1,2,0:T(8,128)(2,1)}, u32[]{:S(2)}, u32[]{:S(2)}) collective-permute-start(bf16[1,2,1,256,640]{4,3,1,2,0:T(8,128)(2,1)S(1)} %bitcast.188), channel_id=1, source_target_pairs={{0,16},{16,0},{1,17},{17,1},{2,18},{18,2},{3,19},{19,3},{4,20},{20... | collective-permute-start | bytes 1966088 | tf_op jit(solution)/shard_map/ppermute | solution.py:331
  187.6 18.0 %collective-permute-start.15 = (bf16[1,2,1,256,640]{4,3,1,2,0:T(8,128)(2,1)}, bf16[1,2,1,256,640]{4,3,1,2,0:T(8,128)(2,1)}, u32[]{:S(2)}, u32[]{:S(2)}) collective-permute-start(bf16[1,2,1,256,640]{4,3,1,2,0:T(8,128)(2,1)} %collective-permute-done.13), channel_id=1, source_target_pairs={{0,16},{16,0},{1,17},{17,1},{2,18},{18,2},{3,19},{19,3},{4,20},{20... | collective-permute-start | bytes 1966088 | tf_op jit(solution)/shard_map/ppermute | solution.py:331
  187.6 32.3 %collective-permute-start.16 = (bf16[1,2,1,256,640]{4,3,1,2,0:T(8,128)(2,1)S(1)}, bf16[1,2,1,256,640]{4,3,1,2,0:T(8,128)(2,1)}, u32[]{:S(2)}, u32[]{:S(2)}) collective-permute-start(bf16[1,2,1,256,640]{4,3,1,2,0:T(8,128)(2,1)S(1)} %bitcast.190), channel_id=1, source_target_pairs={{0,4},{4,0},{1,5},{5,1},{2,6},{6,2},{3,7},{7,3},{8,12},{12,8},{9,1... | collective-permute-start | bytes 1966088 | tf_op jit(solution)/shard_map/ppermute | solution.py:331
  191.5 28.4 %collective-permute-start.17 = (bf16[1,2,1,256,640]{4,3,1,2,0:T(8,128)(2,1)S(1)}, bf16[1,2,1,256,640]{4,3,1,2,0:T(8,128)(2,1)}, u32[]{:S(2)}, u32[]{:S(2)}) collective-permute-start(bf16[1,2,1,256,640]{4,3,1,2,0:T(8,128)(2,1)S(1)} %bitcast.191), channel_id=1, source_target_pairs={{0,16},{16,0},{1,17},{17,1},{2,18},{18,2},{3,19},{19,3},{4,20},{20... | collective-permute-start | bytes 1966088 | tf_op jit(solution)/shard_map/ppermute | solution.py:331
  219.9 147.2 %reduce-scatter.4.cloned.1.call-start = ((), (), s32[]{:S(2)}) async-start(), calls=%async_computation.16 | async-start | bytes 3276800 | tf_op jit(solution)/shard_map/reduce_scatter | solution.py:590
  220.0 15.8 %collective-permute-start.18 = (bf16[1,2,1,256,640]{4,3,1,2,0:T(8,128)(2,1)}, bf16[1,2,1,256,640]{4,3,1,2,0:T(8,128)(2,1)}, u32[]{:S(2)}, u32[]{:S(2)}) collective-permute-start(bf16[1,2,1,256,640]{4,3,1,2,0:T(8,128)(2,1)} %collective-permute-done.16), channel_id=1, source_target_pairs={{0,16},{16,0},{1,17},{17,1},{2,18},{18,2},{3,19},{19,3},{4,20},{20... | collective-permute-start | bytes 1966088 | tf_op jit(solution)/shard_map/ppermute | solution.py:331
  267.1 175.6 %reduce-scatter.6.cloned.1.call-start = ((), (), s32[]{:S(2)}) async-start(), calls=%async_computation.17 | async-start | bytes 3276800 | tf_op jit(solution)/shard_map/reduce_scatter | solution.py:590
  280.9 46.0 %collective-permute-start.23 = (bf16[512,2048]{1,0:T(8,128)(2,1)}, bf16[512,2048]{1,0:T(8,128)(2,1)}, u32[]{:S(2)}, u32[]{:S(2)}) collective-permute-start(bf16[512,2048]{1,0:T(8,128)(2,1)} %dynamic-slice_bitcast_fusion.1), channel_id=1, source_target_pairs={{0,8},{8,0},{1,9},{9,1},{2,10},{10,2},{3,11},{11,3},{4,12},{12,4},... | collective-permute-start | bytes 6291464 | tf_op jit(solution)/shard_map/ppermute | solution.py:331
  282.9 13.9 %collective-permute-start.20 = (bf16[128,2048]{1,0:T(8,128)(2,1)S(1)}, bf16[128,2048]{1,0:T(8,128)(2,1)S(1)}, u32[]{:S(2)}, u32[]{:S(2)}) collective-permute-start(bf16[128,2048]{1,0:T(8,128)(2,1)S(1)} %get-tuple-element.221), channel_id=1, source_target_pairs={{0,1},{1,0},{2,3},{3,2},{4,5},{5,4},{6,7},{7,6},{8,9},{9,8},{10,11... | collective-permute-start | bytes 1572872 | tf_op jit(solution)/shard_map/ppermute | solution.py:415
  284.0 26.7 %collective-permute-start.21 = (bf16[128,2048]{1,0:T(8,128)(2,1)S(1)}, bf16[128,2048]{1,0:T(8,128)(2,1)}, u32[]{:S(2)}, u32[]{:S(2)}) collective-permute-start(bf16[128,2048]{1,0:T(8,128)(2,1)S(1)} %get-tuple-element.223), channel_id=1, source_target_pairs={{0,2},{1,3},{2,0},{3,1},{4,6},{5,7},{6,4},{7,5},{8,10},{9,11},{10,... | collective-permute-start | bytes 1572872 | tf_op jit(solution)/shard_map/ppermute | solution.py:415
  285.5 39.5 %collective-permute-start.22 = (bf16[128,2048]{1,0:T(8,128)(2,1)S(1)}, bf16[128,2048]{1,0:T(8,128)(2,1)}, u32[]{:S(2)}, u32[]{:S(2)}) collective-permute-start(bf16[128,2048]{1,0:T(8,128)(2,1)S(1)} %get-tuple-element.222), channel_id=1, source_target_pairs={{0,3},{1,2},{2,1},{3,0},{4,7},{5,6},{6,5},{7,4},{8,11},{9,10},{10,... | collective-permute-start | bytes 1572872 | tf_op jit(solution)/shard_map/ppermute | solution.py:415
  340.9 12.3 %collective-permute-start.24 = (bf16[128,640]{1,0:T(8,128)(2,1)S(1)}, bf16[128,640]{1,0:T(8,128)(2,1)S(1)}, u32[]{:S(2)}, u32[]{:S(2)}) collective-permute-start(bf16[128,640]{1,0:T(8,128)(2,1)S(1)} %get-tuple-element.174), channel_id=1, source_target_pairs={{1,0},{2,1},{3,2},{4,3},{5,4},{6,5},{7,6},{9,8},{10,9},{11,10},{12... | collective-permute-start | bytes 491528 | tf_op jit(solution)/shard_map/ppermute | solution.py:336
  343.5 12.5 %collective-permute-start.26 = (bf16[128,640]{1,0:T(8,128)(2,1)S(1)}, bf16[128,640]{1,0:T(8,128)(2,1)S(1)}, u32[]{:S(2)}, u32[]{:S(2)}) collective-permute-start(bf16[128,640]{1,0:T(8,128)(2,1)S(1)} %get-tuple-element.176), channel_id=1, source_target_pairs={{3,0},{4,1},{5,2},{6,3},{7,4},{11,8},{12,9},{13,10},{14,11},{15,12... | collective-permute-start | bytes 491528 | tf_op jit(solution)/shard_map/ppermute | solution.py:336
  344.8 22.3 %collective-permute-start.27 = (bf16[128,640]{1,0:T(8,128)(2,1)S(1)}, bf16[128,640]{1,0:T(8,128)(2,1)S(1)}, u32[]{:S(2)}, u32[]{:S(2)}) collective-permute-start(bf16[128,640]{1,0:T(8,128)(2,1)S(1)} %get-tuple-element.177), channel_id=1, source_target_pairs={{4,0},{5,1},{6,2},{7,3},{12,8},{13,9},{14,10},{15,11},{20,16},{21,... | collective-permute-start | bytes 491528 | tf_op jit(solution)/shard_map/ppermute | solution.py:336
  374.4 18.1 %all-to-all-start.5 = ((bf16[8,128,256]{2,1,0:T(8,128)(2,1)}), bf16[8,128,256]{2,1,0:T(8,128)(2,1)S(1)}, u32[]{:S(2)}, u32[]{:S(2)}) async-start(bf16[8,128,256]{2,1,0:T(8,128)(2,1)} %get-tuple-element.187), calls=%async_computation.6 | async-start | bytes 1048576 | tf_op jit(solution)/shard_map/all_to_all | solution.py:643
  377.9 128.3 %reduce-scatter.8.cloned.1.call-start = ((), (), s32[]{:S(2)}) async-start(), calls=%async_computation.18 | async-start | bytes 3276800 | tf_op jit(solution)/shard_map/reduce_scatter | solution.py:590
  401.5 15.1 %collective-permute-start.29 = (bf16[128,2048]{1,0:T(8,128)(2,1)}, bf16[128,2048]{1,0:T(8,128)(2,1)}, u32[]{:S(2)}, u32[]{:S(2)}) collective-permute-start(bf16[128,2048]{1,0:T(8,128)(2,1)} %get-tuple-element.218), channel_id=1, source_target_pairs={{0,1},{1,0},{2,3},{3,2},{4,5},{5,4},{6,7},{7,6},{8,9},{9,8},{10,11... | collective-permute-start | bytes 1572872 | tf_op jit(solution)/shard_map/ppermute | solution.py:415
  401.5 21.9 %collective-permute-start.30 = (bf16[128,2048]{1,0:T(8,128)(2,1)S(1)}, bf16[128,2048]{1,0:T(8,128)(2,1)}, u32[]{:S(2)}, u32[]{:S(2)}) collective-permute-start(bf16[128,2048]{1,0:T(8,128)(2,1)S(1)} %get-tuple-element.220), channel_id=1, source_target_pairs={{0,2},{1,3},{2,0},{3,1},{4,6},{5,7},{6,4},{7,5},{8,10},{9,11},{10,... | collective-permute-start | bytes 1572872 | tf_op jit(solution)/shard_map/ppermute | solution.py:415
  401.9 34.3 %collective-permute-start.31 = (bf16[128,2048]{1,0:T(8,128)(2,1)S(1)}, bf16[128,2048]{1,0:T(8,128)(2,1)}, u32[]{:S(2)}, u32[]{:S(2)}) collective-permute-start(bf16[128,2048]{1,0:T(8,128)(2,1)S(1)} %get-tuple-element.219), channel_id=1, source_target_pairs={{0,3},{1,2},{2,1},{3,0},{4,7},{5,6},{6,5},{7,4},{8,11},{9,10},{10,... | collective-permute-start | bytes 1572872 | tf_op jit(solution)/shard_map/ppermute | solution.py:415
  406.2 36.3 %all-to-all-start.6 = ((bf16[8,128,256]{1,2,0:T(8,128)(2,1)}), bf16[8,128,256]{1,2,0:T(8,128)(2,1)S(1)}, u32[]{:S(2)}, u32[]{:S(2)}) async-start(bf16[8,128,256]{1,2,0:T(8,128)(2,1)} %bitcast.63), calls=%async_computation.8 | async-start | bytes 1048576 | tf_op jit(solution)/shard_map/all_to_all | solution.py:434
  445.5 49.6 %collective-permute-start.37 = (bf16[128,2048]{1,0:T(8,128)(2,1)}, bf16[128,2048]{1,0:T(8,128)(2,1)}, u32[]{:S(2)}, u32[]{:S(2)}) collective-permute-start(bf16[128,2048]{1,0:T(8,128)(2,1)} %get-tuple-element.215), channel_id=1, source_target_pairs={{0,1},{1,0},{2,3},{3,2},{4,5},{5,4},{6,7},{7,6},{8,9},{9,8},{10,11... | collective-permute-start | bytes 1572872 | tf_op jit(solution)/shard_map/ppermute | solution.py:415
  446.2 48.9 %collective-permute-start.38 = (bf16[128,2048]{1,0:T(8,128)(2,1)}, bf16[128,2048]{1,0:T(8,128)(2,1)}, u32[]{:S(2)}, u32[]{:S(2)}) collective-permute-start(bf16[128,2048]{1,0:T(8,128)(2,1)} %get-tuple-element.217), channel_id=1, source_target_pairs={{0,2},{1,3},{2,0},{3,1},{4,6},{5,7},{6,4},{7,5},{8,10},{9,11},{10,... | collective-permute-start | bytes 1572872 | tf_op jit(solution)/shard_map/ppermute | solution.py:415
  448.2 46.9 %collective-permute-start.39 = (bf16[128,2048]{1,0:T(8,128)(2,1)}, bf16[128,2048]{1,0:T(8,128)(2,1)}, u32[]{:S(2)}, u32[]{:S(2)}) collective-permute-start(bf16[128,2048]{1,0:T(8,128)(2,1)} %get-tuple-element.216), channel_id=1, source_target_pairs={{0,3},{1,2},{2,1},{3,0},{4,7},{5,6},{6,5},{7,4},{8,11},{9,10},{10,... | collective-permute-start | bytes 1572872 | tf_op jit(solution)/shard_map/ppermute | solution.py:415
  451.3 18.7 %collective-permute-start.36 = (bf16[1,2,64,1280]{3,2,1,0:T(8,128)(2,1)}, bf16[1,2,64,1280]{3,2,1,0:T(8,128)(2,1)}, u32[]{:S(2)}, u32[]{:S(2)}) collective-permute-start(bf16[1,2,64,1280]{3,2,1,0:T(8,128)(2,1)} %dynamic-slice_bitcast_fusion.13), channel_id=1, source_target_pairs={{0,16},{16,0},{1,17},{17,1},{2,18},{18,2},{3,19},{19,3},{4,20},{20... | collective-permute-start | bytes 983048 | tf_op jit(solution)/shard_map/ppermute | solution.py:331
  453.3 62.8 %all-to-all-start.8 = ((bf16[8,64,1280]{2,1,0:T(8,128)(2,1)}), bf16[8,64,1280]{2,1,0:T(8,128)(2,1)}, u32[]{:S(2)}, u32[]{:S(2)}) async-start(bf16[8,64,1280]{2,1,0:T(8,128)(2,1)} %pad_maximum_fusion), calls=%async_computation.11 | async-start | bytes 2621440 | tf_op jit(solution)/shard_map/all_to_all | solution.py:388
  468.3 20.6 %collective-permute-start.34 = (bf16[2,2,256,256]{3,2,1,0:T(8,128)(2,1)S(1)}, bf16[2,2,256,256]{3,2,1,0:T(8,128)(2,1)S(1)}, u32[]{:S(2)}, u32[]{:S(2)}) collective-permute-start(bf16[2,2,256,256]{3,2,1,0:T(8,128)(2,1)S(1)} %dynamic-slice_bitcast_fusion.6), channel_id=1, source_target_pairs={{0,16},{16,0},{1,17},{17,1},{2,18},{18,2},{3,19},{19,3},{4,20},{20... | collective-permute-start | bytes 1572872 | tf_op jit(solution)/shard_map/ppermute | solution.py:331
  489.1 17.0 %collective-permute-start.35 = (bf16[2,256,256]{2,1,0:T(8,128)(2,1)S(1)}, bf16[2,256,256]{2,1,0:T(8,128)(2,1)S(1)}, u32[]{:S(2)}, u32[]{:S(2)}) collective-permute-start(bf16[2,256,256]{2,1,0:T(8,128)(2,1)S(1)} %fusion.22), channel_id=1, source_target_pairs={{0,4},{4,0},{1,5},{5,1},{2,6},{6,2},{3,7},{7,3},{8,12},{12,8},{9,1... | collective-permute-start | bytes 786440 | tf_op jit(solution)/shard_map/ppermute | solution.py:331
  509.3 16.0 %collective-permute-start.40 = (bf16[1,64,1280]{2,1,0:T(8,128)(2,1)}, bf16[1,64,1280]{2,1,0:T(8,128)(2,1)}, u32[]{:S(2)}, u32[]{:S(2)}) collective-permute-start(bf16[1,64,1280]{2,1,0:T(8,128)(2,1)} %fusion.23), channel_id=1, source_target_pairs={{0,4},{4,0},{1,5},{5,1},{2,6},{6,2},{3,7},{7,3},{8,12},{12,8},{9,1... | collective-permute-start | bytes 491528 | tf_op jit(solution)/shard_map/ppermute | solution.py:331
  516.1 18.4 %all-to-all-start.7 = ((bf16[8,64,896]{2,1,0:T(8,128)(2,1)}), bf16[8,64,896]{2,1,0:T(8,128)(2,1)}, u32[]{:S(2)}, u32[]{:S(2)}) async-start(bf16[8,64,896]{2,1,0:T(8,128)(2,1)} %pad_maximum_fusion.1), calls=%async_computation.10 | async-start | bytes 1835008 | tf_op jit(solution)/shard_map/all_to_all | solution.py:388
  (70 other events, 516.6 us)
Sparse Core Ops, SparseCore 0:
  10.8 47.7 all-gather.6
  60.8 55.6 all-gather.14
  119.6 37.8 all-gather.10
  159.5 45.0 all-gather.8
  220.1 24.1 all-gather.12
  267.2 62.9 reduce-scatter.3
  367.3 56.9 reduce-scatter.5
  427.3 60.4 reduce-scatter.7

commit v4 on v3

--- a/solution.py
+++ b/solution.py
@@ -518,7 +518,8 @@
     joined = lax.all_to_all(
         joined_team.reshape(team, tokens, -1), TEAM, 0, 0, tiled=True
     )
-    joined, down_near = tie(joined, down_near)
+    joined, w_gate, w_up, down_near = tie(joined, w_gate, w_up, down_near)
+    gate_up_block = team_columns([w_gate, w_up])
 
     half = HEAD_DIM // 2
     frequency = 10000.0 ** (-jnp.arange(half, dtype=f32) / half)
@@ -538,9 +539,11 @@
     )(joined, cosine, sine, gq, gk)
 
     kv_blocks = [kv_low] + [shifted(kv_low, step) for step in range(1, back + 1)]
-    kv_blocks, down_far, w_gate, cotangent_in = tie(kv_blocks, down_far, w_gate, cotangent)
-    gate_block = team_columns([w_gate])
-    down_blocks = down_near + sum([exchange(piece, "y") for piece in down_far[1:]], [])
+    kv_blocks, down_far, gate_up_block, cotangent_in = tie(
+        kv_blocks, down_far, gate_up_block, cotangent
+    )
+    gate_block, up_block = gate_up_block[..., :ff], gate_up_block[..., ff:]
+    gate_far = exchange(gate_block, "zh")
     grads_out = lax.all_gather(cotangent_in, TEAM, axis=0, tiled=True)
     tiled_positions = jnp.tile(positions[None, :], (1, GROUP))
     attended, inverse = whole(
@@ -554,9 +557,13 @@
         tokens * 2000 * 10,
     )(tiled_positions, query_low, *kv_blocks)
 
-    attended, out_full, gate_block, w_up = tie(attended, out_full, gate_block, w_up)
-    gate_far, gate_near = exchange(gate_block, "zh"), exchange(gate_block, "y")
-    up_block = team_columns([w_up])
+    gate_near = exchange(gate_block, "y")
+    down_blocks = down_near + sum([exchange(piece, "y") for piece in down_far[1:]], [])
+    attended, out_full, gate_far, up_block, gate_near, down_blocks = tie(
+        attended, out_full, gate_far, up_block, gate_near, down_blocks
+    )
+    up_far, up_near = exchange(up_block, "zh"), exchange(up_block, "y")
+    gate_blocks = gate_near + sum([exchange(piece, "y") for piece in gate_far[1:]], [])
     middle = inputs + dot_nt(attended, out_full)
     scale_mid = row_scale(middle)
     normed_mid = middle * scale_mid
@@ -564,18 +571,12 @@
     mid_team = lax.all_gather(mid_low, TEAM, axis=0, tiled=True)
 
     products = 2 * mid_team.shape[0] * model * ff
-    grads_out, down_blocks, gate_far, gate_near, up_block = tie(
-        grads_out, down_blocks, gate_far, gate_near, up_block
-    )
-    up_far, up_near = exchange(up_block, "zh"), exchange(up_block, "y")
-    gate_blocks = gate_near + sum([exchange(piece, "y") for piece in gate_far[1:]], [])
+    up_blocks = up_near + sum([exchange(piece, "y") for piece in up_far[1:]], [])
     (hidden_grad,) = by_tokens(
         ffn_dz_kernel, offsets, [grads_out], down_blocks, [(ff, f32)], "ffn_dz", products
     )
-    mid_team, hidden_grad, gate_blocks, up_far, up_near, attended_in = tie(
-        mid_team, hidden_grad, gate_blocks, up_far, up_near, attended
-    )
-    up_blocks = up_near + sum([exchange(piece, "y") for piece in up_far[1:]], [])
+    hidden_grad, gate_blocks, up_blocks = tie(hidden_grad, gate_blocks, up_blocks)
+    mid_team, hidden_grad, attended_in = tie(mid_team, hidden_grad, attended)
     attended_team = lax.all_gather(attended_in, TEAM, axis=0, tiled=True)
     hidden, gate_grad, up_grad, mid_part = by_tokens(
         ffn_mid_kernel,

time: 553 us -> 551 us (level)
  waiting for transfers between devices: 246 us -> 254 us
  starting transfers between devices: 106 us -> 98.9 us
    ppermute x27, waiting for transfers between devices: 128 us -> 138 us  [swap(): return lax.ppermute(value, axis, [(i, i ^ k) for i in range(n)])]
    all_to_all x1, waiting for transfers between devices: 8.93 us -> 0.01 us  [local(): lax.all_to_all(joined_team.reshape(team, tokens, -1), TEAM, 0, 0, tiled=T...]
    all_to_all x4 -> x3, starting transfers between devices: 19.3 us -> 13.2 us  [team_columns(): blocks = lax.all_to_all(blocks.transpose(1, 0, 2), TEAM, 0, 0, tiled=True)]
    all_gather x1, waiting for transfers between devices: 0.01 us -> 5.96 us  [local(): attended_team = lax.all_gather(attended_in, TEAM, axis=0, tiled=True)]
    unnamed x119 -> x111, local copies, waits for them, and re-layouts: 19.6 us -> 14.5 us
  transfers between devices with their start and end apart: 61 -> 60, of which waited for: 33 -> 33; matrix products, arithmetic and copies ran while one was open for 14% -> 14% of each run, Pallas kernels for 14% -> 14%
where the time goes in v4:
time: 551 us; the launch traced here: 544 us
  waiting for transfers between devices  254 us (46%)
  starting transfers between devices  98.9 us (18%)
  Pallas kernels  76.5 us (14%)
  local copies, waits for them, and re-layouts  47.1 us (9%)
  other arithmetic  36.3 us (7%)
  matrix products  15.5 us (3%)
  between operations  15.4 us (3%)
    ppermute x27, waiting for transfers between devices, swap(): return lax.ppermute(value, axis, [(i, i ^ k) for i in range(n)])  138 us
    ppermute x9, waiting for transfers between devices, team_chips(): lax.ppermute(block(chip ^ k), CHIPS, [(i, i ^ k) for i in range(chips)])  64.7 us
    ppermute x27, starting transfers between devices, swap(): return lax.ppermute(value, axis, [(i, i ^ k) for i in range(n)])  39.1 us
    pallas_call x3, Pallas kernels, by_tokens(): pl.pallas_call(functools.partial(kernel, lax.axis_size('core')), out_shap...  32.8 us
    ppermute x8, waiting for transfers between devices, shifted(): lax.ppermute(value, SEQ, [(i, i + step) for i in range(n) if 0 <= i + ste...  23.2 us
    pallas_call x3, Pallas kernels, weight_grad(): pl.pallas_call(weight_grad_kernel, out_shape=jax.ShapeDtypeStruct((model,...  19.4 us
    ppermute x8, starting transfers between devices, shifted(): lax.ppermute(value, SEQ, [(i, i + step) for i in range(n) if 0 <= i + ste...  16.1 us
    unnamed x111, local copies, waits for them, and re-layouts  14.5 us
  transfers between devices with their start and end apart: 60, of which 33 were waited for; matrix products, arithmetic and copies ran while one was open for 14% of the time, Pallas kernels for 14%

profile of v4, /device:TPU:0, one launch (start us, length us, event | category | flops | bytes accessed | tf_op | source)
XLA Modules:
  0.0 544.0 jit_solution(13566788037792636341)
XLA Ops:
  11.5 5.2 all-to-all-start
  16.7 6.6 %all-to-all-done = bf16[8,64,256]{2,1,0:T(8,128)(2,1)S(1)} async-done(((bf16[8,64,256]{2,1,0:T(8,128)(2,1)}), bf16[8,64,256]{2,1,0:T(8,128)(2,1)S(1)}, u32[]{:S(2)}, u32[]{:S(2)}) %all-to-all-start) | async-done | bytes 262176 | tf_op jit(solution)/shard_map/all_to_all | solution.py:347
  29.3 3.5 all-to-all-start.1
  33.1 13.3 %collective-permute-done.4 = bf16[1,1,64,1280]{3,2,1,0:T(8,128)(2,1)} collective-permute-done((bf16[1,1,64,1280]{3,2,1,0:T(8,128)(2,1)S(1)}, bf16[1,1,64,1280]{3,2,1,0:T(8,128)(2,1)}, u32[]{:S(2)}, u32[]{:S(2)}) %collective-permute-start.4) | collective-permute-done | bytes 163872 | tf_op jit(solution)/shard_map/ppermute | solution.py:331
  53.6 3.9 collective-permute-done.2
  58.6 4.3 convolution_convert_fusion.4
  68.0 15.5 %collective-permute-done.6 = bf16[1,2,1,256,640]{4,3,1,2,0:T(8,128)(2,1)S(1)} collective-permute-done((bf16[1,2,1,256,640]{4,3,1,2,0:T(8,128)(2,1)S(1)}, bf16[1,2,1,256,640]{4,3,1,2,0:T(8,128)(2,1)S(1)}, u32[]{:S(2)}, u32[]{:S(2)}) %collective-permute-start.6) | collective-permute-done | bytes 655392 | tf_op jit(solution)/shard_map/ppermute | solution.py:331
  86.2 4.4 all-to-all-start.3
  93.9 4.9 heads_forward.1
  101.6 3.7 collective-permute-start.7
  110.1 12.3 %collective-permute-done.11 = bf16[1,2,1,256,640]{4,3,1,2,0:T(8,128)(2,1)} collective-permute-done((bf16[1,2,1,256,640]{4,3,1,2,0:T(8,128)(2,1)S(1)}, bf16[1,2,1,256,640]{4,3,1,2,0:T(8,128)(2,1)}, u32[]{:S(2)}, u32[]{:S(2)}) %collective-permute-start.11) | collective-permute-done | bytes 655392 | tf_op jit(solution)/shard_map/ppermute | solution.py:331
  135.3 8.6 %collective-permute-start.12 = (bf16[1,2,1,256,640]{4,3,1,2,0:T(8,128)(2,1)S(1)}, bf16[1,2,1,256,640]{4,3,1,2,0:T(8,128)(2,1)}, u32[]{:S(2)}, u32[]{:S(2)}) collective-permute-start(bf16[1,2,1,256,640]{4,3,1,2,0:T(8,128)(2,1)S(1)} %get-tuple-element.149), channel_id=1, source_target_pairs={{0,4},{4,0},{1,5},{5,1},{2,6},{6,2},{3,7},{7,3},{8,12},{12,8},{9,1... | collective-permute-start | bytes 1966088 | tf_op jit(solution)/shard_map/ppermute | solution.py:331
  146.0 6.1 %attend_forward.1 = (bf16[128,1280]{1,0:T(8,128)(2,1)}, f32[8,512]{1,0:T(8,128)S(1)}) custom-call(s32[1,512]{1,0:T(1,128)S(1)} %bitcast.189, bf16[128,1280]{1,0:T(8,128)(2,1)S(1)} %copy-done.6, bf16[128,640]{1,0:T(8,128)(2,1)S(1)} %get-tuple-element.124.refs_0_, bf16[128,640]{1,0:T(8,128)(2,1)S(1)} %copy-done.12, bf16[128,640]{1,0:T(8,128)(2,1)S(1)} %copy-done.15, ...), custom_call_target="tpu_custom_call" | custom-call | flops 419430400 | bytes 2560000 | tf_op jit(solution)/shard_map/attend_forward/pallas_call | solution.py:549
  152.1 5.9 %copy.76 = bf16[2,2,2,4,64,1280]{5,4,3,2,1,0:T(8,128)(2,1)} copy(bf16[2,2,2,4,64,1280]{5,4,2,0,3,1:T(8,128)(2,1)} %bitcast.209) | data formatting | bytes 10485760 | tf_op jit(solution)/shard_map/transpose | solution.py:513
  158.0 13.5 %collective-permute-done.12 = bf16[1,2,1,256,640]{4,3,1,2,0:T(8,128)(2,1)} collective-permute-done((bf16[1,2,1,256,640]{4,3,1,2,0:T(8,128)(2,1)S(1)}, bf16[1,2,1,256,640]{4,3,1,2,0:T(8,128)(2,1)}, u32[]{:S(2)}, u32[]{:S(2)}) %collective-permute-start.12) | collective-permute-done | bytes 655392 | tf_op jit(solution)/shard_map/ppermute | solution.py:331
  173.8 4.7 multiply_reduce_fusion.2
  183.0 27.5 %collective-permute-done.17 = bf16[1,2,1,256,640]{4,3,1,2,0:T(8,128)(2,1)} collective-permute-done((bf16[1,2,1,256,640]{4,3,1,2,0:T(8,128)(2,1)S(1)}, bf16[1,2,1,256,640]{4,3,1,2,0:T(8,128)(2,1)}, u32[]{:S(2)}, u32[]{:S(2)}) %collective-permute-start.17) | collective-permute-done | bytes 655392 | tf_op jit(solution)/shard_map/ppermute | solution.py:331
  212.7 6.5 %ffn_dz.1.dz_ref = f32[1024,640]{1,0:T(8,128)S(1)} custom-call(s32[8]{0:T(128)S(1)} %stack.35.offsets, bf16[1024,2048]{1,0:T(8,128)(2,1)} %all-gather.11.cloned.1.call-done.grads_ref.rows_ref, bf16[512,640]{1,0:T(8,128)(2,1)S(1)} %bitcast.184, bf16[512,640]{1,0:T(8,128)(2,1)S(1)} %bitcast.195, bf16[512,640]{1,0:T(8,128)(2,1)} %bitcast.29.refs_2_, ...), custom_call_target="tpu_custom_call" | custom-call | flops 2684354560 | bytes 6815744 | tf_op jit(solution)/shard_map/ffn_dz/pallas_call | solution.py:303
  220.6 4.8 collective-permute-done.18
  228.3 19.1 %ffn_mid.1 = (bf16[1024,640]{1,0:T(8,128)(2,1)}, bf16[1024,640]{1,0:T(8,128)(2,1)}, bf16[1024,640]{1,0:T(8,128)(2,1)}, bf16[1024,2048]{1,0:T(8,128)(2,1)}) custom-call(s32[8]{0:T(128)S(1)} %stack.35.offsets, bf16[1024,2048]{1,0:T(8,128)(2,1)} %all-gather.9.cloned.1.call-done.mid_ref.rows_ref, f32[1024,640]{1,0:T(8,128)} %copy-done.20, ...), custom_call_target="tpu_custom_call" | custom-call | flops 10737418240 | bytes 10747904 | tf_op jit(solution)/shard_map/ffn_mid/pallas_call | solution.py:303
  247.4 6.0 %all-gather.13.cloned.1.call-done = bf16[1024,1280]{1,0:T(8,128)(2,1)} async-done(((bf16[128,1280]{1,0:T(8,128)(2,1)}), bf16[1024,1280]{1,0:T(8,128)(2,1)}) %all-gather.13.cloned.1.call-update) | async-done | bytes 2621456 | tf_op jit(solution)/shard_map/all_gather | solution.py:580
  259.1 6.5 %down_grad.1 = bf16[2048,640]{1,0:T(8,128)(2,1)} custom-call(bf16[1024,2048]{1,0:T(8,128)(2,1)S(1)} %copy-done.4, bf16[1024,640]{1,0:T(8,128)(2,1)S(1)} %copy-done.21), custom_call_target="tpu_custom_call" | custom-call | flops 2684354560 | bytes 8126464 | tf_op jit(solution)/shard_map/down_grad/pallas_call | solution.py:268
  265.9 4.4 fusion.2
  270.4 7.2 %ffn_out.1 = bf16[1024,2048]{1,0:T(8,128)(2,1)} custom-call(s32[8]{0:T(128)S(1)} %stack.35.offsets, bf16[1024,640]{1,0:T(8,128)(2,1)S(1)} %copy-done.21, bf16[512,640]{1,0:T(8,128)(2,1)S(1)} %bitcast.185, bf16[512,640]{1,0:T(8,128)(2,1)S(1)} %bitcast.196, bf16[512,640]{1,0:T(8,128)(2,1)} %bitcast.29.refs_2_, bf16[512,640]{1,0:T(8,128)(2,1)} %bitcast.30.refs_3_), custom_call_target="tpu_custom_call" | custom-call | flops 2684354560 | bytes 3932160 | tf_op jit(solution)/shard_map/ffn_out/pallas_call | solution.py:303
  286.0 10.6 %collective-permute-done.20 = bf16[128,2048]{1,0:T(8,128)(2,1)S(1)} collective-permute-done((bf16[128,2048]{1,0:T(8,128)(2,1)S(1)}, bf16[128,2048]{1,0:T(8,128)(2,1)S(1)}, u32[]{:S(2)}, u32[]{:S(2)}) %collective-permute-start.20) | collective-permute-done | bytes 524320 | tf_op jit(solution)/shard_map/ppermute | solution.py:415
  296.6 11.3 %collective-permute-done.21 = bf16[128,2048]{1,0:T(8,128)(2,1)} collective-permute-done((bf16[128,2048]{1,0:T(8,128)(2,1)S(1)}, bf16[128,2048]{1,0:T(8,128)(2,1)}, u32[]{:S(2)}, u32[]{:S(2)}) %collective-permute-start.21) | collective-permute-done | bytes 524320 | tf_op jit(solution)/shard_map/ppermute | solution.py:415
  307.8 16.4 %collective-permute-done.22 = bf16[128,2048]{1,0:T(8,128)(2,1)} collective-permute-done((bf16[128,2048]{1,0:T(8,128)(2,1)S(1)}, bf16[128,2048]{1,0:T(8,128)(2,1)}, u32[]{:S(2)}, u32[]{:S(2)}) %collective-permute-start.22) | collective-permute-done | bytes 524320 | tf_op jit(solution)/shard_map/ppermute | solution.py:415
  326.1 4.9 fusion.1
  333.8 6.1 %attend_backward.1 = (f32[128,1280]{1,0:T(8,128)S(1)}, f32[128,640]{1,0:T(8,128)S(1)}, bf16[128,640]{1,0:T(8,128)(2,1)S(1)}, bf16[128,640]{1,0:T(8,128)(2,1)S(1)...) custom-call(s32[1,512]{1,0:T(1,128)S(1)} %bitcast.190, bf16[128,1280]{1,0:T(8,128)(2,1)S(1)} %copy-done.7, ...), custom_call_target="tpu_custom_call" | custom-call | flops 1048576000 | bytes 5120000 | tf_op jit(solution)/shard_map/attend_backward/pallas_call | solution.py:614
  345.5 6.5 %gate_grad.1 = bf16[2048,640]{1,0:T(8,128)(2,1)} custom-call(bf16[1024,2048]{1,0:T(8,128)(2,1)S(1)} %copy-done.2, bf16[1024,640]{1,0:T(8,128)(2,1)S(1)} %copy-done.23), custom_call_target="tpu_custom_call" | custom-call | flops 2684354560 | bytes 8126464 | tf_op jit(solution)/shard_map/gate_grad/pallas_call | solution.py:268
  352.0 3.8 collective-permute-done.26.refs_2_
  355.8 8.9 %collective-permute-done.27.refs_3_ = bf16[128,640]{1,0:T(8,128)(2,1)S(1)} collective-permute-done((bf16[128,640]{1,0:T(8,128)(2,1)S(1)}, bf16[128,640]{1,0:T(8,128)(2,1)S(1)}, u32[]{:S(2)}, u32[]{:S(2)}) %collective-permute-start.27) | collective-permute-done | bytes 163872 | tf_op jit(solution)/shard_map/ppermute | solution.py:336
  364.7 7.2 %heads_backward.1 = (bf16[8,128,256]{2,1,0:T(8,128)(2,1)}, f32[1,128]{1,0:T(1,128)S(1)}) custom-call(bf16[8,128,256]{2,1,0:T(8,128)(2,1)S(1)} %all-to-all-done.2.qkv_ref, f32[128,64]{1,0:T(8,128)S(1)} %get-tuple-element.233.cos_ref, f32[128,64]{1,0:T(8,128)S(1)} %get-tuple-element.232.sin_ref, f32[1,64]{1,0:T(1,128)S(1)} %bitcast.192, ...), custom_call_target="tpu_custom_call" | custom-call | flops 7372800 | bytes 3932160 | tf_op jit(solution)/shard_map/heads_backward/pallas_call | solution.py:631
  379.0 6.4 %up_grad.1 = bf16[2048,640]{1,0:T(8,128)(2,1)} custom-call(bf16[1024,2048]{1,0:T(8,128)(2,1)S(1)} %copy-done.3, bf16[1024,640]{1,0:T(8,128)(2,1)S(1)} %copy-done.22), custom_call_target="tpu_custom_call" | custom-call | flops 2684354560 | bytes 8126464 | tf_op jit(solution)/shard_map/up_grad/pallas_call | solution.py:268
  385.4 4.6 all-to-all-done.4
  392.1 3.8 collective-permute-done.28
  406.5 6.7 %collective-permute-done.29 = bf16[128,2048]{1,0:T(8,128)(2,1)} collective-permute-done((bf16[128,2048]{1,0:T(8,128)(2,1)S(1)}, bf16[128,2048]{1,0:T(8,128)(2,1)}, u32[]{:S(2)}, u32[]{:S(2)}) %collective-permute-start.29) | collective-permute-done | bytes 524320 | tf_op jit(solution)/shard_map/ppermute | solution.py:415
  413.2 5.4 collective-permute-done.30
  418.6 14.3 %collective-permute-done.31 = bf16[128,2048]{1,0:T(8,128)(2,1)} collective-permute-done((bf16[128,2048]{1,0:T(8,128)(2,1)S(1)}, bf16[128,2048]{1,0:T(8,128)(2,1)}, u32[]{:S(2)}, u32[]{:S(2)}) %collective-permute-start.31) | collective-permute-done | bytes 524320 | tf_op jit(solution)/shard_map/ppermute | solution.py:415
  450.7 4.4 all-to-all-start.7
  455.2 3.5 convolution_convert_fusion.2
  460.9 4.9 collective-permute-done.33
  467.8 18.6 %collective-permute-done.34 = bf16[2,2,256,256]{3,2,1,0:T(8,128)(2,1)S(1)} collective-permute-done((bf16[2,2,256,256]{3,2,1,0:T(8,128)(2,1)S(1)}, bf16[2,2,256,256]{3,2,1,0:T(8,128)(2,1)S(1)}, u32[]{:S(2)}, u32[]{:S(2)}) %collective-permute-start.34) | collective-permute-done | bytes 524320 | tf_op jit(solution)/shard_map/ppermute | solution.py:331
  486.5 5.7 %collective-permute-start.35 = (bf16[2,256,256]{2,1,0:T(8,128)(2,1)S(1)}, bf16[2,256,256]{2,1,0:T(8,128)(2,1)S(1)}, u32[]{:S(2)}, u32[]{:S(2)}) collective-permute-start(bf16[2,256,256]{2,1,0:T(8,128)(2,1)S(1)} %fusion.22), channel_id=1, source_target_pairs={{0,4},{4,0},{1,5},{5,1},{2,6},{6,2},{3,7},{7,3},{8,12},{12,8},{9,1... | collective-permute-start | bytes 786440 | tf_op jit(solution)/shard_map/ppermute | solution.py:331
  495.0 9.2 %collective-permute-done.35 = bf16[2,256,256]{2,1,0:T(8,128)(2,1)S(1)} collective-permute-done((bf16[2,256,256]{2,1,0:T(8,128)(2,1)S(1)}, bf16[2,256,256]{2,1,0:T(8,128)(2,1)S(1)}, u32[]{:S(2)}, u32[]{:S(2)}) %collective-permute-start.35) | collective-permute-done | bytes 262176 | tf_op jit(solution)/shard_map/ppermute | solution.py:331
  510.9 4.2 collective-permute-done.42
  515.1 4.2 all-to-all-start.6
  529.1 3.7 all-to-all-done.6
  (282 shorter events, 155.0 us)
Async XLA Ops:
  7.2 51.4 %all-gather.7.cloned.1.call-start = ((), (), s32[]{:S(2)}) async-start(), calls=%async_computation.11 | async-start | bytes 4718592 | tf_op jit(solution)/shard_map/all_gather | solution.py:494
  23.3 27.0 %collective-permute-start = (bf16[1,2,1,256,256]{4,3,1,2,0:T(8,128)(2,1)S(1)}, bf16[1,2,1,256,256]{4,3,1,2,0:T(8,128)(2,1)S(1)}, u32[]{:S(2)}, u32[]{:S(2)}) collective-permute-start(bf16[1,2,1,256,256]{4,3,1,2,0:T(8,128)(2,1)S(1)} %bitcast.228), channel_id=1, source_target_pairs={{0,16},{16,0},{1,17},{17,1},{2,18},{18,2},{3,19},{19,3},{4,20},{20... | collective-permute-start | bytes 786440 | tf_op jit(solution)/shard_map/ppermute | solution.py:331
  24.8 24.3 %collective-permute-start.1 = (bf16[1,2,1,256,256]{4,3,1,2,0:T(8,128)(2,1)S(1)}, bf16[1,2,1,256,256]{4,3,1,2,0:T(8,128)(2,1)S(1)}, u32[]{:S(2)}, u32[]{:S(2)}) collective-permute-start(bf16[1,2,1,256,256]{4,3,1,2,0:T(8,128)(2,1)S(1)} %bitcast.229), channel_id=1, source_target_pairs={{0,4},{4,0},{1,5},{5,1},{2,6},{6,2},{3,7},{7,3},{8,12},{12,8},{9,1... | collective-permute-start | bytes 786440 | tf_op jit(solution)/shard_map/ppermute | solution.py:331
  27.4 19.8 %collective-permute-start.3 = (bf16[1,1,64,1280]{3,2,1,0:T(8,128)(2,1)S(1)}, bf16[1,1,64,1280]{3,2,1,0:T(8,128)(2,1)}, u32[]{:S(2)}, u32[]{:S(2)}) collective-permute-start(bf16[1,1,64,1280]{3,2,1,0:T(8,128)(2,1)S(1)} %bitcast.243), channel_id=1, source_target_pairs={{0,16},{16,0},{1,17},{17,1},{2,18},{18,2},{3,19},{19,3},{4,20},{20... | collective-permute-start | bytes 491528 | tf_op jit(solution)/shard_map/ppermute | solution.py:331
  27.9 18.4 %collective-permute-start.4 = (bf16[1,1,64,1280]{3,2,1,0:T(8,128)(2,1)S(1)}, bf16[1,1,64,1280]{3,2,1,0:T(8,128)(2,1)}, u32[]{:S(2)}, u32[]{:S(2)}) collective-permute-start(bf16[1,1,64,1280]{3,2,1,0:T(8,128)(2,1)S(1)} %bitcast.244), channel_id=1, source_target_pairs={{0,4},{4,0},{1,5},{5,1},{2,6},{6,2},{3,7},{7,3},{8,12},{12,8},{9,1... | collective-permute-start | bytes 491528 | tf_op jit(solution)/shard_map/ppermute | solution.py:331
  29.3 28.3 %all-to-all-start.1 = ((bf16[8,64,640]{2,1,0:T(8,128)(2,1)}), bf16[8,64,640]{2,1,0:T(8,128)(2,1)S(1)}, u32[]{:S(2)}, u32[]{:S(2)}) async-start(bf16[8,64,640]{2,1,0:T(8,128)(2,1)} %copy.74), calls=%async_computation.1 | async-start | bytes 1310720 | tf_op jit(solution)/shard_map/all_to_all | solution.py:347
  32.8 119.3 %all-gather.15.cloned.1.call-start = ((), (), s32[]{:S(2)}) async-start(), calls=%async_computation.18 | async-start | bytes 5898240 | tf_op jit(solution)/shard_map/all_gather | solution.py:510
  62.9 20.6 %all-to-all-start.2 = ((bf16[8,128,256]{2,1,0:T(8,128)(2,1)}), bf16[8,128,256]{2,1,0:T(8,128)(2,1)S(1)}, u32[]{:S(2)}, u32[]{:S(2)}) async-start(bf16[8,128,256]{2,1,0:T(8,128)(2,1)} %bitcast.11), calls=%async_computation.2 | async-start | bytes 1048576 | tf_op jit(solution)/shard_map/all_to_all | solution.py:518
  66.4 17.1 %collective-permute-start.6 = (bf16[1,2,1,256,640]{4,3,1,2,0:T(8,128)(2,1)S(1)}, bf16[1,2,1,256,640]{4,3,1,2,0:T(8,128)(2,1)S(1)}, u32[]{:S(2)}, u32[]{:S(2)}) collective-permute-start(bf16[1,2,1,256,640]{4,3,1,2,0:T(8,128)(2,1)S(1)} %bitcast.182), channel_id=1, source_target_pairs={{0,16},{16,0},{1,17},{17,1},{2,18},{18,2},{3,19},{19,3},{4,20},{20... | collective-permute-start | bytes 1966088 | tf_op jit(solution)/shard_map/ppermute | solution.py:331
  86.2 47.3 %all-to-all-start.3 = ((bf16[8,64,1280]{2,1,0:T(8,128)(2,1)}), bf16[8,64,1280]{2,1,0:T(8,128)(2,1)}, u32[]{:S(2)}, u32[]{:S(2)}) async-start(bf16[8,64,1280]{2,1,0:T(8,128)(2,1)} %copy.75), calls=%async_computation.3 | async-start | bytes 2621440 | tf_op jit(solution)/shard_map/all_to_all | solution.py:347
  90.6 122.1 %all-gather.11.cloned.1.call-start = ((), (), s32[]{:S(2)}) async-start(), calls=%async_computation.13 | async-start | bytes 4718592 | tf_op jit(solution)/shard_map/all_gather | solution.py:547
  90.6 31.8 %collective-permute-start.11 = (bf16[1,2,1,256,640]{4,3,1,2,0:T(8,128)(2,1)S(1)}, bf16[1,2,1,256,640]{4,3,1,2,0:T(8,128)(2,1)}, u32[]{:S(2)}, u32[]{:S(2)}) collective-permute-start(bf16[1,2,1,256,640]{4,3,1,2,0:T(8,128)(2,1)S(1)} %bitcast.183), channel_id=1, source_target_pairs={{0,4},{4,0},{1,5},{5,1},{2,6},{6,2},{3,7},{7,3},{8,12},{12,8},{9,1... | collective-permute-start | bytes 1966088 | tf_op jit(solution)/shard_map/ppermute | solution.py:331
  99.5 26.4 %collective-permute-start.10 = (bf16[128,640]{1,0:T(8,128)(2,1)S(1)}, bf16[128,640]{1,0:T(8,128)(2,1)S(1)}, u32[]{:S(2)}, u32[]{:S(2)}) collective-permute-start(bf16[128,640]{1,0:T(8,128)(2,1)S(1)} %get-tuple-element.124.refs_0_), channel_id=1, source_target_pairs={{0,4},{1,5},{2,6},{3,7},{8,12},{9,13},{10,14},{11,15},{16,20},{17,... | collective-permute-start | bytes 491528 | tf_op jit(solution)/shard_map/ppermute | solution.py:336
  101.6 24.3 %collective-permute-start.7 = (bf16[128,640]{1,0:T(8,128)(2,1)S(1)}, bf16[128,640]{1,0:T(8,128)(2,1)S(1)}, u32[]{:S(2)}, u32[]{:S(2)}) collective-permute-start(bf16[128,640]{1,0:T(8,128)(2,1)S(1)} %get-tuple-element.124.refs_0_), channel_id=1, source_target_pairs={{0,1},{1,2},{2,3},{3,4},{4,5},{5,6},{6,7},{8,9},{9,10},{10,11},{11... | collective-permute-start | bytes 491528 | tf_op jit(solution)/shard_map/ppermute | solution.py:336
  105.3 24.1 %collective-permute-start.8 = (bf16[128,640]{1,0:T(8,128)(2,1)S(1)}, bf16[128,640]{1,0:T(8,128)(2,1)S(1)}, u32[]{:S(2)}, u32[]{:S(2)}) collective-permute-start(bf16[128,640]{1,0:T(8,128)(2,1)S(1)} %get-tuple-element.124.refs_0_), channel_id=1, source_target_pairs={{0,2},{1,3},{2,4},{3,5},{4,6},{5,7},{8,10},{9,11},{10,12},{11,13},... | collective-permute-start | bytes 491528 | tf_op jit(solution)/shard_map/ppermute | solution.py:336
  108.7 24.1 %collective-permute-start.9 = (bf16[128,640]{1,0:T(8,128)(2,1)S(1)}, bf16[128,640]{1,0:T(8,128)(2,1)S(1)}, u32[]{:S(2)}, u32[]{:S(2)}) collective-permute-start(bf16[128,640]{1,0:T(8,128)(2,1)S(1)} %get-tuple-element.124.refs_0_), channel_id=1, source_target_pairs={{0,3},{1,4},{2,5},{3,6},{4,7},{8,11},{9,12},{10,13},{11,14},{12,15... | collective-permute-start | bytes 491528 | tf_op jit(solution)/shard_map/ppermute | solution.py:336
  133.6 94.7 %all-gather.9.cloned.1.call-start = ((), (), s32[]{:S(2)}) async-start(), calls=%async_computation.12 | async-start | bytes 4718592 | tf_op jit(solution)/shard_map/all_gather | solution.py:571
  135.3 36.1 %collective-permute-start.12 = (bf16[1,2,1,256,640]{4,3,1,2,0:T(8,128)(2,1)S(1)}, bf16[1,2,1,256,640]{4,3,1,2,0:T(8,128)(2,1)}, u32[]{:S(2)}, u32[]{:S(2)}) collective-permute-start(bf16[1,2,1,256,640]{4,3,1,2,0:T(8,128)(2,1)S(1)} %get-tuple-element.149), channel_id=1, source_target_pairs={{0,4},{4,0},{1,5},{5,1},{2,6},{6,2},{3,7},{7,3},{8,12},{12,8},{9,1... | collective-permute-start | bytes 1966088 | tf_op jit(solution)/shard_map/ppermute | solution.py:331
  143.9 27.5 %collective-permute-start.13 = (bf16[1,2,1,256,640]{4,3,1,2,0:T(8,128)(2,1)S(1)}, bf16[1,2,1,256,640]{4,3,1,2,0:T(8,128)(2,1)}, u32[]{:S(2)}, u32[]{:S(2)}) collective-permute-start(bf16[1,2,1,256,640]{4,3,1,2,0:T(8,128)(2,1)S(1)} %get-tuple-element.149), channel_id=1, source_target_pairs={{0,16},{16,0},{1,17},{17,1},{2,18},{18,2},{3,19},{19,3},{4,20},{20... | collective-permute-start | bytes 1966088 | tf_op jit(solution)/shard_map/ppermute | solution.py:331
  144.9 28.9 %collective-permute-start.14 = (bf16[1,2,1,256,640]{4,3,1,2,0:T(8,128)(2,1)}, bf16[1,2,1,256,640]{4,3,1,2,0:T(8,128)(2,1)}, u32[]{:S(2)}, u32[]{:S(2)}) collective-permute-start(bf16[1,2,1,256,640]{4,3,1,2,0:T(8,128)(2,1)} %collective-permute-done.11), channel_id=1, source_target_pairs={{0,16},{16,0},{1,17},{17,1},{2,18},{18,2},{3,19},{19,3},{4,20},{20... | collective-permute-start | bytes 1966088 | tf_op jit(solution)/shard_map/ppermute | solution.py:331
  180.5 72.9 %all-gather.13.cloned.1.call-start = ((), (), s32[]{:S(2)}) async-start(), calls=%async_computation.14 | async-start | bytes 2949120 | tf_op jit(solution)/shard_map/all_gather | solution.py:580
  180.5 30.0 %collective-permute-start.17 = (bf16[1,2,1,256,640]{4,3,1,2,0:T(8,128)(2,1)S(1)}, bf16[1,2,1,256,640]{4,3,1,2,0:T(8,128)(2,1)}, u32[]{:S(2)}, u32[]{:S(2)}) collective-permute-start(bf16[1,2,1,256,640]{4,3,1,2,0:T(8,128)(2,1)S(1)} %get-tuple-element.153), channel_id=1, source_target_pairs={{0,4},{4,0},{1,5},{5,1},{2,6},{6,2},{3,7},{7,3},{8,12},{12,8},{9,1... | collective-permute-start | bytes 1966088 | tf_op jit(solution)/shard_map/ppermute | solution.py:331
  181.0 39.6 %collective-permute-start.16 = (bf16[1,2,1,256,640]{4,3,1,2,0:T(8,128)(2,1)S(1)}, bf16[1,2,1,256,640]{4,3,1,2,0:T(8,128)(2,1)}, u32[]{:S(2)}, u32[]{:S(2)}) collective-permute-start(bf16[1,2,1,256,640]{4,3,1,2,0:T(8,128)(2,1)S(1)} %get-tuple-element.153), channel_id=1, source_target_pairs={{0,16},{16,0},{1,17},{17,1},{2,18},{18,2},{3,19},{19,3},{4,20},{20... | collective-permute-start | bytes 1966088 | tf_op jit(solution)/shard_map/ppermute | solution.py:331
  182.5 38.1 %collective-permute-start.15 = (bf16[1,2,1,256,640]{4,3,1,2,0:T(8,128)(2,1)}, bf16[1,2,1,256,640]{4,3,1,2,0:T(8,128)(2,1)}, u32[]{:S(2)}, u32[]{:S(2)}) collective-permute-start(bf16[1,2,1,256,640]{4,3,1,2,0:T(8,128)(2,1)} %collective-permute-done.12), channel_id=1, source_target_pairs={{0,16},{16,0},{1,17},{17,1},{2,18},{18,2},{3,19},{19,3},{4,20},{20... | collective-permute-start | bytes 1966088 | tf_op jit(solution)/shard_map/ppermute | solution.py:331
  210.5 14.9 %collective-permute-start.18 = (bf16[1,2,1,256,640]{4,3,1,2,0:T(8,128)(2,1)}, bf16[1,2,1,256,640]{4,3,1,2,0:T(8,128)(2,1)}, u32[]{:S(2)}, u32[]{:S(2)}) collective-permute-start(bf16[1,2,1,256,640]{4,3,1,2,0:T(8,128)(2,1)} %collective-permute-done.17), channel_id=1, source_target_pairs={{0,16},{16,0},{1,17},{17,1},{2,18},{18,2},{3,19},{19,3},{4,20},{20... | collective-permute-start | bytes 1966088 | tf_op jit(solution)/shard_map/ppermute | solution.py:331
  228.3 136.5 %reduce-scatter.4.cloned.1.call-start = ((), (), s32[]{:S(2)}) async-start(), calls=%async_computation.15 | async-start | bytes 3276800 | tf_op jit(solution)/shard_map/reduce_scatter | solution.py:591
  265.7 173.2 %reduce-scatter.6.cloned.1.call-start = ((), (), s32[]{:S(2)}) async-start(), calls=%async_computation.16 | async-start | bytes 3276800 | tf_op jit(solution)/shard_map/reduce_scatter | solution.py:591
  280.7 45.4 %collective-permute-start.23 = (bf16[512,2048]{1,0:T(8,128)(2,1)}, bf16[512,2048]{1,0:T(8,128)(2,1)}, u32[]{:S(2)}, u32[]{:S(2)}) collective-permute-start(bf16[512,2048]{1,0:T(8,128)(2,1)} %dynamic-slice_bitcast_fusion.1), channel_id=1, source_target_pairs={{0,8},{8,0},{1,9},{9,1},{2,10},{10,2},{3,11},{11,3},{4,12},{12,4},... | collective-permute-start | bytes 6291464 | tf_op jit(solution)/shard_map/ppermute | solution.py:331
  282.4 14.1 %collective-permute-start.20 = (bf16[128,2048]{1,0:T(8,128)(2,1)S(1)}, bf16[128,2048]{1,0:T(8,128)(2,1)S(1)}, u32[]{:S(2)}, u32[]{:S(2)}) collective-permute-start(bf16[128,2048]{1,0:T(8,128)(2,1)S(1)} %get-tuple-element.223), channel_id=1, source_target_pairs={{0,1},{1,0},{2,3},{3,2},{4,5},{5,4},{6,7},{7,6},{8,9},{9,8},{10,11... | collective-permute-start | bytes 1572872 | tf_op jit(solution)/shard_map/ppermute | solution.py:415
  283.5 24.3 %collective-permute-start.21 = (bf16[128,2048]{1,0:T(8,128)(2,1)S(1)}, bf16[128,2048]{1,0:T(8,128)(2,1)}, u32[]{:S(2)}, u32[]{:S(2)}) collective-permute-start(bf16[128,2048]{1,0:T(8,128)(2,1)S(1)} %get-tuple-element.225), channel_id=1, source_target_pairs={{0,2},{1,3},{2,0},{3,1},{4,6},{5,7},{6,4},{7,5},{8,10},{9,11},{10,... | collective-permute-start | bytes 1572872 | tf_op jit(solution)/shard_map/ppermute | solution.py:415
  284.4 39.8 %collective-permute-start.22 = (bf16[128,2048]{1,0:T(8,128)(2,1)S(1)}, bf16[128,2048]{1,0:T(8,128)(2,1)}, u32[]{:S(2)}, u32[]{:S(2)}) collective-permute-start(bf16[128,2048]{1,0:T(8,128)(2,1)S(1)} %get-tuple-element.224), channel_id=1, source_target_pairs={{0,3},{1,2},{2,1},{3,0},{4,7},{5,6},{6,5},{7,4},{8,11},{9,10},{10,... | collective-permute-start | bytes 1572872 | tf_op jit(solution)/shard_map/ppermute | solution.py:415
  342.5 13.3 %collective-permute-start.26 = (bf16[128,640]{1,0:T(8,128)(2,1)S(1)}, bf16[128,640]{1,0:T(8,128)(2,1)S(1)}, u32[]{:S(2)}, u32[]{:S(2)}) collective-permute-start(bf16[128,640]{1,0:T(8,128)(2,1)S(1)} %get-tuple-element.178), channel_id=1, source_target_pairs={{3,0},{4,1},{5,2},{6,3},{7,4},{11,8},{12,9},{13,10},{14,11},{15,12... | collective-permute-start | bytes 491528 | tf_op jit(solution)/shard_map/ppermute | solution.py:336
  343.8 20.9 %collective-permute-start.27 = (bf16[128,640]{1,0:T(8,128)(2,1)S(1)}, bf16[128,640]{1,0:T(8,128)(2,1)S(1)}, u32[]{:S(2)}, u32[]{:S(2)}) collective-permute-start(bf16[128,640]{1,0:T(8,128)(2,1)S(1)} %get-tuple-element.179), channel_id=1, source_target_pairs={{4,0},{5,1},{6,2},{7,3},{12,8},{13,9},{14,10},{15,11},{20,16},{21,... | collective-permute-start | bytes 491528 | tf_op jit(solution)/shard_map/ppermute | solution.py:336
  371.9 18.1 %all-to-all-start.4 = ((bf16[8,128,256]{2,1,0:T(8,128)(2,1)}), bf16[8,128,256]{2,1,0:T(8,128)(2,1)S(1)}, u32[]{:S(2)}, u32[]{:S(2)}) async-start(bf16[8,128,256]{2,1,0:T(8,128)(2,1)} %get-tuple-element.189), calls=%async_computation.5 | async-start | bytes 1048576 | tf_op jit(solution)/shard_map/all_to_all | solution.py:644
  375.4 128.9 %reduce-scatter.8.cloned.1.call-start = ((), (), s32[]{:S(2)}) async-start(), calls=%async_computation.17 | async-start | bytes 3276800 | tf_op jit(solution)/shard_map/reduce_scatter | solution.py:591
  398.2 14.9 %collective-permute-start.29 = (bf16[128,2048]{1,0:T(8,128)(2,1)S(1)}, bf16[128,2048]{1,0:T(8,128)(2,1)}, u32[]{:S(2)}, u32[]{:S(2)}) collective-permute-start(bf16[128,2048]{1,0:T(8,128)(2,1)S(1)} %get-tuple-element.220), channel_id=1, source_target_pairs={{0,1},{1,0},{2,3},{3,2},{4,5},{5,4},{6,7},{7,6},{8,9},{9,8},{10,11... | collective-permute-start | bytes 1572872 | tf_op jit(solution)/shard_map/ppermute | solution.py:415
  398.3 20.3 %collective-permute-start.30 = (bf16[128,2048]{1,0:T(8,128)(2,1)S(1)}, bf16[128,2048]{1,0:T(8,128)(2,1)}, u32[]{:S(2)}, u32[]{:S(2)}) collective-permute-start(bf16[128,2048]{1,0:T(8,128)(2,1)S(1)} %get-tuple-element.222), channel_id=1, source_target_pairs={{0,2},{1,3},{2,0},{3,1},{4,6},{5,7},{6,4},{7,5},{8,10},{9,11},{10,... | collective-permute-start | bytes 1572872 | tf_op jit(solution)/shard_map/ppermute | solution.py:415
  398.7 34.3 %collective-permute-start.31 = (bf16[128,2048]{1,0:T(8,128)(2,1)S(1)}, bf16[128,2048]{1,0:T(8,128)(2,1)}, u32[]{:S(2)}, u32[]{:S(2)}) collective-permute-start(bf16[128,2048]{1,0:T(8,128)(2,1)S(1)} %get-tuple-element.221), channel_id=1, source_target_pairs={{0,3},{1,2},{2,1},{3,0},{4,7},{5,6},{6,5},{7,4},{8,11},{9,10},{10,... | collective-permute-start | bytes 1572872 | tf_op jit(solution)/shard_map/ppermute | solution.py:415
  402.9 34.9 %all-to-all-start.5 = ((bf16[8,128,256]{1,2,0:T(8,128)(2,1)}), bf16[8,128,256]{1,2,0:T(8,128)(2,1)S(1)}, u32[]{:S(2)}, u32[]{:S(2)}) async-start(bf16[8,128,256]{1,2,0:T(8,128)(2,1)} %bitcast.61), calls=%async_computation.7 | async-start | bytes 1048576 | tf_op jit(solution)/shard_map/all_to_all | solution.py:434
  441.5 50.6 %collective-permute-start.37 = (bf16[128,2048]{1,0:T(8,128)(2,1)}, bf16[128,2048]{1,0:T(8,128)(2,1)}, u32[]{:S(2)}, u32[]{:S(2)}) collective-permute-start(bf16[128,2048]{1,0:T(8,128)(2,1)} %get-tuple-element.217), channel_id=1, source_target_pairs={{0,1},{1,0},{2,3},{3,2},{4,5},{5,4},{6,7},{7,6},{8,9},{9,8},{10,11... | collective-permute-start | bytes 1572872 | tf_op jit(solution)/shard_map/ppermute | solution.py:415
  441.7 50.5 %collective-permute-start.38 = (bf16[128,2048]{1,0:T(8,128)(2,1)}, bf16[128,2048]{1,0:T(8,128)(2,1)}, u32[]{:S(2)}, u32[]{:S(2)}) collective-permute-start(bf16[128,2048]{1,0:T(8,128)(2,1)} %get-tuple-element.219), channel_id=1, source_target_pairs={{0,2},{1,3},{2,0},{3,1},{4,6},{5,7},{6,4},{7,5},{8,10},{9,11},{10,... | collective-permute-start | bytes 1572872 | tf_op jit(solution)/shard_map/ppermute | solution.py:415
  443.5 48.6 %collective-permute-start.39 = (bf16[128,2048]{1,0:T(8,128)(2,1)S(1)}, bf16[128,2048]{1,0:T(8,128)(2,1)}, u32[]{:S(2)}, u32[]{:S(2)}) collective-permute-start(bf16[128,2048]{1,0:T(8,128)(2,1)S(1)} %get-tuple-element.218), channel_id=1, source_target_pairs={{0,3},{1,2},{2,1},{3,0},{4,7},{5,6},{6,5},{7,4},{8,11},{9,10},{10,... | collective-permute-start | bytes 1572872 | tf_op jit(solution)/shard_map/ppermute | solution.py:415
  446.7 19.2 %collective-permute-start.36 = (bf16[1,2,64,1280]{3,2,1,0:T(8,128)(2,1)}, bf16[1,2,64,1280]{3,2,1,0:T(8,128)(2,1)}, u32[]{:S(2)}, u32[]{:S(2)}) collective-permute-start(bf16[1,2,64,1280]{3,2,1,0:T(8,128)(2,1)} %dynamic-slice_bitcast_fusion.13), channel_id=1, source_target_pairs={{0,16},{16,0},{1,17},{17,1},{2,18},{18,2},{3,19},{19,3},{4,20},{20... | collective-permute-start | bytes 983048 | tf_op jit(solution)/shard_map/ppermute | solution.py:331
  450.7 64.3 %all-to-all-start.7 = ((bf16[8,64,1280]{2,1,0:T(8,128)(2,1)}), bf16[8,64,1280]{2,1,0:T(8,128)(2,1)}, u32[]{:S(2)}, u32[]{:S(2)}) async-start(bf16[8,64,1280]{2,1,0:T(8,128)(2,1)} %pad_maximum_fusion), calls=%async_computation.10 | async-start | bytes 2621440 | tf_op jit(solution)/shard_map/all_to_all | solution.py:388
  465.7 20.6 %collective-permute-start.34 = (bf16[2,2,256,256]{3,2,1,0:T(8,128)(2,1)S(1)}, bf16[2,2,256,256]{3,2,1,0:T(8,128)(2,1)S(1)}, u32[]{:S(2)}, u32[]{:S(2)}) collective-permute-start(bf16[2,2,256,256]{3,2,1,0:T(8,128)(2,1)S(1)} %dynamic-slice_bitcast_fusion.6), channel_id=1, source_target_pairs={{0,16},{16,0},{1,17},{17,1},{2,18},{18,2},{3,19},{19,3},{4,20},{20... | collective-permute-start | bytes 1572872 | tf_op jit(solution)/shard_map/ppermute | solution.py:331
  486.5 17.7 %collective-permute-start.35 = (bf16[2,256,256]{2,1,0:T(8,128)(2,1)S(1)}, bf16[2,256,256]{2,1,0:T(8,128)(2,1)S(1)}, u32[]{:S(2)}, u32[]{:S(2)}) collective-permute-start(bf16[2,256,256]{2,1,0:T(8,128)(2,1)S(1)} %fusion.22), channel_id=1, source_target_pairs={{0,4},{4,0},{1,5},{5,1},{2,6},{6,2},{3,7},{7,3},{8,12},{12,8},{9,1... | collective-permute-start | bytes 786440 | tf_op jit(solution)/shard_map/ppermute | solution.py:331
  506.7 16.9 %collective-permute-start.40 = (bf16[1,64,1280]{2,1,0:T(8,128)(2,1)}, bf16[1,64,1280]{2,1,0:T(8,128)(2,1)}, u32[]{:S(2)}, u32[]{:S(2)}) collective-permute-start(bf16[1,64,1280]{2,1,0:T(8,128)(2,1)} %fusion.23), channel_id=1, source_target_pairs={{0,4},{4,0},{1,5},{5,1},{2,6},{6,2},{3,7},{7,3},{8,12},{12,8},{9,1... | collective-permute-start | bytes 491528 | tf_op jit(solution)/shard_map/ppermute | solution.py:331
  515.1 17.7 %all-to-all-start.6 = ((bf16[8,64,896]{2,1,0:T(8,128)(2,1)}), bf16[8,64,896]{2,1,0:T(8,128)(2,1)}, u32[]{:S(2)}, u32[]{:S(2)}) async-start(bf16[8,64,896]{2,1,0:T(8,128)(2,1)} %pad_maximum_fusion.1), calls=%async_computation.9 | async-start | bytes 1835008 | tf_op jit(solution)/shard_map/all_to_all | solution.py:388
  (65 other events, 469.6 us)
Sparse Core Ops, SparseCore 0:
  10.8 47.7 all-gather.6
  60.8 53.7 all-gather.14
  133.7 49.7 all-gather.10
  185.5 42.6 all-gather.8
  230.2 23.0 all-gather.12
  265.8 61.3 reduce-scatter.3
  364.9 58.1 reduce-scatter.5
  426.0 60.4 reduce-scatter.7

commit v5 on v4

--- a/solution.py
+++ b/solution.py
@@ -559,8 +559,8 @@
 
     gate_near = exchange(gate_block, "y")
     down_blocks = down_near + sum([exchange(piece, "y") for piece in down_far[1:]], [])
-    attended, out_full, gate_far, up_block, gate_near, down_blocks = tie(
-        attended, out_full, gate_far, up_block, gate_near, down_blocks
+    attended, out_full, gate_far, up_block, gate_near = tie(
+        attended, out_full, gate_far, up_block, gate_near
     )
     up_far, up_near = exchange(up_block, "zh"), exchange(up_block, "y")
     gate_blocks = gate_near + sum([exchange(piece, "y") for piece in gate_far[1:]], [])

time: 551 us -> 562 us (1.020)
  waiting for transfers between devices: 254 us -> 261 us
    ppermute x27, waiting for transfers between devices: 138 us -> 147 us  [swap(): return lax.ppermute(value, axis, [(i, i ^ k) for i in range(n)])]
    unnamed x111 -> x117, local copies, waits for them, and re-layouts: 14.5 us -> 16.5 us
  transfers between devices with their start and end apart: 60 -> 60, of which waited for: 33 -> 32; matrix products, arithmetic and copies ran while one was open for 14% -> 14% of each run, Pallas kernels for 14% -> 14%
where the time goes in v5:
time: 562 us; the launch traced here: 554 us
  waiting for transfers between devices  261 us (46%)
  starting transfers between devices  101 us (18%)
  Pallas kernels  76.1 us (14%)
  local copies, waits for them, and re-layouts  49 us (9%)
  other arithmetic  36.4 us (6%)
  matrix products  15.6 us (3%)
  between operations  15.4 us (3%)
    ppermute x27, waiting for transfers between devices, swap(): return lax.ppermute(value, axis, [(i, i ^ k) for i in range(n)])  147 us
    ppermute x9, waiting for transfers between devices, team_chips(): lax.ppermute(block(chip ^ k), CHIPS, [(i, i ^ k) for i in range(chips)])  64.8 us
    ppermute x27, starting transfers between devices, swap(): return lax.ppermute(value, axis, [(i, i ^ k) for i in range(n)])  40.6 us
    pallas_call x3, Pallas kernels, by_tokens(): pl.pallas_call(functools.partial(kernel, lax.axis_size('core')), out_shap...  32.4 us
    ppermute x8, waiting for transfers between devices, shifted(): lax.ppermute(value, SEQ, [(i, i + step) for i in range(n) if 0 <= i + ste...  22.4 us
    pallas_call x3, Pallas kernels, weight_grad(): pl.pallas_call(weight_grad_kernel, out_shape=jax.ShapeDtypeStruct((model,...  19.4 us
    unnamed x117, local copies, waits for them, and re-layouts  16.5 us
    ppermute x8, starting transfers between devices, shifted(): lax.ppermute(value, SEQ, [(i, i + step) for i in range(n) if 0 <= i + ste...  16.1 us
  transfers between devices with their start and end apart: 60, of which 32 were waited for; matrix products, arithmetic and copies ran while one was open for 14% of the time, Pallas kernels for 14%

profile of v5, /device:TPU:0, one launch (start us, length us, event | category | flops | bytes accessed | tf_op | source)
XLA Modules:
  0.0 554.5 jit_solution(1507695165306168623)
XLA Ops:
  11.5 5.2 all-to-all-start
  16.7 6.6 %all-to-all-done = bf16[8,64,256]{2,1,0:T(8,128)(2,1)S(1)} async-done(((bf16[8,64,256]{2,1,0:T(8,128)(2,1)}), bf16[8,64,256]{2,1,0:T(8,128)(2,1)S(1)}, u32[]{:S(2)}, u32[]{:S(2)}) %all-to-all-start) | async-done | bytes 262176 | tf_op jit(solution)/shard_map/all_to_all | solution.py:347
  33.1 13.3 %collective-permute-done.4 = bf16[1,1,64,1280]{3,2,1,0:T(8,128)(2,1)} collective-permute-done((bf16[1,1,64,1280]{3,2,1,0:T(8,128)(2,1)S(1)}, bf16[1,1,64,1280]{3,2,1,0:T(8,128)(2,1)}, u32[]{:S(2)}, u32[]{:S(2)}) %collective-permute-start.4) | collective-permute-done | bytes 163872 | tf_op jit(solution)/shard_map/ppermute | solution.py:331
  53.6 3.9 collective-permute-done.2
  58.6 4.3 convolution_convert_fusion.4
  68.0 15.5 %collective-permute-done.6 = bf16[1,2,1,256,640]{4,3,1,2,0:T(8,128)(2,1)S(1)} collective-permute-done((bf16[1,2,1,256,640]{4,3,1,2,0:T(8,128)(2,1)S(1)}, bf16[1,2,1,256,640]{4,3,1,2,0:T(8,128)(2,1)S(1)}, u32[]{:S(2)}, u32[]{:S(2)}) %collective-permute-start.6) | collective-permute-done | bytes 655392 | tf_op jit(solution)/shard_map/ppermute | solution.py:331
  86.2 4.4 all-to-all-start.3
  93.9 4.9 heads_forward.1
  101.6 3.7 collective-permute-start.7
  110.1 12.3 %collective-permute-done.11 = bf16[1,2,1,256,640]{4,3,1,2,0:T(8,128)(2,1)S(1)} collective-permute-done((bf16[1,2,1,256,640]{4,3,1,2,0:T(8,128)(2,1)S(1)}, bf16[1,2,1,256,640]{4,3,1,2,0:T(8,128)(2,1)S(1)}, u32[]{:S(2)}, u32[]{:S(2)}) %collective-permute-start.11) | collective-permute-done | bytes 655392 | tf_op jit(solution)/shard_map/ppermute | solution.py:331
  135.3 8.6 %collective-permute-start.12 = (bf16[1,2,1,256,640]{4,3,1,2,0:T(8,128)(2,1)S(1)}, bf16[1,2,1,256,640]{4,3,1,2,0:T(8,128)(2,1)}, u32[]{:S(2)}, u32[]{:S(2)}) collective-permute-start(bf16[1,2,1,256,640]{4,3,1,2,0:T(8,128)(2,1)S(1)} %get-tuple-element.141), channel_id=1, source_target_pairs={{0,4},{4,0},{1,5},{5,1},{2,6},{6,2},{3,7},{7,3},{8,12},{12,8},{9,1... | collective-permute-start | bytes 1966088 | tf_op jit(solution)/shard_map/ppermute | solution.py:331
  144.9 6.1 %attend_forward.1 = (bf16[128,1280]{1,0:T(8,128)(2,1)}, f32[8,512]{1,0:T(8,128)S(1)}) custom-call(s32[1,512]{1,0:T(1,128)S(1)} %bitcast.189, bf16[128,1280]{1,0:T(8,128)(2,1)S(1)} %copy-done.9, bf16[128,640]{1,0:T(8,128)(2,1)S(1)} %get-tuple-element.120.refs_0_, bf16[128,640]{1,0:T(8,128)(2,1)S(1)} %copy-done.15, bf16[128,640]{1,0:T(8,128)(2,1)S(1)} %copy-done.18, ...), custom_call_target="tpu_custom_call" | custom-call | flops 419430400 | bytes 2560000 | tf_op jit(solution)/shard_map/attend_forward/pallas_call | solution.py:549
  151.1 5.7 %copy.76 = bf16[2,2,2,4,64,1280]{5,4,3,2,1,0:T(8,128)(2,1)} copy(bf16[2,2,2,4,64,1280]{5,4,2,0,3,1:T(8,128)(2,1)} %bitcast.211) | data formatting | bytes 10485760 | tf_op jit(solution)/shard_map/transpose | solution.py:513
  156.7 14.7 %collective-permute-done.12 = bf16[1,2,1,256,640]{4,3,1,2,0:T(8,128)(2,1)} collective-permute-done((bf16[1,2,1,256,640]{4,3,1,2,0:T(8,128)(2,1)S(1)}, bf16[1,2,1,256,640]{4,3,1,2,0:T(8,128)(2,1)}, u32[]{:S(2)}, u32[]{:S(2)}) %collective-permute-start.12) | collective-permute-done | bytes 655392 | tf_op jit(solution)/shard_map/ppermute | solution.py:331
  171.4 4.7 multiply_reduce_fusion.2
  182.4 25.4 %collective-permute-done.17 = bf16[1,2,1,256,640]{4,3,1,2,0:T(8,128)(2,1)} collective-permute-done((bf16[1,2,1,256,640]{4,3,1,2,0:T(8,128)(2,1)S(1)}, bf16[1,2,1,256,640]{4,3,1,2,0:T(8,128)(2,1)}, u32[]{:S(2)}, u32[]{:S(2)}) %collective-permute-start.17) | collective-permute-done | bytes 655392 | tf_op jit(solution)/shard_map/ppermute | solution.py:331
  212.2 6.3 %ffn_dz.1.dz_ref = f32[1024,640]{1,0:T(8,128)S(1)} custom-call(s32[8]{0:T(128)S(1)} %stack.35.offsets, bf16[1024,2048]{1,0:T(8,128)(2,1)} %all-gather.11.cloned.1.call-done.grads_ref.rows_ref, bf16[512,640]{1,0:T(8,128)(2,1)S(1)} %bitcast.184, bf16[512,640]{1,0:T(8,128)(2,1)S(1)} %bitcast.195, bf16[512,640]{1,0:T(8,128)(2,1)S(1)} %bitcast.197, ...), custom_call_target="tpu_custom_call" | custom-call | flops 2684354560 | bytes 6815744 | tf_op jit(solution)/shard_map/ffn_dz/pallas_call | solution.py:303
  220.1 4.4 collective-permute-done.15
  224.5 12.1 %collective-permute-done.18 = bf16[1,2,1,256,640]{4,3,1,2,0:T(8,128)(2,1)} collective-permute-done((bf16[1,2,1,256,640]{4,3,1,2,0:T(8,128)(2,1)}, bf16[1,2,1,256,640]{4,3,1,2,0:T(8,128)(2,1)}, u32[]{:S(2)}, u32[]{:S(2)}) %collective-permute-start.18) | collective-permute-done | bytes 655392 | tf_op jit(solution)/shard_map/ppermute | solution.py:331
  236.7 19.1 %ffn_mid.1 = (bf16[1024,640]{1,0:T(8,128)(2,1)}, bf16[1024,640]{1,0:T(8,128)(2,1)}, bf16[1024,640]{1,0:T(8,128)(2,1)}, bf16[1024,2048]{1,0:T(8,128)(2,1)}) custom-call(s32[8]{0:T(128)S(1)} %stack.35.offsets, bf16[1024,2048]{1,0:T(8,128)(2,1)} %all-gather.9.cloned.1.call-done.mid_ref.rows_ref, f32[1024,640]{1,0:T(8,128)} %copy-done.23, ...), custom_call_target="tpu_custom_call" | custom-call | flops 10737418240 | bytes 10747904 | tf_op jit(solution)/shard_map/ffn_mid/pallas_call | solution.py:303
  255.8 8.1 %all-gather.13.cloned.1.call-done = bf16[1024,1280]{1,0:T(8,128)(2,1)} async-done(((bf16[128,1280]{1,0:T(8,128)(2,1)}), bf16[1024,1280]{1,0:T(8,128)(2,1)}) %all-gather.13.cloned.1.call-update) | async-done | bytes 2621456 | tf_op jit(solution)/shard_map/all_gather | solution.py:580
  269.7 6.5 %down_grad.1 = bf16[2048,640]{1,0:T(8,128)(2,1)} custom-call(bf16[1024,2048]{1,0:T(8,128)(2,1)S(1)} %copy-done.4, bf16[1024,640]{1,0:T(8,128)(2,1)S(1)} %copy-done.24), custom_call_target="tpu_custom_call" | custom-call | flops 2684354560 | bytes 8126464 | tf_op jit(solution)/shard_map/down_grad/pallas_call | solution.py:268
  276.5 4.5 fusion.2
  281.0 6.9 %ffn_out.1 = bf16[1024,2048]{1,0:T(8,128)(2,1)} custom-call(s32[8]{0:T(128)S(1)} %stack.35.offsets, bf16[1024,640]{1,0:T(8,128)(2,1)S(1)} %copy-done.24, bf16[512,640]{1,0:T(8,128)(2,1)S(1)} %bitcast.185, bf16[512,640]{1,0:T(8,128)(2,1)S(1)} %bitcast.196, bf16[512,640]{1,0:T(8,128)(2,1)S(1)} %bitcast.198, bf16[512,640]{1,0:T(8,128)(2,1)} %bitcast.30.refs_3_), custom_call_target="tpu_custom_call" | custom-call | flops 2684354560 | bytes 3932160 | tf_op jit(solution)/shard_map/ffn_out/pallas_call | solution.py:303
  296.4 10.6 %collective-permute-done.20 = bf16[128,2048]{1,0:T(8,128)(2,1)S(1)} collective-permute-done((bf16[128,2048]{1,0:T(8,128)(2,1)S(1)}, bf16[128,2048]{1,0:T(8,128)(2,1)S(1)}, u32[]{:S(2)}, u32[]{:S(2)}) %collective-permute-start.20) | collective-permute-done | bytes 524320 | tf_op jit(solution)/shard_map/ppermute | solution.py:415
  306.9 11.3 %collective-permute-done.21 = bf16[128,2048]{1,0:T(8,128)(2,1)} collective-permute-done((bf16[128,2048]{1,0:T(8,128)(2,1)S(1)}, bf16[128,2048]{1,0:T(8,128)(2,1)}, u32[]{:S(2)}, u32[]{:S(2)}) %collective-permute-start.21) | collective-permute-done | bytes 524320 | tf_op jit(solution)/shard_map/ppermute | solution.py:415
  318.3 16.5 %collective-permute-done.22 = bf16[128,2048]{1,0:T(8,128)(2,1)} collective-permute-done((bf16[128,2048]{1,0:T(8,128)(2,1)S(1)}, bf16[128,2048]{1,0:T(8,128)(2,1)}, u32[]{:S(2)}, u32[]{:S(2)}) %collective-permute-start.22) | collective-permute-done | bytes 524320 | tf_op jit(solution)/shard_map/ppermute | solution.py:415
  336.7 4.9 fusion.1
  344.4 6.1 %attend_backward.1 = (f32[128,1280]{1,0:T(8,128)S(1)}, f32[128,640]{1,0:T(8,128)S(1)}, bf16[128,640]{1,0:T(8,128)(2,1)S(1)}, bf16[128,640]{1,0:T(8,128)(2,1)S(1)...) custom-call(s32[1,512]{1,0:T(1,128)S(1)} %bitcast.190, bf16[128,1280]{1,0:T(8,128)(2,1)S(1)} %copy-done.10, ...), custom_call_target="tpu_custom_call" | custom-call | flops 1048576000 | bytes 5120000 | tf_op jit(solution)/shard_map/attend_backward/pallas_call | solution.py:614
  356.1 6.5 %gate_grad.1 = bf16[2048,640]{1,0:T(8,128)(2,1)} custom-call(bf16[1024,2048]{1,0:T(8,128)(2,1)S(1)} %copy-done.2, bf16[1024,640]{1,0:T(8,128)(2,1)S(1)} %copy-done.26), custom_call_target="tpu_custom_call" | custom-call | flops 2684354560 | bytes 8126464 | tf_op jit(solution)/shard_map/gate_grad/pallas_call | solution.py:268
  362.6 3.6 collective-permute-done.26.refs_2_
  366.3 9.1 %collective-permute-done.27.refs_3_ = bf16[128,640]{1,0:T(8,128)(2,1)S(1)} collective-permute-done((bf16[128,640]{1,0:T(8,128)(2,1)S(1)}, bf16[128,640]{1,0:T(8,128)(2,1)S(1)}, u32[]{:S(2)}, u32[]{:S(2)}) %collective-permute-start.27) | collective-permute-done | bytes 163872 | tf_op jit(solution)/shard_map/ppermute | solution.py:336
  375.4 7.2 %heads_backward.1 = (bf16[8,128,256]{2,1,0:T(8,128)(2,1)}, f32[1,128]{1,0:T(1,128)S(1)}) custom-call(bf16[8,128,256]{2,1,0:T(8,128)(2,1)S(1)} %all-to-all-done.2.qkv_ref, f32[128,64]{1,0:T(8,128)S(1)} %get-tuple-element.225.cos_ref, f32[128,64]{1,0:T(8,128)S(1)} %get-tuple-element.224.sin_ref, f32[1,64]{1,0:T(1,128)S(1)} %bitcast.192, ...), custom_call_target="tpu_custom_call" | custom-call | flops 7372800 | bytes 3932160 | tf_op jit(solution)/shard_map/heads_backward/pallas_call | solution.py:631
  389.6 6.4 %up_grad.1 = bf16[2048,640]{1,0:T(8,128)(2,1)} custom-call(bf16[1024,2048]{1,0:T(8,128)(2,1)S(1)} %copy-done.3, bf16[1024,640]{1,0:T(8,128)(2,1)S(1)} %copy-done.25), custom_call_target="tpu_custom_call" | custom-call | flops 2684354560 | bytes 8126464 | tf_op jit(solution)/shard_map/up_grad/pallas_call | solution.py:268
  396.0 4.6 all-to-all-done.4
  402.7 3.8 collective-permute-done.28
  417.1 6.7 %collective-permute-done.29 = bf16[128,2048]{1,0:T(8,128)(2,1)} collective-permute-done((bf16[128,2048]{1,0:T(8,128)(2,1)S(1)}, bf16[128,2048]{1,0:T(8,128)(2,1)}, u32[]{:S(2)}, u32[]{:S(2)}) %collective-permute-start.29) | collective-permute-done | bytes 524320 | tf_op jit(solution)/shard_map/ppermute | solution.py:415
  423.8 5.6 %collective-permute-done.30 = bf16[128,2048]{1,0:T(8,128)(2,1)} collective-permute-done((bf16[128,2048]{1,0:T(8,128)(2,1)S(1)}, bf16[128,2048]{1,0:T(8,128)(2,1)}, u32[]{:S(2)}, u32[]{:S(2)}) %collective-permute-start.30) | collective-permute-done | bytes 524320 | tf_op jit(solution)/shard_map/ppermute | solution.py:415
  429.4 14.2 %collective-permute-done.31 = bf16[128,2048]{1,0:T(8,128)(2,1)} collective-permute-done((bf16[128,2048]{1,0:T(8,128)(2,1)S(1)}, bf16[128,2048]{1,0:T(8,128)(2,1)}, u32[]{:S(2)}, u32[]{:S(2)}) %collective-permute-start.31) | collective-permute-done | bytes 524320 | tf_op jit(solution)/shard_map/ppermute | solution.py:415
  461.3 4.5 all-to-all-start.7
  465.8 3.5 convolution_convert_fusion.2
  471.4 4.9 collective-permute-done.33
  478.4 18.6 %collective-permute-done.34 = bf16[2,2,256,256]{3,2,1,0:T(8,128)(2,1)S(1)} collective-permute-done((bf16[2,2,256,256]{3,2,1,0:T(8,128)(2,1)S(1)}, bf16[2,2,256,256]{3,2,1,0:T(8,128)(2,1)S(1)}, u32[]{:S(2)}, u32[]{:S(2)}) %collective-permute-start.34) | collective-permute-done | bytes 524320 | tf_op jit(solution)/shard_map/ppermute | solution.py:331
  497.1 5.6 %collective-permute-start.35 = (bf16[2,256,256]{2,1,0:T(8,128)(2,1)S(1)}, bf16[2,256,256]{2,1,0:T(8,128)(2,1)S(1)}, u32[]{:S(2)}, u32[]{:S(2)}) collective-permute-start(bf16[2,256,256]{2,1,0:T(8,128)(2,1)S(1)} %fusion.22), channel_id=1, source_target_pairs={{0,4},{4,0},{1,5},{5,1},{2,6},{6,2},{3,7},{7,3},{8,12},{12,8},{9,1... | collective-permute-start | bytes 786440 | tf_op jit(solution)/shard_map/ppermute | solution.py:331
  505.5 9.2 %collective-permute-done.35 = bf16[2,256,256]{2,1,0:T(8,128)(2,1)S(1)} collective-permute-done((bf16[2,256,256]{2,1,0:T(8,128)(2,1)S(1)}, bf16[2,256,256]{2,1,0:T(8,128)(2,1)S(1)}, u32[]{:S(2)}, u32[]{:S(2)}) %collective-permute-start.35) | collective-permute-done | bytes 262176 | tf_op jit(solution)/shard_map/ppermute | solution.py:331
  521.4 4.1 collective-permute-done.42
  525.6 4.2 all-to-all-start.6
  539.7 3.7 all-to-all-done.6
  (288 shorter events, 156.4 us)
Async XLA Ops:
  7.2 51.4 %all-gather.7.cloned.1.call-start = ((), (), s32[]{:S(2)}) async-start(), calls=%async_computation.11 | async-start | bytes 4718592 | tf_op jit(solution)/shard_map/all_gather | solution.py:494
  23.3 27.0 %collective-permute-start = (bf16[1,2,1,256,256]{4,3,1,2,0:T(8,128)(2,1)S(1)}, bf16[1,2,1,256,256]{4,3,1,2,0:T(8,128)(2,1)S(1)}, u32[]{:S(2)}, u32[]{:S(2)}) collective-permute-start(bf16[1,2,1,256,256]{4,3,1,2,0:T(8,128)(2,1)S(1)} %bitcast.230), channel_id=1, source_target_pairs={{0,16},{16,0},{1,17},{17,1},{2,18},{18,2},{3,19},{19,3},{4,20},{20... | collective-permute-start | bytes 786440 | tf_op jit(solution)/shard_map/ppermute | solution.py:331
  24.8 24.3 %collective-permute-start.1 = (bf16[1,2,1,256,256]{4,3,1,2,0:T(8,128)(2,1)S(1)}, bf16[1,2,1,256,256]{4,3,1,2,0:T(8,128)(2,1)S(1)}, u32[]{:S(2)}, u32[]{:S(2)}) collective-permute-start(bf16[1,2,1,256,256]{4,3,1,2,0:T(8,128)(2,1)S(1)} %bitcast.231), channel_id=1, source_target_pairs={{0,4},{4,0},{1,5},{5,1},{2,6},{6,2},{3,7},{7,3},{8,12},{12,8},{9,1... | collective-permute-start | bytes 786440 | tf_op jit(solution)/shard_map/ppermute | solution.py:331
  27.4 19.8 %collective-permute-start.3 = (bf16[1,1,64,1280]{3,2,1,0:T(8,128)(2,1)S(1)}, bf16[1,1,64,1280]{3,2,1,0:T(8,128)(2,1)}, u32[]{:S(2)}, u32[]{:S(2)}) collective-permute-start(bf16[1,1,64,1280]{3,2,1,0:T(8,128)(2,1)S(1)} %bitcast.245), channel_id=1, source_target_pairs={{0,16},{16,0},{1,17},{17,1},{2,18},{18,2},{3,19},{19,3},{4,20},{20... | collective-permute-start | bytes 491528 | tf_op jit(solution)/shard_map/ppermute | solution.py:331
  27.9 18.4 %collective-permute-start.4 = (bf16[1,1,64,1280]{3,2,1,0:T(8,128)(2,1)S(1)}, bf16[1,1,64,1280]{3,2,1,0:T(8,128)(2,1)}, u32[]{:S(2)}, u32[]{:S(2)}) collective-permute-start(bf16[1,1,64,1280]{3,2,1,0:T(8,128)(2,1)S(1)} %bitcast.246), channel_id=1, source_target_pairs={{0,4},{4,0},{1,5},{5,1},{2,6},{6,2},{3,7},{7,3},{8,12},{12,8},{9,1... | collective-permute-start | bytes 491528 | tf_op jit(solution)/shard_map/ppermute | solution.py:331
  29.3 28.3 %all-to-all-start.1 = ((bf16[8,64,640]{2,1,0:T(8,128)(2,1)}), bf16[8,64,640]{2,1,0:T(8,128)(2,1)S(1)}, u32[]{:S(2)}, u32[]{:S(2)}) async-start(bf16[8,64,640]{2,1,0:T(8,128)(2,1)} %copy.74), calls=%async_computation.1 | async-start | bytes 1310720 | tf_op jit(solution)/shard_map/all_to_all | solution.py:347
  32.8 118.2 %all-gather.15.cloned.1.call-start = ((), (), s32[]{:S(2)}) async-start(), calls=%async_computation.18 | async-start | bytes 5898240 | tf_op jit(solution)/shard_map/all_gather | solution.py:510
  62.9 20.6 %all-to-all-start.2 = ((bf16[8,128,256]{2,1,0:T(8,128)(2,1)}), bf16[8,128,256]{2,1,0:T(8,128)(2,1)S(1)}, u32[]{:S(2)}, u32[]{:S(2)}) async-start(bf16[8,128,256]{2,1,0:T(8,128)(2,1)} %bitcast.11), calls=%async_computation.2 | async-start | bytes 1048576 | tf_op jit(solution)/shard_map/all_to_all | solution.py:518
  66.4 17.1 %collective-permute-start.6 = (bf16[1,2,1,256,640]{4,3,1,2,0:T(8,128)(2,1)S(1)}, bf16[1,2,1,256,640]{4,3,1,2,0:T(8,128)(2,1)S(1)}, u32[]{:S(2)}, u32[]{:S(2)}) collective-permute-start(bf16[1,2,1,256,640]{4,3,1,2,0:T(8,128)(2,1)S(1)} %bitcast.182), channel_id=1, source_target_pairs={{0,16},{16,0},{1,17},{17,1},{2,18},{18,2},{3,19},{19,3},{4,20},{20... | collective-permute-start | bytes 1966088 | tf_op jit(solution)/shard_map/ppermute | solution.py:331
  86.2 47.4 %all-to-all-start.3 = ((bf16[8,64,1280]{2,1,0:T(8,128)(2,1)}), bf16[8,64,1280]{2,1,0:T(8,128)(2,1)}, u32[]{:S(2)}, u32[]{:S(2)}) async-start(bf16[8,64,1280]{2,1,0:T(8,128)(2,1)} %copy.75), calls=%async_computation.3 | async-start | bytes 2621440 | tf_op jit(solution)/shard_map/all_to_all | solution.py:347
  90.6 120.5 %all-gather.11.cloned.1.call-start = ((), (), s32[]{:S(2)}) async-start(), calls=%async_computation.13 | async-start | bytes 4718592 | tf_op jit(solution)/shard_map/all_gather | solution.py:547
  90.6 31.8 %collective-permute-start.11 = (bf16[1,2,1,256,640]{4,3,1,2,0:T(8,128)(2,1)S(1)}, bf16[1,2,1,256,640]{4,3,1,2,0:T(8,128)(2,1)S(1)}, u32[]{:S(2)}, u32[]{:S(2)}) collective-permute-start(bf16[1,2,1,256,640]{4,3,1,2,0:T(8,128)(2,1)S(1)} %bitcast.183), channel_id=1, source_target_pairs={{0,4},{4,0},{1,5},{5,1},{2,6},{6,2},{3,7},{7,3},{8,12},{12,8},{9,1... | collective-permute-start | bytes 1966088 | tf_op jit(solution)/shard_map/ppermute | solution.py:331
  99.5 26.4 %collective-permute-start.10 = (bf16[128,640]{1,0:T(8,128)(2,1)S(1)}, bf16[128,640]{1,0:T(8,128)(2,1)S(1)}, u32[]{:S(2)}, u32[]{:S(2)}) collective-permute-start(bf16[128,640]{1,0:T(8,128)(2,1)S(1)} %get-tuple-element.120.refs_0_), channel_id=1, source_target_pairs={{0,4},{1,5},{2,6},{3,7},{8,12},{9,13},{10,14},{11,15},{16,20},{17,... | collective-permute-start | bytes 491528 | tf_op jit(solution)/shard_map/ppermute | solution.py:336
  101.6 24.3 %collective-permute-start.7 = (bf16[128,640]{1,0:T(8,128)(2,1)S(1)}, bf16[128,640]{1,0:T(8,128)(2,1)S(1)}, u32[]{:S(2)}, u32[]{:S(2)}) collective-permute-start(bf16[128,640]{1,0:T(8,128)(2,1)S(1)} %get-tuple-element.120.refs_0_), channel_id=1, source_target_pairs={{0,1},{1,2},{2,3},{3,4},{4,5},{5,6},{6,7},{8,9},{9,10},{10,11},{11... | collective-permute-start | bytes 491528 | tf_op jit(solution)/shard_map/ppermute | solution.py:336
  105.3 24.1 %collective-permute-start.8 = (bf16[128,640]{1,0:T(8,128)(2,1)S(1)}, bf16[128,640]{1,0:T(8,128)(2,1)S(1)}, u32[]{:S(2)}, u32[]{:S(2)}) collective-permute-start(bf16[128,640]{1,0:T(8,128)(2,1)S(1)} %get-tuple-element.120.refs_0_), channel_id=1, source_target_pairs={{0,2},{1,3},{2,4},{3,5},{4,6},{5,7},{8,10},{9,11},{10,12},{11,13},... | collective-permute-start | bytes 491528 | tf_op jit(solution)/shard_map/ppermute | solution.py:336
  108.7 24.2 %collective-permute-start.9 = (bf16[128,640]{1,0:T(8,128)(2,1)S(1)}, bf16[128,640]{1,0:T(8,128)(2,1)S(1)}, u32[]{:S(2)}, u32[]{:S(2)}) collective-permute-start(bf16[128,640]{1,0:T(8,128)(2,1)S(1)} %get-tuple-element.120.refs_0_), channel_id=1, source_target_pairs={{0,3},{1,4},{2,5},{3,6},{4,7},{8,11},{9,12},{10,13},{11,14},{12,15... | collective-permute-start | bytes 491528 | tf_op jit(solution)/shard_map/ppermute | solution.py:336
  133.6 103.0 %all-gather.9.cloned.1.call-start = ((), (), s32[]{:S(2)}) async-start(), calls=%async_computation.12 | async-start | bytes 4718592 | tf_op jit(solution)/shard_map/all_gather | solution.py:571
  135.3 36.1 %collective-permute-start.12 = (bf16[1,2,1,256,640]{4,3,1,2,0:T(8,128)(2,1)S(1)}, bf16[1,2,1,256,640]{4,3,1,2,0:T(8,128)(2,1)}, u32[]{:S(2)}, u32[]{:S(2)}) collective-permute-start(bf16[1,2,1,256,640]{4,3,1,2,0:T(8,128)(2,1)S(1)} %get-tuple-element.141), channel_id=1, source_target_pairs={{0,4},{4,0},{1,5},{5,1},{2,6},{6,2},{3,7},{7,3},{8,12},{12,8},{9,1... | collective-permute-start | bytes 1966088 | tf_op jit(solution)/shard_map/ppermute | solution.py:331
  143.9 27.5 %collective-permute-start.13 = (bf16[1,2,1,256,640]{4,3,1,2,0:T(8,128)(2,1)S(1)}, bf16[1,2,1,256,640]{4,3,1,2,0:T(8,128)(2,1)}, u32[]{:S(2)}, u32[]{:S(2)}) collective-permute-start(bf16[1,2,1,256,640]{4,3,1,2,0:T(8,128)(2,1)S(1)} %get-tuple-element.141), channel_id=1, source_target_pairs={{0,16},{16,0},{1,17},{17,1},{2,18},{18,2},{3,19},{19,3},{4,20},{20... | collective-permute-start | bytes 1966088 | tf_op jit(solution)/shard_map/ppermute | solution.py:331
  178.1 85.9 %all-gather.13.cloned.1.call-start = ((), (), s32[]{:S(2)}) async-start(), calls=%async_computation.14 | async-start | bytes 2949120 | tf_op jit(solution)/shard_map/all_gather | solution.py:580
  178.2 29.7 %collective-permute-start.17 = (bf16[1,2,1,256,640]{4,3,1,2,0:T(8,128)(2,1)S(1)}, bf16[1,2,1,256,640]{4,3,1,2,0:T(8,128)(2,1)}, u32[]{:S(2)}, u32[]{:S(2)}) collective-permute-start(bf16[1,2,1,256,640]{4,3,1,2,0:T(8,128)(2,1)S(1)} %get-tuple-element.145), channel_id=1, source_target_pairs={{0,4},{4,0},{1,5},{5,1},{2,6},{6,2},{3,7},{7,3},{8,12},{12,8},{9,1... | collective-permute-start | bytes 1966088 | tf_op jit(solution)/shard_map/ppermute | solution.py:331
  178.2 32.8 %collective-permute-start.14 = (bf16[1,2,1,256,640]{4,3,1,2,0:T(8,128)(2,1)}, bf16[1,2,1,256,640]{4,3,1,2,0:T(8,128)(2,1)}, u32[]{:S(2)}, u32[]{:S(2)}) collective-permute-start(bf16[1,2,1,256,640]{4,3,1,2,0:T(8,128)(2,1)} %copy-done.5), channel_id=1, source_target_pairs={{0,16},{16,0},{1,17},{17,1},{2,18},{18,2},{3,19},{19,3},{4,20},{20... | collective-permute-start | bytes 1966088 | tf_op jit(solution)/shard_map/ppermute | solution.py:331
  180.4 44.1 %collective-permute-start.16 = (bf16[1,2,1,256,640]{4,3,1,2,0:T(8,128)(2,1)S(1)}, bf16[1,2,1,256,640]{4,3,1,2,0:T(8,128)(2,1)}, u32[]{:S(2)}, u32[]{:S(2)}) collective-permute-start(bf16[1,2,1,256,640]{4,3,1,2,0:T(8,128)(2,1)S(1)} %get-tuple-element.145), channel_id=1, source_target_pairs={{0,16},{16,0},{1,17},{17,1},{2,18},{18,2},{3,19},{19,3},{4,20},{20... | collective-permute-start | bytes 1966088 | tf_op jit(solution)/shard_map/ppermute | solution.py:331
  180.5 44.0 %collective-permute-start.15 = (bf16[1,2,1,256,640]{4,3,1,2,0:T(8,128)(2,1)}, bf16[1,2,1,256,640]{4,3,1,2,0:T(8,128)(2,1)}, u32[]{:S(2)}, u32[]{:S(2)}) collective-permute-start(bf16[1,2,1,256,640]{4,3,1,2,0:T(8,128)(2,1)} %collective-permute-done.12), channel_id=1, source_target_pairs={{0,16},{16,0},{1,17},{17,1},{2,18},{18,2},{3,19},{19,3},{4,20},{20... | collective-permute-start | bytes 1966088 | tf_op jit(solution)/shard_map/ppermute | solution.py:331
  207.8 28.8 %collective-permute-start.18 = (bf16[1,2,1,256,640]{4,3,1,2,0:T(8,128)(2,1)}, bf16[1,2,1,256,640]{4,3,1,2,0:T(8,128)(2,1)}, u32[]{:S(2)}, u32[]{:S(2)}) collective-permute-start(bf16[1,2,1,256,640]{4,3,1,2,0:T(8,128)(2,1)} %collective-permute-done.17), channel_id=1, source_target_pairs={{0,16},{16,0},{1,17},{17,1},{2,18},{18,2},{3,19},{19,3},{4,20},{20... | collective-permute-start | bytes 1966088 | tf_op jit(solution)/shard_map/ppermute | solution.py:331
  236.6 138.7 %reduce-scatter.4.cloned.1.call-start = ((), (), s32[]{:S(2)}) async-start(), calls=%async_computation.15 | async-start | bytes 3276800 | tf_op jit(solution)/shard_map/reduce_scatter | solution.py:591
  276.2 173.3 %reduce-scatter.6.cloned.1.call-start = ((), (), s32[]{:S(2)}) async-start(), calls=%async_computation.16 | async-start | bytes 3276800 | tf_op jit(solution)/shard_map/reduce_scatter | solution.py:591
  291.1 45.6 %collective-permute-start.23 = (bf16[512,2048]{1,0:T(8,128)(2,1)}, bf16[512,2048]{1,0:T(8,128)(2,1)}, u32[]{:S(2)}, u32[]{:S(2)}) collective-permute-start(bf16[512,2048]{1,0:T(8,128)(2,1)} %dynamic-slice_bitcast_fusion.1), channel_id=1, source_target_pairs={{0,8},{8,0},{1,9},{9,1},{2,10},{10,2},{3,11},{11,3},{4,12},{12,4},... | collective-permute-start | bytes 6291464 | tf_op jit(solution)/shard_map/ppermute | solution.py:331
  292.8 14.1 %collective-permute-start.20 = (bf16[128,2048]{1,0:T(8,128)(2,1)S(1)}, bf16[128,2048]{1,0:T(8,128)(2,1)S(1)}, u32[]{:S(2)}, u32[]{:S(2)}) collective-permute-start(bf16[128,2048]{1,0:T(8,128)(2,1)S(1)} %get-tuple-element.215), channel_id=1, source_target_pairs={{0,1},{1,0},{2,3},{3,2},{4,5},{5,4},{6,7},{7,6},{8,9},{9,8},{10,11... | collective-permute-start | bytes 1572872 | tf_op jit(solution)/shard_map/ppermute | solution.py:415
  293.9 24.3 %collective-permute-start.21 = (bf16[128,2048]{1,0:T(8,128)(2,1)S(1)}, bf16[128,2048]{1,0:T(8,128)(2,1)}, u32[]{:S(2)}, u32[]{:S(2)}) collective-permute-start(bf16[128,2048]{1,0:T(8,128)(2,1)S(1)} %get-tuple-element.217), channel_id=1, source_target_pairs={{0,2},{1,3},{2,0},{3,1},{4,6},{5,7},{6,4},{7,5},{8,10},{9,11},{10,... | collective-permute-start | bytes 1572872 | tf_op jit(solution)/shard_map/ppermute | solution.py:415
  294.9 39.9 %collective-permute-start.22 = (bf16[128,2048]{1,0:T(8,128)(2,1)S(1)}, bf16[128,2048]{1,0:T(8,128)(2,1)}, u32[]{:S(2)}, u32[]{:S(2)}) collective-permute-start(bf16[128,2048]{1,0:T(8,128)(2,1)S(1)} %get-tuple-element.216), channel_id=1, source_target_pairs={{0,3},{1,2},{2,1},{3,0},{4,7},{5,6},{6,5},{7,4},{8,11},{9,10},{10,... | collective-permute-start | bytes 1572872 | tf_op jit(solution)/shard_map/ppermute | solution.py:415
  353.1 13.2 %collective-permute-start.26 = (bf16[128,640]{1,0:T(8,128)(2,1)S(1)}, bf16[128,640]{1,0:T(8,128)(2,1)S(1)}, u32[]{:S(2)}, u32[]{:S(2)}) collective-permute-start(bf16[128,640]{1,0:T(8,128)(2,1)S(1)} %get-tuple-element.170), channel_id=1, source_target_pairs={{3,0},{4,1},{5,2},{6,3},{7,4},{11,8},{12,9},{13,10},{14,11},{15,12... | collective-permute-start | bytes 491528 | tf_op jit(solution)/shard_map/ppermute | solution.py:336
  354.4 21.0 %collective-permute-start.27 = (bf16[128,640]{1,0:T(8,128)(2,1)S(1)}, bf16[128,640]{1,0:T(8,128)(2,1)S(1)}, u32[]{:S(2)}, u32[]{:S(2)}) collective-permute-start(bf16[128,640]{1,0:T(8,128)(2,1)S(1)} %get-tuple-element.171), channel_id=1, source_target_pairs={{4,0},{5,1},{6,2},{7,3},{12,8},{13,9},{14,10},{15,11},{20,16},{21,... | collective-permute-start | bytes 491528 | tf_op jit(solution)/shard_map/ppermute | solution.py:336
  382.5 18.1 %all-to-all-start.4 = ((bf16[8,128,256]{2,1,0:T(8,128)(2,1)}), bf16[8,128,256]{2,1,0:T(8,128)(2,1)S(1)}, u32[]{:S(2)}, u32[]{:S(2)}) async-start(bf16[8,128,256]{2,1,0:T(8,128)(2,1)} %get-tuple-element.181), calls=%async_computation.5 | async-start | bytes 1048576 | tf_op jit(solution)/shard_map/all_to_all | solution.py:644
  386.0 128.8 %reduce-scatter.8.cloned.1.call-start = ((), (), s32[]{:S(2)}) async-start(), calls=%async_computation.17 | async-start | bytes 3276800 | tf_op jit(solution)/shard_map/reduce_scatter | solution.py:591
  408.9 14.9 %collective-permute-start.29 = (bf16[128,2048]{1,0:T(8,128)(2,1)S(1)}, bf16[128,2048]{1,0:T(8,128)(2,1)}, u32[]{:S(2)}, u32[]{:S(2)}) collective-permute-start(bf16[128,2048]{1,0:T(8,128)(2,1)S(1)} %get-tuple-element.212), channel_id=1, source_target_pairs={{0,1},{1,0},{2,3},{3,2},{4,5},{5,4},{6,7},{7,6},{8,9},{9,8},{10,11... | collective-permute-start | bytes 1572872 | tf_op jit(solution)/shard_map/ppermute | solution.py:415
  409.0 20.4 %collective-permute-start.30 = (bf16[128,2048]{1,0:T(8,128)(2,1)S(1)}, bf16[128,2048]{1,0:T(8,128)(2,1)}, u32[]{:S(2)}, u32[]{:S(2)}) collective-permute-start(bf16[128,2048]{1,0:T(8,128)(2,1)S(1)} %get-tuple-element.214), channel_id=1, source_target_pairs={{0,2},{1,3},{2,0},{3,1},{4,6},{5,7},{6,4},{7,5},{8,10},{9,11},{10,... | collective-permute-start | bytes 1572872 | tf_op jit(solution)/shard_map/ppermute | solution.py:415
  409.3 34.3 %collective-permute-start.31 = (bf16[128,2048]{1,0:T(8,128)(2,1)S(1)}, bf16[128,2048]{1,0:T(8,128)(2,1)}, u32[]{:S(2)}, u32[]{:S(2)}) collective-permute-start(bf16[128,2048]{1,0:T(8,128)(2,1)S(1)} %get-tuple-element.213), channel_id=1, source_target_pairs={{0,3},{1,2},{2,1},{3,0},{4,7},{5,6},{6,5},{7,4},{8,11},{9,10},{10,... | collective-permute-start | bytes 1572872 | tf_op jit(solution)/shard_map/ppermute | solution.py:415
  413.6 34.9 %all-to-all-start.5 = ((bf16[8,128,256]{1,2,0:T(8,128)(2,1)}), bf16[8,128,256]{1,2,0:T(8,128)(2,1)S(1)}, u32[]{:S(2)}, u32[]{:S(2)}) async-start(bf16[8,128,256]{1,2,0:T(8,128)(2,1)} %bitcast.61), calls=%async_computation.7 | async-start | bytes 1048576 | tf_op jit(solution)/shard_map/all_to_all | solution.py:434
  452.2 50.5 %collective-permute-start.37 = (bf16[128,2048]{1,0:T(8,128)(2,1)}, bf16[128,2048]{1,0:T(8,128)(2,1)}, u32[]{:S(2)}, u32[]{:S(2)}) collective-permute-start(bf16[128,2048]{1,0:T(8,128)(2,1)} %get-tuple-element.209), channel_id=1, source_target_pairs={{0,1},{1,0},{2,3},{3,2},{4,5},{5,4},{6,7},{7,6},{8,9},{9,8},{10,11... | collective-permute-start | bytes 1572872 | tf_op jit(solution)/shard_map/ppermute | solution.py:415
  452.5 50.2 %collective-permute-start.38 = (bf16[128,2048]{1,0:T(8,128)(2,1)}, bf16[128,2048]{1,0:T(8,128)(2,1)}, u32[]{:S(2)}, u32[]{:S(2)}) collective-permute-start(bf16[128,2048]{1,0:T(8,128)(2,1)} %get-tuple-element.211), channel_id=1, source_target_pairs={{0,2},{1,3},{2,0},{3,1},{4,6},{5,7},{6,4},{7,5},{8,10},{9,11},{10,... | collective-permute-start | bytes 1572872 | tf_op jit(solution)/shard_map/ppermute | solution.py:415
  454.4 48.3 %collective-permute-start.39 = (bf16[128,2048]{1,0:T(8,128)(2,1)S(1)}, bf16[128,2048]{1,0:T(8,128)(2,1)}, u32[]{:S(2)}, u32[]{:S(2)}) collective-permute-start(bf16[128,2048]{1,0:T(8,128)(2,1)S(1)} %get-tuple-element.210), channel_id=1, source_target_pairs={{0,3},{1,2},{2,1},{3,0},{4,7},{5,6},{6,5},{7,4},{8,11},{9,10},{10,... | collective-permute-start | bytes 1572872 | tf_op jit(solution)/shard_map/ppermute | solution.py:415
  457.5 19.0 %collective-permute-start.36 = (bf16[1,2,64,1280]{3,2,1,0:T(8,128)(2,1)}, bf16[1,2,64,1280]{3,2,1,0:T(8,128)(2,1)}, u32[]{:S(2)}, u32[]{:S(2)}) collective-permute-start(bf16[1,2,64,1280]{3,2,1,0:T(8,128)(2,1)} %dynamic-slice_bitcast_fusion.13), channel_id=1, source_target_pairs={{0,16},{16,0},{1,17},{17,1},{2,18},{18,2},{3,19},{19,3},{4,20},{20... | collective-permute-start | bytes 983048 | tf_op jit(solution)/shard_map/ppermute | solution.py:331
  461.3 64.3 %all-to-all-start.7 = ((bf16[8,64,1280]{2,1,0:T(8,128)(2,1)}), bf16[8,64,1280]{2,1,0:T(8,128)(2,1)}, u32[]{:S(2)}, u32[]{:S(2)}) async-start(bf16[8,64,1280]{2,1,0:T(8,128)(2,1)} %pad_maximum_fusion), calls=%async_computation.10 | async-start | bytes 2621440 | tf_op jit(solution)/shard_map/all_to_all | solution.py:388
  476.3 20.6 %collective-permute-start.34 = (bf16[2,2,256,256]{3,2,1,0:T(8,128)(2,1)S(1)}, bf16[2,2,256,256]{3,2,1,0:T(8,128)(2,1)S(1)}, u32[]{:S(2)}, u32[]{:S(2)}) collective-permute-start(bf16[2,2,256,256]{3,2,1,0:T(8,128)(2,1)S(1)} %dynamic-slice_bitcast_fusion.6), channel_id=1, source_target_pairs={{0,16},{16,0},{1,17},{17,1},{2,18},{18,2},{3,19},{19,3},{4,20},{20... | collective-permute-start | bytes 1572872 | tf_op jit(solution)/shard_map/ppermute | solution.py:331
  497.1 17.6 %collective-permute-start.35 = (bf16[2,256,256]{2,1,0:T(8,128)(2,1)S(1)}, bf16[2,256,256]{2,1,0:T(8,128)(2,1)S(1)}, u32[]{:S(2)}, u32[]{:S(2)}) collective-permute-start(bf16[2,256,256]{2,1,0:T(8,128)(2,1)S(1)} %fusion.22), channel_id=1, source_target_pairs={{0,4},{4,0},{1,5},{5,1},{2,6},{6,2},{3,7},{7,3},{8,12},{12,8},{9,1... | collective-permute-start | bytes 786440 | tf_op jit(solution)/shard_map/ppermute | solution.py:331
  517.3 16.9 %collective-permute-start.40 = (bf16[1,64,1280]{2,1,0:T(8,128)(2,1)}, bf16[1,64,1280]{2,1,0:T(8,128)(2,1)}, u32[]{:S(2)}, u32[]{:S(2)}) collective-permute-start(bf16[1,64,1280]{2,1,0:T(8,128)(2,1)} %fusion.23), channel_id=1, source_target_pairs={{0,4},{4,0},{1,5},{5,1},{2,6},{6,2},{3,7},{7,3},{8,12},{12,8},{9,1... | collective-permute-start | bytes 491528 | tf_op jit(solution)/shard_map/ppermute | solution.py:331
  525.6 17.7 %all-to-all-start.6 = ((bf16[8,64,896]{2,1,0:T(8,128)(2,1)}), bf16[8,64,896]{2,1,0:T(8,128)(2,1)}, u32[]{:S(2)}, u32[]{:S(2)}) async-start(bf16[8,64,896]{2,1,0:T(8,128)(2,1)} %pad_maximum_fusion.1), calls=%async_computation.9 | async-start | bytes 1835008 | tf_op jit(solution)/shard_map/all_to_all | solution.py:388
  (68 other events, 470.4 us)
Sparse Core Ops, SparseCore 0:
  10.8 47.7 all-gather.6
  60.8 53.7 all-gather.14
  133.7 49.7 all-gather.10
  185.5 41.7 all-gather.8
  236.8 27.1 all-gather.12
  276.3 61.3 reduce-scatter.3
  375.5 58.0 reduce-scatter.5
  436.6 60.4 reduce-scatter.7
